TPU v7x, 256 devices: a whole 4x4x8 slice. The times are simulated.
256 devices in a mesh: mem: 32 (over z, x_lo, core), space: 8 (over x_hi, y).
Axes of the slice: x: 4 (x_hi: 2, x_lo: 2; x = x_hi * 2 + x_lo), y: 4, z: 8, core: 2. Of those that a mesh axis runs over, the one named last changes fastest.
Arguments:
- prior_sample_set: float32 [1024, 512, 128], P('mem', 'space'), may hold values from -6 to 6
- perturbed_obs: float32 [1024, 512, 128], P('mem', 'space'), may hold values from -6 to 6
- measured_slot_table: int32 [512, 128], P('space'), may hold values from 0 to 127
- obs_var: float32 [512, 128], P('space'), may hold values from 0.25 to 2
- neighbours: int32 [512, 2], P('space'), may hold values from 0 to 511, as said below
- norm_gain: float32 [64], replicated, may hold values from 0.5 to 1.5
- w_in: bfloat16 [64, 512], replicated, may hold values from -0.75 to 0.75
- b_in: float32 [512], replicated, may hold values from -3 to 3
- w_out: bfloat16 [512, 64], replicated, may hold values from -0.25 to 0.25
- b_out: float32 [64], replicated, may hold values from -1.2 to 1.2
Outputs:
- analysis: float32 [1024, 512, 128], P('mem', 'space')
Inputs may be any that keep to these rules, and one draw needn't show every extreme that they name: `neighbours`: row p names 2 different blocks among p - 1, p, p + 1 taken modulo 512, in the order of these offsets. `measured_slot_table`: entry [b, j] names a variable of patch b.
All inputs are finite; a program needn't handle non-finite values.
Results may differ from a plain program's by a relative error of at most 0.0026.
Values sent between devices are 32-bit elements; how exact they have to be, the bound alone decides.
No kernel may reach another device: no remote copies, remote signals or barrier semaphores. Data moves between devices by JAX's collectives and lax.ppermute only.
A program may use at most 64 MiB of HBM per device.

v0:
```python
import jax
import jax.numpy as jnp
from jax import lax
from jax.experimental import pallas as pl
from jax.experimental.pallas import tpu as pltpu
from jax.sharding import PartitionSpec as P

LEV = 64
HID = 512
HOPS = 2
PV = 128
NMEM = 32
PAIRS = 32
F32 = jnp.float32
BF16 = jnp.bfloat16


def owner_of(pair):
    chip, core = pair // 2, pair % 2
    z, x = (chip, 0) if chip < 8 else (15 - chip, 1)
    return (z * 2 + x) * 2 + core


def pair_of(member):
    z, x, core = member // 4, (member // 2) % 2, member % 2
    return 2 * jnp.where(x == 0, z, 15 - z) + core


def neighbour_moves(step):
    runs = 8
    moves = []
    for run in range(runs):
        for pair in range(PAIRS):
            there = (run * PAIRS + pair + step) % (runs * PAIRS)
            moves.append(
                (owner_of(pair) * runs + run, owner_of(there % PAIRS) * runs + there // PAIRS)
            )
    return moves


def dot(a, b):
    return jnp.dot(a, b, preferred_element_type=F32)


def tdot(a, b):
    return lax.dot_general(a, b, (((0,), (0,)), ((), ())), preferred_element_type=F32)


def split(a):
    high = a.astype(BF16)
    return high, (a - high.astype(F32)).astype(BF16)


def dot3(a, b):
    (ah, al), (bh, bl) = split(a), split(b)
    return dot(ah, bh) + (dot(ah, bl) + dot(al, bh))


def to_send_kernel(x_ref, o_ref):
    for patch in range(2 * PAIRS):
        row = 2 * owner_of(patch // 2) + patch % 2
        o_ref[row] = x_ref[pl.ds(patch, NMEM, stride=2 * PAIRS), :]


def from_sent_kernel(x_ref, o_ref):
    for patch in range(2 * PAIRS):
        row = 2 * owner_of(patch // 2) + patch % 2
        o_ref[pl.ds(patch, NMEM, stride=2 * PAIRS), :] = x_ref[row]


def forecast_kernel(x_ref, g_ref, wi_ref, bi_ref, wo_ref, bo_ref, o_ref, wi2, wo2):
    wi = (wi_ref[...].astype(F32) * 0.5).astype(BF16)
    zi = jnp.zeros_like(wi)
    wi2[:LEV, :HID] = wi
    wi2[:LEV, HID:] = zi
    wi2[LEV:, :HID] = zi
    wi2[LEV:, HID:] = wi
    wo = wo_ref[...]
    zo = jnp.zeros_like(wo)
    wo2[:HID, :] = jnp.concatenate([wo, zo], axis=1)
    wo2[HID:, :] = jnp.concatenate([zo, wo], axis=1)
    gain = jnp.concatenate([g_ref[...]] * 2, axis=1)
    bi = jnp.concatenate([bi_ref[...]] * 2, axis=1) * 0.5
    bo = jnp.concatenate([bo_ref[...]] * 2, axis=1)
    row = lax.broadcasted_iota(jnp.int32, (2 * PV, PV), 0)
    col = lax.broadcasted_iota(jnp.int32, (2 * PV, PV), 1)
    halves = jnp.where((row % PV) // LEV == col // LEV, 1.0, 0.0).astype(BF16)
    chunk = 8
    for first in range(0, 2 * PAIRS, chunk):
        x = jnp.concatenate(
            [x_ref[pl.ds(first + i, NMEM, stride=2 * PAIRS), :] for i in range(chunk)], axis=0
        )
        for _ in range(HOPS):
            squares = jnp.concatenate(split(x * x), axis=1)
            inverse = lax.rsqrt(dot(squares, halves) * (1.0 / LEV) + 1e-6)
            normed = (x * inverse * gain).astype(BF16)
            h = dot(normed, wi2[...]) + bi
            hidden = (h + h * jnp.tanh(h)).astype(BF16)
            x = x + dot(hidden, wo2[...]) + bo
        for i in range(chunk):
            patch = first + i
            o_ref[2 * owner_of(patch // 2) + patch % 2] = x[i * NMEM : (i + 1) * NMEM]


def update_kernel(
    idx_ref, f_ref, fl_ref, fr_ref, p_ref, pl_ref, pr_ref, slot_ref, var_ref, o_ref,
    ah, al, bh, bl, dh, dl, s_ref, x_ref,
):
    members = NMEM * NMEM
    fields = (fl_ref, f_ref.at[:, 0], f_ref.at[:, 1], fr_ref)
    readings = (pl_ref, p_ref.at[:, 0], p_ref.at[:, 1], pr_ref)
    root = lax.rsqrt(var_ref[...])
    for w in range(4):
        x = fields[w][...].reshape(members, PV)
        if w in (1, 2):
            a = x - jnp.mean(x, axis=0, keepdims=True)
            ah[w - 1], al[w - 1] = split(a)
        slots = jnp.broadcast_to(slot_ref[w : w + 1, :], (members, PV))
        y = jnp.take_along_axis(x, slots, axis=1, mode="promise_in_bounds")
        r = root[w : w + 1, :]
        b = (y - jnp.mean(y, axis=0, keepdims=True)) * r
        bh[w], bl[w] = split(b)
        d = (readings[w][...].reshape(members, PV) - y) * r
        dh[w], dl[w] = split(d)
    eye = jnp.where(
        lax.broadcasted_iota(jnp.int32, (2 * PV, 2 * PV), 0)
        == lax.broadcasted_iota(jnp.int32, (2 * PV, 2 * PV), 1),
        1.0,
        0.0,
    )
    scale = 1.0 / (members - 1)
    cross, deltas = [], []
    for j in range(2):
        one, two = idx_ref[j, 0], idx_ref[j, 1]
        rh = jnp.concatenate([bh[one], bh[two]], axis=1)
        rl = jnp.concatenate([bl[one], bl[two]], axis=1)
        mixed = tdot(rh, rl)
        s = (tdot(rh, rh) + (mixed + mixed.T)) * scale + eye
        cross.append((tdot(rh, ah[j]) + (tdot(rh, al[j]) + tdot(rl, ah[j]))) * scale)
        s2 = dot3(s, s)
        top = jnp.max(jnp.sqrt(jnp.sum(jnp.abs(s2), axis=0, keepdims=True)))
        c = 2.0 / (top + 1.0)
        delta = (top - 1.0) / (top + 1.0)
        mu = 2.0 / (2.0 - delta * delta)
        x1 = (mu * c) * (2.0 * eye - c * s)
        t1 = (mu * c) * (2.0 * s - c * s2)
        delta = delta * delta / (2.0 - delta * delta)
        mu = 2.0 / (2.0 - delta * delta)
        s_ref[j] = s
        x_ref[j] = mu * (2.0 * x1 - dot3(x1, t1))
        deltas.append(delta * delta / (2.0 - delta * delta))

    def more(state):
        return jnp.maximum(state[0], state[1]) > 0.02

    def sharpen(state):
        after = []
        for j in range(2):
            delta = state[j]
            x = x_ref[j]
            mu = 2.0 / (2.0 - delta * delta)
            x_ref[j] = mu * (2.0 * x - dot3(x, dot3(s_ref[j], x)))
            after.append(delta * delta / (2.0 - delta * delta))
        return tuple(after)

    lax.while_loop(more, sharpen, tuple(deltas))
    for j in range(2):
        s, x, g = s_ref[j], x_ref[j], cross[j]
        k = dot3(x, g)
        for _ in range(2):
            k = k + dot3(
                x, g - jnp.dot(s, k, precision=lax.Precision.HIGHEST, preferred_element_type=F32)
            )
        kh, kl = split(k)
        one, two = idx_ref[j, 0], idx_ref[j, 1]
        ih = jnp.concatenate([dh[one], dh[two]], axis=1)
        il = jnp.concatenate([dl[one], dl[two]], axis=1)
        gained = dot(ih, kh) + (dot(ih, kl) + dot(il, kh))
        o_ref[:, j] = fields[1 + j][...] + gained.reshape(NMEM, NMEM, PV)


def vmem_call(kernel, out, scratch=(), smem=0, limit=48, n_in=1):
    specs = [pl.BlockSpec(memory_space=pltpu.SMEM)] * smem
    specs += [pl.BlockSpec(memory_space=pltpu.VMEM)] * (n_in - smem)
    return pl.pallas_call(
        kernel,
        out_shape=jax.ShapeDtypeStruct(out, F32),
        in_specs=specs,
        out_specs=pl.BlockSpec(memory_space=pltpu.VMEM),
        scratch_shapes=list(scratch),
        compiler_params=pltpu.CompilerParams(vmem_limit_bytes=limit << 20),
    )


def body(
    prior_sample_set, perturbed_obs, measured_slot_table, obs_var, neighbours,
    norm_gain, w_in, b_in, w_out, b_out,
):
    rows = 2 * PAIRS * NMEM
    sent = (2 * PAIRS, NMEM, PV)
    packed = (NMEM, 2, NMEM, PV)
    both = ("mem", "space")
    first = 2 * pair_of(lax.axis_index("mem"))

    pert_send = vmem_call(to_send_kernel, sent)(perturbed_obs.reshape(rows, PV))
    pert = lax.all_to_all(pert_send.reshape(packed), "mem", 0, 0, tiled=True)

    field_send = vmem_call(
        forecast_kernel, sent,
        [pltpu.VMEM((2 * LEV, 2 * HID), BF16), pltpu.VMEM((2 * HID, 2 * LEV), BF16)], n_in=6,
    )(
        prior_sample_set.reshape(rows, PV), norm_gain.reshape(1, -1), w_in, b_in.reshape(1, -1),
        w_out, b_out.reshape(1, -1),
    )
    meta = jnp.concatenate([measured_slot_table.astype(F32), obs_var], axis=-1)
    field_send, meta = lax.optimization_barrier((field_send, meta))
    field = lax.all_to_all(field_send.reshape(packed), "mem", 0, 0, tiled=True)

    runs = [(i, (i + 1) % 8) for i in range(8)]
    before = lax.ppermute(meta[-1:], "space", runs)
    after = lax.ppermute(meta[:1], "space", [(j, i) for i, j in runs])
    window = lax.dynamic_slice_in_dim(
        jnp.concatenate([before, meta, after], axis=0), first, 4, 0
    )
    slots, variances = window[:, :PV].astype(jnp.int32), window[:, PV:]
    named = lax.dynamic_slice_in_dim(neighbours, first, 2, 0)
    own = jnp.arange(2, dtype=jnp.int32)[:, None]
    place = lax.axis_index("space") * (2 * PAIRS) + first + own
    index = (named - place + 1) % 512 + own

    rightward, leftward = neighbour_moves(1), neighbour_moves(-1)
    pert_left = lax.ppermute(pert[:, 1], both, rightward)
    pert_right = lax.ppermute(pert[:, 0], both, leftward)
    field_left = lax.ppermute(field[:, 1], both, rightward)
    field_right = lax.ppermute(field[:, 0], both, leftward)

    members = NMEM * NMEM
    half = pltpu.VMEM((2, members, PV), BF16)
    full = pltpu.VMEM((4, members, PV), BF16)
    square = pltpu.VMEM((2, 2 * PV, 2 * PV), F32)
    analysis = vmem_call(
        update_kernel, packed, [half, half, full, full, full, full, square, square], smem=1, n_in=9
    )(index, field, field_left, field_right, pert, pert_left, pert_right, slots, variances)
    returned = lax.all_to_all(analysis, "mem", 0, 0, tiled=True)
    out = vmem_call(from_sent_kernel, (rows, PV))(returned.reshape(sent))
    return out.reshape(prior_sample_set.shape)


def solution(mesh):
    rows = P("space", None)
    cube = P("mem", "space", None)
    return jax.shard_map(
        body,
        mesh=mesh,
        in_specs=(cube, cube, rows, rows, rows, P(), P(), P(), P(), P()),
        out_specs=cube,
        check_vma=False,
    )
```

profile of v0, /device:TPU:3, one launch (start us, length us, event | category | flops | bytes accessed | tf_op | source)
XLA Modules:
  0.0 141.4 jit_solution(11730649742172462792)
XLA Ops:
  0.0 1.2 copy-done.2
  1.2 1.6 %shard_map.101 = f32[64,32,128]{2,1,0:T(8,128)} custom-call(f32[2048,128]{1,0:T(8,128)S(1)} %bitcast.27), custom_call_target="tpu_custom_call" | custom-call | tf_op jit(solution)/shard_map/pallas_call | solution.py:205
  2.9 10.5 %all-to-all-start.1 = ((f32[32,2,32,128]{3,2,1,0:T(8,128)}), f32[32,2,32,128]{3,2,1,0:T(8,128)S(1)}, u32[]{:S(2)}, u32[]{:S(2)}) async-start(f32[32,2,32,128]{3,2,1,0:T(8,128)} %bitcast.8), calls=%async_computation.1 | async-start | bytes 2097152 | tf_op jit(solution)/shard_map/all_to_all | solution.py:206
  13.4 0.0 copy-start.7
  13.4 0.8 copy-done.7
  14.2 0.1 copy.22.wo_ref
  14.4 0.0 copy-start.4
  14.4 0.0 copy-start.5
  14.4 0.0 copy-start.6
  14.4 0.7 copy-done.3
  15.1 8.8 %shard_map.100 = f32[64,32,128]{2,1,0:T(8,128)} custom-call(f32[2048,128]{1,0:T(8,128)S(1)} %bitcast.26, f32[1,64]{1,0:T(1,128)S(1)} %bitcast.29, bf16[64,512]{1,0:T(8,128)(2,1)S(1)} %copy-done.3, f32[1,512]{1,0:T(1,128)S(1)} %bitcast.28, bf16[512,64]{1,0:T(8,128)(2,1)S(1)} %copy.22.wo_ref, f32[1,64]{1,0:T(1,128)S(1)} %bitcast.30), custom_call_target="tpu_custom_call" | custom-call | tf_op jit(solution)/shard_map/pallas_call | solution.py:208
  23.9 17.7 %all-to-all-done.1.p_ref = f32[32,2,32,128]{3,2,1,0:T(8,128)S(1)} async-done(((f32[32,2,32,128]{3,2,1,0:T(8,128)}), f32[32,2,32,128]{3,2,1,0:T(8,128)S(1)}, u32[]{:S(2)}, u32[]{:S(2)}) %all-to-all-start.1) | async-done | bytes 1048608 | tf_op jit(solution)/shard_map/all_to_all | solution.py:206
  41.6 4.7 %all-to-all-start = ((f32[32,2,32,128]{3,2,1,0:T(8,128)}), f32[32,2,32,128]{3,2,1,0:T(8,128)S(1)}, u32[]{:S(2)}, u32[]{:S(2)}) async-start(f32[32,2,32,128]{3,2,1,0:T(8,128)} %bitcast.4), calls=%async_computation | async-start | bytes 2097152 | tf_op jit(solution)/shard_map/all_to_all | solution.py:217
  46.3 1.4 collective-permute-start.4
  47.7 3.8 %collective-permute-start.5 = (f32[1,256]{1,0:T(1,128)S(1)}, f32[1,256]{1,0:T(1,128)S(1)}, u32[]{:S(2)}, u32[]{:S(2)}) collective-permute-start(f32[1,256]{1,0:T(1,128)S(1)} %get-tuple-element.14), channel_id=1, source_target_pairs={{1,0},{2,1},{3,2},{4,3},{5,4},{6,5},{7,6},{0,7},{9,8},{10,9},{11,1... | collective-permute-start | bytes 3080 | tf_op jit(solution)/shard_map/ppermute | solution.py:221
  51.5 0.1 constant_dynamic-slice_fusion
  51.6 0.1 copy.27
  51.7 1.0 slice_bitcast_fusion
  52.7 0.9 collective-permute-start.3
  53.6 1.7 %collective-permute-start.2 = (f32[32,32,128]{2,1,0:T(8,128)}, f32[32,32,128]{2,1,0:T(8,128)S(1)}, u32[]{:S(2)}, u32[]{:S(2)}) collective-permute-start(f32[32,32,128]{2,1,0:T(8,128)} %get-tuple-element.10), channel_id=1, source_target_pairs={{0,8},{8,32},{32,40},{40,64},{64,72},{72,96},{96,104},{104,128},{1... | collective-permute-start | bytes 1572872 | tf_op jit(solution)/shard_map/ppermute | solution.py:232
  55.4 19.9 %all-to-all-done.f_ref = f32[32,2,32,128]{3,2,1,0:T(8,128)S(1)} async-done(((f32[32,2,32,128]{3,2,1,0:T(8,128)}), f32[32,2,32,128]{3,2,1,0:T(8,128)S(1)}, u32[]{:S(2)}, u32[]{:S(2)}) %all-to-all-start) | async-done | bytes 1048608 | tf_op jit(solution)/shard_map/all_to_all | solution.py:217
  75.3 1.1 slice_bitcast_fusion.2
  76.3 0.6 collective-permute-start.1
  76.9 2.0 %collective-permute-start = (f32[32,32,128]{2,1,0:T(8,128)}, f32[32,32,128]{2,1,0:T(8,128)}, u32[]{:S(2)}, u32[]{:S(2)}) collective-permute-start(f32[32,32,128]{2,1,0:T(8,128)} %get-tuple-element.12), channel_id=1, source_target_pairs={{0,8},{8,32},{32,40},{40,64},{64,72},{72,96},{96,104},{104,128},{1... | collective-permute-start | bytes 1572872 | tf_op jit(solution)/shard_map/ppermute | solution.py:234
  79.0 0.1 fusion.2.idx_ref
  79.0 0.0 collective-permute-done.5
  79.1 0.0 collective-permute-done.3.pr_ref
  79.1 7.0 %collective-permute-done.1.fr_ref = f32[32,32,128]{2,1,0:T(8,128)} collective-permute-done((f32[32,32,128]{2,1,0:T(8,128)}, f32[32,32,128]{2,1,0:T(8,128)}, u32[]{:S(2)}, u32[]{:S(2)}) %collective-permute-start.1) | collective-permute-done | bytes 524320 | tf_op jit(solution)/shard_map/ppermute | solution.py:235
  86.1 0.0 collective-permute-done.fl_ref
  86.1 13.8 %shard_map.102 = f32[32,2,32,128]{3,2,1,0:T(8,128)S(1)} custom-call(s32[2,2]{1,0:T(2,128)S(1)} %fusion.2.idx_ref, f32[32,2,32,128]{3,2,1,0:T(8,128)S(1)} %all-to-all-done.f_ref, f32[32,32,128]{2,1,0:T(8,128)} %collective-permute-done.fl_ref, f32[32,32,128]{2,1,0:T(8,128)} %collective-permute-done.1.fr_ref, f32[32,2,32,128]{3,2,1,0:T(8,128)S(1)} %all-to-all-done.1.p_ref, ...), custom_call_target="tpu_custom_call" | custom-call | tf_op jit(solution)/shard_map/pallas_call | solution.py:241
  100.0 39.5 %all_to_all.15 = f32[32,2,32,128]{3,2,1,0:T(8,128)S(1)} all-to-all(f32[32,2,32,128]{3,2,1,0:T(8,128)S(1)} %shard_map.102), channel_id=1, replica_groups=mesh['mem'=32,'space'=8] {'mem'}, dimensions={0} | all-to-all | bytes 2097152 | tf_op jit(solution)/shard_map/all_to_all | solution.py:244
  139.5 1.9 %shard_map.103 = f32[2048,128]{1,0:T(8,128)} custom-call(f32[64,32,128]{2,1,0:T(8,128)S(1)} %bitcast.25), custom_call_target="tpu_custom_call" | custom-call | tf_op jit(solution)/shard_map/pallas_call | solution.py:245
  (21 shorter events, 0.1 us)
Async XLA Ops:
  0.0 51.5 %copy-start = (s32[64,2]{0,1:T(2,128)S(1)}, s32[64,2]{0,1:T(2,128)}, u32[]{:S(2)}) copy-start(s32[64,2]{0,1:T(2,128)} %param.14) | copy-start | bytes 1540
  0.0 1.2 copy-start.2
  2.8 10.5 %copy-start.8 = (s32[64,128]{1,0:T(8,128)S(1)}, s32[64,128]{1,0:T(8,128)}, u32[]{:S(2)}) copy-start(s32[64,128]{1,0:T(8,128)} %param.12) | copy-start | bytes 98308
  2.9 11.6 %copy-start.1 = (f32[32,64,128]{2,1,0:T(8,128)S(1)}, f32[32,64,128]{2,1,0:T(8,128)}, u32[]{:S(2)}) copy-start(f32[32,64,128]{2,1,0:T(8,128)} %param.10) | copy-start | bytes 3145732
  2.9 38.8 %all-to-all-start.1 = ((f32[32,2,32,128]{3,2,1,0:T(8,128)}), f32[32,2,32,128]{3,2,1,0:T(8,128)S(1)}, u32[]{:S(2)}, u32[]{:S(2)}) async-start(f32[32,2,32,128]{3,2,1,0:T(8,128)} %bitcast.8), calls=%async_computation.1 | async-start | bytes 2097152 | tf_op jit(solution)/shard_map/all_to_all | solution.py:206
  13.4 0.8 copy-start.7
  14.2 0.8 copy-start.3
  14.4 0.7 copy-start.4
  14.4 0.7 copy-start.5
  14.4 0.7 copy-start.6
  15.1 8.8 %copy-start.9 = (f32[64,128]{1,0:T(8,128)S(1)}, f32[64,128]{1,0:T(8,128)}, u32[]{:S(2)}) copy-start(f32[64,128]{1,0:T(8,128)} %param.13) | copy-start | bytes 98308
  41.6 33.6 %all-to-all-start = ((f32[32,2,32,128]{3,2,1,0:T(8,128)}), f32[32,2,32,128]{3,2,1,0:T(8,128)S(1)}, u32[]{:S(2)}, u32[]{:S(2)}) async-start(f32[32,2,32,128]{3,2,1,0:T(8,128)} %bitcast.4), calls=%async_computation | async-start | bytes 2097152 | tf_op jit(solution)/shard_map/all_to_all | solution.py:217
  46.3 30.6 %collective-permute-start.4 = (f32[1,256]{1,0:T(1,128)S(1)}, f32[1,256]{1,0:T(1,128)S(1)}, u32[]{:S(2)}, u32[]{:S(2)}) collective-permute-start(f32[1,256]{1,0:T(1,128)S(1)} %get-tuple-element.13), channel_id=1, source_target_pairs={{0,1},{1,2},{2,3},{3,4},{4,5},{5,6},{6,7},{7,0},{8,9},{9,10},{10,1... | collective-permute-start | bytes 3080 | tf_op jit(solution)/shard_map/ppermute | solution.py:220
  47.7 31.3 %collective-permute-start.5 = (f32[1,256]{1,0:T(1,128)S(1)}, f32[1,256]{1,0:T(1,128)S(1)}, u32[]{:S(2)}, u32[]{:S(2)}) collective-permute-start(f32[1,256]{1,0:T(1,128)S(1)} %get-tuple-element.14), channel_id=1, source_target_pairs={{1,0},{2,1},{3,2},{4,3},{5,4},{6,5},{7,6},{0,7},{9,8},{10,9},{11,1... | collective-permute-start | bytes 3080 | tf_op jit(solution)/shard_map/ppermute | solution.py:221
  52.7 26.4 %collective-permute-start.3 = (f32[32,32,128]{2,1,0:T(8,128)}, f32[32,32,128]{2,1,0:T(8,128)S(1)}, u32[]{:S(2)}, u32[]{:S(2)}) collective-permute-start(f32[32,32,128]{2,1,0:T(8,128)} %get-tuple-element.9), channel_id=1, source_target_pairs={{0,31},{8,0},{32,8},{40,32},{64,40},{72,64},{96,72},{104,96},{128,... | collective-permute-start | bytes 1572872 | tf_op jit(solution)/shard_map/ppermute | solution.py:233
  53.6 25.5 %collective-permute-start.2 = (f32[32,32,128]{2,1,0:T(8,128)}, f32[32,32,128]{2,1,0:T(8,128)S(1)}, u32[]{:S(2)}, u32[]{:S(2)}) collective-permute-start(f32[32,32,128]{2,1,0:T(8,128)} %get-tuple-element.10), channel_id=1, source_target_pairs={{0,8},{8,32},{32,40},{40,64},{64,72},{72,96},{96,104},{104,128},{1... | collective-permute-start | bytes 1572872 | tf_op jit(solution)/shard_map/ppermute | solution.py:232
  76.3 9.8 %collective-permute-start.1 = (f32[32,32,128]{2,1,0:T(8,128)}, f32[32,32,128]{2,1,0:T(8,128)}, u32[]{:S(2)}, u32[]{:S(2)}) collective-permute-start(f32[32,32,128]{2,1,0:T(8,128)} %get-tuple-element.11), channel_id=1, source_target_pairs={{0,31},{8,0},{32,8},{40,32},{64,40},{72,64},{96,72},{104,96},{128,... | collective-permute-start | bytes 1572872 | tf_op jit(solution)/shard_map/ppermute | solution.py:235
  76.9 9.2 %collective-permute-start = (f32[32,32,128]{2,1,0:T(8,128)}, f32[32,32,128]{2,1,0:T(8,128)}, u32[]{:S(2)}, u32[]{:S(2)}) collective-permute-start(f32[32,32,128]{2,1,0:T(8,128)} %get-tuple-element.12), channel_id=1, source_target_pairs={{0,8},{8,32},{32,40},{40,64},{64,72},{72,96},{96,104},{104,128},{1... | collective-permute-start | bytes 1572872 | tf_op jit(solution)/shard_map/ppermute | solution.py:234
where the time goes:
time: 142 us; the launch traced here: 141 us
  waiting for transfers between devices  44.7 us (31%)
  blocking collectives  39.5 us (28%)
  Pallas kernels  26.2 us (18%)
  starting transfers between devices  25.7 us (18%)
  local copies, waits for them, and re-layouts  5.15 us (4%)
    all_to_all x1, blocking collectives, body(): returned = lax.all_to_all(analysis, 'mem', 0, 0, tiled=True)  39.5 us
    all_to_all x1, waiting for transfers between devices, body(): field = lax.all_to_all(field_send.reshape(packed), 'mem', 0, 0, tiled=True)  19.9 us
    all_to_all x1, waiting for transfers between devices, body(): pert = lax.all_to_all(pert_send.reshape(packed), 'mem', 0, 0, tiled=True)  17.7 us
    pallas_call x1, Pallas kernels, body(): vmem_call(update_kernel, packed, [half, half, full, full, full, full, squ...  13.8 us
    all_to_all x1, starting transfers between devices, body(): pert = lax.all_to_all(pert_send.reshape(packed), 'mem', 0, 0, tiled=True)  10.5 us
    pallas_call x1, Pallas kernels, body(): vmem_call(forecast_kernel, sent, [pltpu.VMEM((2 * LEV, 2 * HID), BF16), p...  8.78 us
    ppermute x1, waiting for transfers between devices, body(): field_right = lax.ppermute(field[:, 0], both, leftward)  7.03 us
    all_to_all x1, starting transfers between devices, body(): field = lax.all_to_all(field_send.reshape(packed), 'mem', 0, 0, tiled=True)  4.68 us
  transfers between devices with their start and end apart: 8, of which 3 were waited for; matrix products, arithmetic and copies ran while one was open for 2% of the time, Pallas kernels for 6%

commit v1 on v0

--- a/solution.py
+++ b/solution.py
@@ -1,3 +1,5 @@
+import functools
+
 import jax
 import jax.numpy as jnp
 from jax import lax
@@ -10,6 +12,7 @@
 HOPS = 2
 PV = 128
 NMEM = 32
+PART = 16
 PAIRS = 32
 F32 = jnp.float32
 BF16 = jnp.bfloat16
@@ -56,16 +59,19 @@
     return dot(ah, bh) + (dot(ah, bl) + dot(al, bh))
 
 
-def to_send_kernel(x_ref, o_ref):
+def to_send_kernel(x_ref, *o_refs):
     for patch in range(2 * PAIRS):
         row = 2 * owner_of(patch // 2) + patch % 2
-        o_ref[row] = x_ref[pl.ds(patch, NMEM, stride=2 * PAIRS), :]
-
-
-def from_sent_kernel(x_ref, o_ref):
+        for part, o_ref in enumerate(o_refs):
+            first = patch + 2 * PAIRS * PART * part
+            o_ref[row] = x_ref[pl.ds(first, PART, stride=2 * PAIRS), :]
+
+
+def from_sent_kernel(x_ref, *rest):
+    o_ref = rest[-1]
     for patch in range(2 * PAIRS):
         row = 2 * owner_of(patch // 2) + patch % 2
-        o_ref[pl.ds(patch, NMEM, stride=2 * PAIRS), :] = x_ref[row]
+        o_ref[pl.ds(patch, PART, stride=2 * PAIRS), :] = x_ref[row]
 
 
 def forecast_kernel(x_ref, g_ref, wi_ref, bi_ref, wo_ref, bo_ref, o_ref, wi2, wo2):
@@ -102,26 +108,20 @@
             o_ref[2 * owner_of(patch // 2) + patch % 2] = x[i * NMEM : (i + 1) * NMEM]
 
 
-def update_kernel(
-    idx_ref, f_ref, fl_ref, fr_ref, p_ref, pl_ref, pr_ref, slot_ref, var_ref, o_ref,
-    ah, al, bh, bl, dh, dl, s_ref, x_ref,
+def solve_kernel(
+    idx_ref, f_ref, fl_ref, fr_ref, slot_ref, var_ref, k_ref, ah, al, bh, bl, s_ref, x_ref
 ):
     members = NMEM * NMEM
     fields = (fl_ref, f_ref.at[:, 0], f_ref.at[:, 1], fr_ref)
-    readings = (pl_ref, p_ref.at[:, 0], p_ref.at[:, 1], pr_ref)
     root = lax.rsqrt(var_ref[...])
     for w in range(4):
         x = fields[w][...].reshape(members, PV)
         if w in (1, 2):
             a = x - jnp.mean(x, axis=0, keepdims=True)
             ah[w - 1], al[w - 1] = split(a)
-        slots = jnp.broadcast_to(slot_ref[w : w + 1, :], (members, PV))
-        y = jnp.take_along_axis(x, slots, axis=1, mode="promise_in_bounds")
-        r = root[w : w + 1, :]
-        b = (y - jnp.mean(y, axis=0, keepdims=True)) * r
+        y = observe(x, slot_ref, w)
+        b = (y - jnp.mean(y, axis=0, keepdims=True)) * root[w : w + 1, :]
         bh[w], bl[w] = split(b)
-        d = (readings[w][...].reshape(members, PV) - y) * r
-        dh[w], dl[w] = split(d)
     eye = jnp.where(
         lax.broadcasted_iota(jnp.int32, (2 * PV, 2 * PV), 0)
         == lax.broadcasted_iota(jnp.int32, (2 * PV, 2 * PV), 1),
@@ -171,24 +171,74 @@
             k = k + dot3(
                 x, g - jnp.dot(s, k, precision=lax.Precision.HIGHEST, preferred_element_type=F32)
             )
-        kh, kl = split(k)
+        k_ref[j] = k
+
+
+def apply_kernel(
+    part, idx_ref, k_ref, f_ref, fl_ref, fr_ref, p_ref, pl_ref, pr_ref, slot_ref, var_ref, o_ref,
+    dh, dl,
+):
+    members = NMEM * PART
+    here = pl.ds(part * PART, PART)
+    fields = (fl_ref.at[:, here], f_ref.at[:, 0, here], f_ref.at[:, 1, here], fr_ref.at[:, here])
+    readings = (pl_ref, p_ref.at[:, 0], p_ref.at[:, 1], pr_ref)
+    root = lax.rsqrt(var_ref[...])
+    for w in range(4):
+        y = observe(fields[w][...].reshape(members, PV), slot_ref, w)
+        d = (readings[w][...].reshape(members, PV) - y) * root[w : w + 1, :]
+        dh[w], dl[w] = split(d)
+    for j in range(2):
+        kh, kl = split(k_ref[j])
         one, two = idx_ref[j, 0], idx_ref[j, 1]
         ih = jnp.concatenate([dh[one], dh[two]], axis=1)
         il = jnp.concatenate([dl[one], dl[two]], axis=1)
         gained = dot(ih, kh) + (dot(ih, kl) + dot(il, kh))
-        o_ref[:, j] = fields[1 + j][...] + gained.reshape(NMEM, NMEM, PV)
-
-
-def vmem_call(kernel, out, scratch=(), smem=0, limit=48, n_in=1):
+        o_ref[:, j] = fields[1 + j][...] + gained.reshape(NMEM, PART, PV)
+
+
+def observe(x, slot_ref, w):
+    slots = jnp.broadcast_to(slot_ref[w : w + 1, :], x.shape)
+    return jnp.take_along_axis(x, slots, axis=1, mode="promise_in_bounds")
+
+
+def is_shape(x):
+    return isinstance(x, tuple) and isinstance(x[0], int)
+
+
+def rows_call(part, x, held=None):
+    rows = 2 * PAIRS * PART
+    specs = [pl.BlockSpec(x.shape, lambda i: (0, 0, 0))]
+    if held is not None:
+        specs.append(pl.BlockSpec(memory_space=pl.ANY))
+    return pl.pallas_call(
+        from_sent_kernel,
+        grid=(1,),
+        out_shape=jax.ShapeDtypeStruct((2 * PAIRS * NMEM, PV), F32),
+        in_specs=specs,
+        out_specs=pl.BlockSpec((rows, PV), lambda i: (part, 0)),
+        input_output_aliases={} if held is None else {1: 0},
+        compiler_params=pltpu.CompilerParams(vmem_limit_bytes=16 << 20),
+        cost_estimate=pl.CostEstimate(flops=10**9, bytes_accessed=1 << 20, transcendentals=0),
+    )(x, *([] if held is None else [held]))
+
+
+def vmem_call(kernel, out, scratch=(), smem=0, limit=48, n_in=1, us=2):
     specs = [pl.BlockSpec(memory_space=pltpu.SMEM)] * smem
     specs += [pl.BlockSpec(memory_space=pltpu.VMEM)] * (n_in - smem)
     return pl.pallas_call(
         kernel,
-        out_shape=jax.ShapeDtypeStruct(out, F32),
+        out_shape=jax.tree.map(
+            lambda shape: jax.ShapeDtypeStruct(shape, F32), out, is_leaf=is_shape
+        ),
         in_specs=specs,
-        out_specs=pl.BlockSpec(memory_space=pltpu.VMEM),
+        out_specs=jax.tree.map(
+            lambda _: pl.BlockSpec(memory_space=pltpu.VMEM), out, is_leaf=is_shape
+        ),
         scratch_shapes=list(scratch),
         compiler_params=pltpu.CompilerParams(vmem_limit_bytes=limit << 20),
+        cost_estimate=pl.CostEstimate(
+            flops=us * 10**9, bytes_accessed=1 << 20, transcendentals=0
+        ),
     )
 
 
@@ -202,20 +252,19 @@
     both = ("mem", "space")
     first = 2 * pair_of(lax.axis_index("mem"))
 
-    pert_send = vmem_call(to_send_kernel, sent)(perturbed_obs.reshape(rows, PV))
-    pert = lax.all_to_all(pert_send.reshape(packed), "mem", 0, 0, tiled=True)
-
     field_send = vmem_call(
         forecast_kernel, sent,
-        [pltpu.VMEM((2 * LEV, 2 * HID), BF16), pltpu.VMEM((2 * HID, 2 * LEV), BF16)], n_in=6,
+        [pltpu.VMEM((2 * LEV, 2 * HID), BF16), pltpu.VMEM((2 * HID, 2 * LEV), BF16)], n_in=6, us=8,
     )(
         prior_sample_set.reshape(rows, PV), norm_gain.reshape(1, -1), w_in, b_in.reshape(1, -1),
         w_out, b_out.reshape(1, -1),
     )
-    meta = jnp.concatenate([measured_slot_table.astype(F32), obs_var], axis=-1)
-    field_send, meta = lax.optimization_barrier((field_send, meta))
+    field_send, readings, slot_table, variances, named = lax.optimization_barrier(
+        (field_send, perturbed_obs, measured_slot_table, obs_var, neighbours)
+    )
     field = lax.all_to_all(field_send.reshape(packed), "mem", 0, 0, tiled=True)
 
+    meta = jnp.concatenate([slot_table.astype(F32), variances], axis=-1)
     runs = [(i, (i + 1) % 8) for i in range(8)]
     before = lax.ppermute(meta[-1:], "space", runs)
     after = lax.ppermute(meta[:1], "space", [(j, i) for i, j in runs])
@@ -223,26 +272,48 @@
         jnp.concatenate([before, meta, after], axis=0), first, 4, 0
     )
     slots, variances = window[:, :PV].astype(jnp.int32), window[:, PV:]
-    named = lax.dynamic_slice_in_dim(neighbours, first, 2, 0)
     own = jnp.arange(2, dtype=jnp.int32)[:, None]
     place = lax.axis_index("space") * (2 * PAIRS) + first + own
-    index = (named - place + 1) % 512 + own
+    index = (lax.dynamic_slice_in_dim(named, first, 2, 0) - place + 1) % 512 + own
+    readings, slots, variances, index = lax.optimization_barrier(
+        (readings, slots, variances, index)
+    )
+    piece = (2 * PAIRS, PART, PV)
+    sends = vmem_call(to_send_kernel, (piece, piece))(readings.reshape(rows, PV))
 
     rightward, leftward = neighbour_moves(1), neighbour_moves(-1)
-    pert_left = lax.ppermute(pert[:, 1], both, rightward)
-    pert_right = lax.ppermute(pert[:, 0], both, leftward)
     field_left = lax.ppermute(field[:, 1], both, rightward)
     field_right = lax.ppermute(field[:, 0], both, leftward)
+    packed = (NMEM, 2, PART, PV)
+    send, _ = lax.optimization_barrier((sends[0], field))
+    pert_a = lax.all_to_all(send.reshape(packed), "mem", 0, 0, tiled=True)
+    send, _ = lax.optimization_barrier((sends[1], pert_a))
+    pert_b = lax.all_to_all(send.reshape(packed), "mem", 0, 0, tiled=True)
+
+    def halo(pert):
+        return lax.ppermute(pert[:, 1], both, rightward), lax.ppermute(pert[:, 0], both, leftward)
 
     members = NMEM * NMEM
     half = pltpu.VMEM((2, members, PV), BF16)
     full = pltpu.VMEM((4, members, PV), BF16)
     square = pltpu.VMEM((2, 2 * PV, 2 * PV), F32)
-    analysis = vmem_call(
-        update_kernel, packed, [half, half, full, full, full, full, square, square], smem=1, n_in=9
-    )(index, field, field_left, field_right, pert, pert_left, pert_right, slots, variances)
-    returned = lax.all_to_all(analysis, "mem", 0, 0, tiled=True)
-    out = vmem_call(from_sent_kernel, (rows, PV))(returned.reshape(sent))
+    index, _ = lax.optimization_barrier((index, pert_a))
+    halo_a = halo(pert_a)
+    gain = vmem_call(
+        solve_kernel, (2, 2 * PV, PV), [half, half, full, full, square, square], smem=1, n_in=6,
+        us=15,
+    )(index, field, field_left, field_right, slots, variances)
+    pert_b, gain = lax.optimization_barrier((pert_b, gain))
+    halo_b = halo(pert_b)
+
+    quarter = pltpu.VMEM((4, NMEM * PART, PV), BF16)
+    out = None
+    for part, (pert, sides) in enumerate(((pert_a, halo_a), (pert_b, halo_b))):
+        analysis = vmem_call(
+            functools.partial(apply_kernel, part), packed, [quarter, quarter], smem=1, n_in=10
+        )(index, gain, field, field_left, field_right, pert, *sides, slots, variances)
+        returned = lax.all_to_all(analysis, "mem", 0, 0, tiled=True)
+        out = rows_call(part, returned.reshape(piece), out)
     return out.reshape(prior_sample_set.shape)
 
 

time: 142 us -> 151 us (1.063)
  blocking collectives: 39.5 us -> 0 us
  waiting for transfers between devices: 44.7 us -> 66 us
  starting transfers between devices: 25.7 us -> 45.4 us
  Pallas kernels: 26.2 us -> 29.8 us
  local copies, waits for them, and re-layouts: 5.15 us -> 7.97 us
    all_to_all x1 -> x0, blocking collectives: 39.5 us -> none  [body(): returned = lax.all_to_all(analysis, 'mem', 0, 0, tiled=True)]
    all_to_all x1 -> x4, waiting for transfers between devices: 17.7 us -> 35.5 us  [the longest x2 19.1 us: body(): returned = lax.all_to_all(analysis, 'mem', 0, 0, tiled=True)]
    all_to_all x1 -> x4, starting transfers between devices: 10.5 us -> 26.6 us  [the longest x2 16.6 us: body(): returned = lax.all_to_all(analysis, 'mem', 0, 0, tiled=True)]
    ppermute x2 -> x4, waiting for transfers between devices: 0.01 us -> 9.75 us  [the longest x2 5.11 us: halo(): lax.ppermute(pert[:, 1], both, rightward)]
    ppermute x1, waiting for transfers between devices: 7.03 us -> 0.01 us  [body(): field_right = lax.ppermute(field[:, 0], both, leftward)]
    all_to_all x1, starting transfers between devices: 4.68 us -> 10.5 us  [body(): field = lax.all_to_all(field_send.reshape(packed), 'mem', 0, 0, tiled=True)]
    ppermute x1, waiting for transfers between devices: 0.01 us -> 5.27 us  [body(): before = lax.ppermute(meta[-1:], 'space', runs)]
    all_to_all x1, waiting for transfers between devices: 19.9 us -> 15.4 us  [body(): field = lax.all_to_all(field_send.reshape(packed), 'mem', 0, 0, tiled=True)]
  transfers between devices with their start and end apart: 8 -> 13, of which waited for: 3 -> 8; matrix products, arithmetic and copies ran while one was open for 2% -> 1% of each run, Pallas kernels for 6% -> 11%
where the time goes in v1:
time: 151 us; the launch traced here: 149 us
  waiting for transfers between devices  66 us (44%)
  starting transfers between devices  45.4 us (30%)
  Pallas kernels  29.8 us (20%)
  local copies, waits for them, and re-layouts  7.97 us (5%)
    all_to_all x2, waiting for transfers between devices, body(): returned = lax.all_to_all(analysis, 'mem', 0, 0, tiled=True)  19.1 us
    all_to_all x2, starting transfers between devices, body(): returned = lax.all_to_all(analysis, 'mem', 0, 0, tiled=True)  16.6 us
    all_to_all x1, waiting for transfers between devices, body(): field = lax.all_to_all(field_send.reshape(packed), 'mem', 0, 0, tiled=True)  15.4 us
    all_to_all x1, waiting for transfers between devices, body(): pert_a = lax.all_to_all(send.reshape(packed), 'mem', 0, 0, tiled=True)  14.5 us
    pallas_call x1, Pallas kernels, body(): vmem_call(solve_kernel, (2, 2 * PV, PV), [half, half, full, full, square,...  12.1 us
    all_to_all x1, starting transfers between devices, body(): field = lax.all_to_all(field_send.reshape(packed), 'mem', 0, 0, tiled=True)  10.5 us
    pallas_call x1, Pallas kernels, body(): vmem_call(forecast_kernel, sent, [pltpu.VMEM((2 * LEV, 2 * HID), BF16), p...  8.76 us
    unnamed x25, local copies, waits for them, and re-layouts  5.95 us
  transfers between devices with their start and end apart: 13, of which 8 were waited for; matrix products, arithmetic and copies ran while one was open for 1% of the time, Pallas kernels for 11%

profile of v1, /device:TPU:3, one launch (start us, length us, event | category | flops | bytes accessed | tf_op | source)
XLA Modules:
  0.0 149.4 jit_solution(12477572987379287521)
XLA Ops:
  0.0 1.0 copy.29.wo_ref
  1.7 1.2 copy-done
  2.9 8.8 %shard_map.100 = f32[64,32,128]{2,1,0:T(8,128)} custom-call(f32[2048,128]{1,0:T(8,128)S(1)} %bitcast.33, f32[1,64]{1,0:T(1,128)S(1)} %bitcast.36, bf16[64,512]{1,0:T(8,128)(2,1)S(1)} %copy-done.2, f32[1,512]{1,0:T(1,128)S(1)} %bitcast.35, bf16[512,64]{1,0:T(8,128)(2,1)S(1)} %copy.29.wo_ref, f32[1,64]{1,0:T(1,128)S(1)} %bitcast.37), custom_call_target="tpu_custom_call" | custom-call | flops 8000000000 | bytes 1048576 | tf_op jit(solution)/shard_map/pallas_call | solution.py:255
  11.7 10.5 %all-to-all-start = ((f32[32,2,32,128]{3,2,1,0:T(8,128)}), f32[32,2,32,128]{3,2,1,0:T(8,128)S(1)}, u32[]{:S(2)}, u32[]{:S(2)}) async-start(f32[32,2,32,128]{3,2,1,0:T(8,128)} %bitcast.5), calls=%async_computation | async-start | bytes 2097152 | tf_op jit(solution)/shard_map/all_to_all | solution.py:265
  22.3 0.7 copy-done.9
  23.0 4.3 %collective-permute-start.1 = (f32[1,256]{1,0:T(1,128)S(1)}, f32[1,256]{1,0:T(1,128)S(1)}, u32[]{:S(2)}, u32[]{:S(2)}) collective-permute-start(f32[1,256]{1,0:T(1,128)S(1)} %get-tuple-element.44), channel_id=1, source_target_pairs={{1,0},{2,1},{3,2},{4,3},{5,4},{6,5},{7,6},{0,7},{9,8},{10,9},{11,1... | collective-permute-start | bytes 3080 | tf_op jit(solution)/shard_map/ppermute | solution.py:270
  27.3 0.7 copy-done.11
  28.2 5.3 %collective-permute-done = f32[1,256]{1,0:T(1,128)S(1)} collective-permute-done((f32[1,256]{1,0:T(1,128)S(1)}, f32[1,256]{1,0:T(1,128)S(1)}, u32[]{:S(2)}, u32[]{:S(2)}) %collective-permute-start) | collective-permute-done | bytes 1056 | tf_op jit(solution)/shard_map/ppermute | solution.py:269
  33.5 1.6 %shard_map.101 = (f32[64,16,128]{2,1,0:T(8,128)}, f32[64,16,128]{2,1,0:T(8,128)}) custom-call(f32[2048,128]{1,0:T(8,128)S(1)} %bitcast.34), custom_call_target="tpu_custom_call" | custom-call | flops 2000000000 | bytes 1048576 | tf_op jit(solution)/shard_map/pallas_call | solution.py:282
  35.0 15.4 %all-to-all-done.f_ref = f32[32,2,32,128]{3,2,1,0:T(8,128)S(1)} async-done(((f32[32,2,32,128]{3,2,1,0:T(8,128)}), f32[32,2,32,128]{3,2,1,0:T(8,128)S(1)}, u32[]{:S(2)}, u32[]{:S(2)}) %all-to-all-start) | async-done | bytes 1048608 | tf_op jit(solution)/shard_map/all_to_all | solution.py:265
  50.5 4.6 %all-to-all-start.1 = ((f32[32,2,16,128]{3,2,1,0:T(8,128)}), f32[32,2,16,128]{3,2,1,0:T(8,128)S(1)}, u32[]{:S(2)}, u32[]{:S(2)}) async-start(f32[32,2,16,128]{3,2,1,0:T(8,128)} %bitcast.6), calls=%async_computation.1 | async-start | bytes 1048576 | tf_op jit(solution)/shard_map/all_to_all | solution.py:289
  55.1 1.1 slice_bitcast_fusion
  56.2 1.3 collective-permute-start.2
  57.5 14.5 %all-to-all-done.1.p_ref = f32[32,2,16,128]{3,2,1,0:T(8,128)S(1)} async-done(((f32[32,2,16,128]{3,2,1,0:T(8,128)}), f32[32,2,16,128]{3,2,1,0:T(8,128)S(1)}, u32[]{:S(2)}, u32[]{:S(2)}) %all-to-all-start.1) | async-done | bytes 524320 | tf_op jit(solution)/shard_map/all_to_all | solution.py:289
  72.0 5.4 %all-to-all-start.2 = ((f32[32,2,16,128]{3,2,1,0:T(8,128)}), f32[32,2,16,128]{3,2,1,0:T(8,128)S(1)}, u32[]{:S(2)}, u32[]{:S(2)}) async-start(f32[32,2,16,128]{3,2,1,0:T(8,128)} %bitcast.7), calls=%async_computation.2 | async-start | bytes 1048576 | tf_op jit(solution)/shard_map/all_to_all | solution.py:291
  77.4 0.8 slice_bitcast_fusion.2
  78.2 1.3 collective-permute-start.6
  79.6 12.1 %shard_map.102.k_ref = f32[2,256,128]{2,1,0:T(8,128)S(1)} custom-call(s32[2,2]{1,0:T(2,128)S(1)} %fusion.3.idx_ref, f32[32,2,32,128]{3,2,1,0:T(8,128)S(1)} %all-to-all-done.f_ref, f32[32,32,128]{2,1,0:T(8,128)S(1)} %collective-permute-done.2.fl_ref, f32[32,32,128]{2,1,0:T(8,128)S(1)} %collective-permute-done.3.fr_ref, ...), custom_call_target="tpu_custom_call" | custom-call | flops 15000000512 | bytes 1048576 | tf_op jit(solution)/shard_map/pallas_call | solution.py:302
  91.7 0.7 copy-done.6
  92.4 1.9 %all-to-all-done.2.p_ref = f32[32,2,16,128]{3,2,1,0:T(8,128)S(1)} async-done(((f32[32,2,16,128]{3,2,1,0:T(8,128)}), f32[32,2,16,128]{3,2,1,0:T(8,128)S(1)}, u32[]{:S(2)}, u32[]{:S(2)}) %all-to-all-start.2) | async-done | bytes 524320 | tf_op jit(solution)/shard_map/all_to_all | solution.py:291
  94.3 0.9 copy-done.7
  95.3 2.7 %shard_map.104 = f32[32,2,16,128]{3,2,1,0:T(8,128)} custom-call(s32[2,2]{1,0:T(2,128)S(1)} %fusion.3.idx_ref, f32[2,256,128]{2,1,0:T(8,128)S(1)} %copy-done.7, f32[32,2,32,128]{3,2,1,0:T(8,128)S(1)} %all-to-all-done.f_ref, f32[32,32,128]{2,1,0:T(8,128)S(1)} %collective-permute-done.2.fl_ref, f32[32,32,128]{2,1,0:T(8,128)S(1)} %collective-permute-done.3.fr_ref, ...), custom_call_target="tpu_custom_call" | custom-call | flops 2000000000 | bytes 1048576 | tf_op jit(solution)/shard_map/pallas_call | solution.py:312
  97.9 7.2 %all-to-all-start.4 = ((f32[32,2,16,128]{3,2,1,0:T(8,128)}), f32[32,2,16,128]{3,2,1,0:T(8,128)S(1)}, u32[]{:S(2)}, u32[]{:S(2)}) async-start(f32[32,2,16,128]{3,2,1,0:T(8,128)} %shard_map.104), calls=%async_computation.4 | async-start | bytes 1048576 | tf_op jit(solution)/shard_map/all_to_all | solution.py:315
  105.2 1.3 collective-permute-start.4
  106.5 5.1 %collective-permute-done.4.pl_ref = f32[32,16,128]{2,1,0:T(8,128)S(1)} collective-permute-done((f32[32,16,128]{2,1,0:T(8,128)S(1)}, f32[32,16,128]{2,1,0:T(8,128)S(1)}, u32[]{:S(2)}, u32[]{:S(2)}) %collective-permute-start.4) | collective-permute-done | bytes 262176 | tf_op jit(solution)/shard_map/ppermute | solution.py:294
  111.6 4.6 %collective-permute-done.5.pr_ref = f32[32,16,128]{2,1,0:T(8,128)S(1)} collective-permute-done((f32[32,16,128]{2,1,0:T(8,128)S(1)}, f32[32,16,128]{2,1,0:T(8,128)S(1)}, u32[]{:S(2)}, u32[]{:S(2)}) %collective-permute-start.5) | collective-permute-done | bytes 262176 | tf_op jit(solution)/shard_map/ppermute | solution.py:294
  116.2 2.3 %shard_map.103 = f32[32,2,16,128]{3,2,1,0:T(8,128)} custom-call(s32[2,2]{1,0:T(2,128)S(1)} %fusion.3.idx_ref, f32[2,256,128]{2,1,0:T(8,128)S(1)} %copy-done.8, f32[32,2,32,128]{3,2,1,0:T(8,128)S(1)} %all-to-all-done.f_ref, f32[32,32,128]{2,1,0:T(8,128)S(1)} %collective-permute-done.2.fl_ref, f32[32,32,128]{2,1,0:T(8,128)S(1)} %collective-permute-done.3.fr_ref, ...), custom_call_target="tpu_custom_call" | custom-call | flops 2000000000 | bytes 1048576 | tf_op jit(solution)/shard_map/pallas_call | solution.py:312
  118.5 3.5 %all-to-all-done.4 = f32[32,2,16,128]{3,2,1,0:T(8,128)S(1)} async-done(((f32[32,2,16,128]{3,2,1,0:T(8,128)}), f32[32,2,16,128]{3,2,1,0:T(8,128)S(1)}, u32[]{:S(2)}, u32[]{:S(2)}) %all-to-all-start.4) | async-done | bytes 524320 | tf_op jit(solution)/shard_map/all_to_all | solution.py:315
  122.0 9.4 %all-to-all-start.3 = ((f32[32,2,16,128]{3,2,1,0:T(8,128)}), f32[32,2,16,128]{3,2,1,0:T(8,128)S(1)}, u32[]{:S(2)}, u32[]{:S(2)}) async-start(f32[32,2,16,128]{3,2,1,0:T(8,128)} %shard_map.103), calls=%async_computation.3 | async-start | bytes 1048576 | tf_op jit(solution)/shard_map/all_to_all | solution.py:315
  131.4 1.2 shard_map.105.rest_0_
  132.6 15.6 %all-to-all-done.3 = f32[32,2,16,128]{3,2,1,0:T(8,128)S(1)} async-done(((f32[32,2,16,128]{3,2,1,0:T(8,128)}), f32[32,2,16,128]{3,2,1,0:T(8,128)S(1)}, u32[]{:S(2)}, u32[]{:S(2)}) %all-to-all-start.3) | async-done | bytes 524320 | tf_op jit(solution)/shard_map/all_to_all | solution.py:315
  148.2 1.2 shard_map.106
  (36 shorter events, 1.0 us)
Async XLA Ops:
  0.0 1.0 copy-start.2
  1.0 0.7 copy-start.3
  1.0 0.7 copy-start.4
  1.0 0.7 copy-start.5
  1.7 1.2 copy-start
  11.7 10.5 %copy-start.10 = (s32[64,128]{1,0:T(8,128)S(1)}, s32[64,128]{1,0:T(8,128)}, u32[]{:S(2)}) copy-start(s32[64,128]{1,0:T(8,128)} %param.12) | copy-start | bytes 98308
  11.7 21.8 %copy-start.1 = (f32[32,64,128]{2,1,0:T(8,128)S(1)}, f32[32,64,128]{2,1,0:T(8,128)}, u32[]{:S(2)}) copy-start(f32[32,64,128]{2,1,0:T(8,128)} %param.11) | copy-start | bytes 3145732
  11.7 38.8 %all-to-all-start = ((f32[32,2,32,128]{3,2,1,0:T(8,128)}), f32[32,2,32,128]{3,2,1,0:T(8,128)S(1)}, u32[]{:S(2)}, u32[]{:S(2)}) async-start(f32[32,2,32,128]{3,2,1,0:T(8,128)} %bitcast.5), calls=%async_computation | async-start | bytes 2097152 | tf_op jit(solution)/shard_map/all_to_all | solution.py:265
  22.2 0.8 copy-start.9
  23.0 5.2 %collective-permute-start.1 = (f32[1,256]{1,0:T(1,128)S(1)}, f32[1,256]{1,0:T(1,128)S(1)}, u32[]{:S(2)}, u32[]{:S(2)}) collective-permute-start(f32[1,256]{1,0:T(1,128)S(1)} %get-tuple-element.44), channel_id=1, source_target_pairs={{1,0},{2,1},{3,2},{4,3},{5,4},{6,5},{7,6},{0,7},{9,8},{10,9},{11,1... | collective-permute-start | bytes 3080 | tf_op jit(solution)/shard_map/ppermute | solution.py:270
  27.3 6.1 %collective-permute-start = (f32[1,256]{1,0:T(1,128)S(1)}, f32[1,256]{1,0:T(1,128)S(1)}, u32[]{:S(2)}, u32[]{:S(2)}) collective-permute-start(f32[1,256]{1,0:T(1,128)S(1)} %get-tuple-element.43), channel_id=1, source_target_pairs={{0,1},{1,2},{2,3},{3,4},{4,5},{5,6},{6,7},{7,0},{8,9},{9,10},{10,1... | collective-permute-start | bytes 3080 | tf_op jit(solution)/shard_map/ppermute | solution.py:269
  27.3 0.7 copy-start.11
  50.5 21.6 %all-to-all-start.1 = ((f32[32,2,16,128]{3,2,1,0:T(8,128)}), f32[32,2,16,128]{3,2,1,0:T(8,128)S(1)}, u32[]{:S(2)}, u32[]{:S(2)}) async-start(f32[32,2,16,128]{3,2,1,0:T(8,128)} %bitcast.6), calls=%async_computation.1 | async-start | bytes 1048576 | tf_op jit(solution)/shard_map/all_to_all | solution.py:289
  56.2 23.4 %collective-permute-start.2 = (f32[32,32,128]{2,1,0:T(8,128)}, f32[32,32,128]{2,1,0:T(8,128)S(1)}, u32[]{:S(2)}, u32[]{:S(2)}) collective-permute-start(f32[32,32,128]{2,1,0:T(8,128)} %get-tuple-element.38), channel_id=1, source_target_pairs={{0,8},{8,32},{32,40},{40,64},{64,72},{72,96},{96,104},{104,128},{1... | collective-permute-start | bytes 1572872 | tf_op jit(solution)/shard_map/ppermute | solution.py:285
  57.5 22.1 %collective-permute-start.3 = (f32[32,32,128]{2,1,0:T(8,128)}, f32[32,32,128]{2,1,0:T(8,128)S(1)}, u32[]{:S(2)}, u32[]{:S(2)}) collective-permute-start(f32[32,32,128]{2,1,0:T(8,128)} %get-tuple-element.37), channel_id=1, source_target_pairs={{0,31},{8,0},{32,8},{40,32},{64,40},{72,64},{96,72},{104,96},{128,... | collective-permute-start | bytes 1572872 | tf_op jit(solution)/shard_map/ppermute | solution.py:286
  72.0 22.3 %all-to-all-start.2 = ((f32[32,2,16,128]{3,2,1,0:T(8,128)}), f32[32,2,16,128]{3,2,1,0:T(8,128)S(1)}, u32[]{:S(2)}, u32[]{:S(2)}) async-start(f32[32,2,16,128]{3,2,1,0:T(8,128)} %bitcast.7), calls=%async_computation.2 | async-start | bytes 1048576 | tf_op jit(solution)/shard_map/all_to_all | solution.py:291
  78.2 16.1 %collective-permute-start.6 = (f32[32,16,128]{2,1,0:T(8,128)}, f32[32,16,128]{2,1,0:T(8,128)S(1)}, u32[]{:S(2)}, u32[]{:S(2)}) collective-permute-start(f32[32,16,128]{2,1,0:T(8,128)} %get-tuple-element.40), channel_id=1, source_target_pairs={{0,8},{8,32},{32,40},{40,64},{64,72},{72,96},{96,104},{104,128},{1... | collective-permute-start | bytes 786440 | tf_op jit(solution)/shard_map/ppermute | solution.py:294
  79.6 14.8 %collective-permute-start.7 = (f32[32,16,128]{2,1,0:T(8,128)}, f32[32,16,128]{2,1,0:T(8,128)}, u32[]{:S(2)}, u32[]{:S(2)}) collective-permute-start(f32[32,16,128]{2,1,0:T(8,128)} %get-tuple-element.39), channel_id=1, source_target_pairs={{0,31},{8,0},{32,8},{40,32},{64,40},{72,64},{96,72},{104,96},{128,... | collective-permute-start | bytes 786440 | tf_op jit(solution)/shard_map/ppermute | solution.py:294
  91.7 0.7 copy-start.6
  94.3 1.0 copy-start.7
  97.9 24.0 %all-to-all-start.4 = ((f32[32,2,16,128]{3,2,1,0:T(8,128)}), f32[32,2,16,128]{3,2,1,0:T(8,128)S(1)}, u32[]{:S(2)}, u32[]{:S(2)}) async-start(f32[32,2,16,128]{3,2,1,0:T(8,128)} %shard_map.104), calls=%async_computation.4 | async-start | bytes 1048576 | tf_op jit(solution)/shard_map/all_to_all | solution.py:315
  105.1 11.1 %copy-start.8 = (f32[2,256,128]{2,1,0:T(8,128)S(1)}, f32[2,256,128]{2,1,0:T(8,128)}, u32[]{:S(2)}) copy-start(f32[2,256,128]{2,1,0:T(8,128)} %copy-done.6) | copy-start | bytes 786436
  105.2 6.4 %collective-permute-start.4 = (f32[32,16,128]{2,1,0:T(8,128)S(1)}, f32[32,16,128]{2,1,0:T(8,128)S(1)}, u32[]{:S(2)}, u32[]{:S(2)}) collective-permute-start(f32[32,16,128]{2,1,0:T(8,128)S(1)} %get-tuple-element.42), channel_id=1, source_target_pairs={{0,8},{8,32},{32,40},{40,64},{64,72},{72,96},{96,104},{104,128},{1... | collective-permute-start | bytes 786440 | tf_op jit(solution)/shard_map/ppermute | solution.py:294
  106.5 9.7 %collective-permute-start.5 = (f32[32,16,128]{2,1,0:T(8,128)S(1)}, f32[32,16,128]{2,1,0:T(8,128)S(1)}, u32[]{:S(2)}, u32[]{:S(2)}) collective-permute-start(f32[32,16,128]{2,1,0:T(8,128)S(1)} %get-tuple-element.41), channel_id=1, source_target_pairs={{0,31},{8,0},{32,8},{40,32},{64,40},{72,64},{96,72},{104,96},{128,... | collective-permute-start | bytes 786440 | tf_op jit(solution)/shard_map/ppermute | solution.py:294
  122.0 26.3 %all-to-all-start.3 = ((f32[32,2,16,128]{3,2,1,0:T(8,128)}), f32[32,2,16,128]{3,2,1,0:T(8,128)S(1)}, u32[]{:S(2)}, u32[]{:S(2)}) async-start(f32[32,2,16,128]{3,2,1,0:T(8,128)} %shard_map.103), calls=%async_computation.3 | async-start | bytes 1048576 | tf_op jit(solution)/shard_map/all_to_all | solution.py:315

commit v2 on v0

--- a/solution.py
+++ b/solution.py
@@ -10,6 +10,7 @@
 HOPS = 2
 PV = 128
 NMEM = 32
+STEP = 8
 PAIRS = 32
 F32 = jnp.float32
 BF16 = jnp.bfloat16
@@ -42,6 +43,10 @@
     return jnp.dot(a, b, preferred_element_type=F32)
 
 
+def dot_t(a, b):
+    return lax.dot_general(a, b, (((1,), (1,)), ((), ())), preferred_element_type=F32)
+
+
 def tdot(a, b):
     return lax.dot_general(a, b, (((0,), (0,)), ((), ())), preferred_element_type=F32)
 
@@ -65,27 +70,23 @@
 def from_sent_kernel(x_ref, o_ref):
     for patch in range(2 * PAIRS):
         row = 2 * owner_of(patch // 2) + patch % 2
-        o_ref[pl.ds(patch, NMEM, stride=2 * PAIRS), :] = x_ref[row]
+        o_ref[pl.ds(patch, STEP, stride=2 * PAIRS), :] = x_ref[row]
 
 
 def forecast_kernel(x_ref, g_ref, wi_ref, bi_ref, wo_ref, bo_ref, o_ref, wi2, wo2):
-    wi = (wi_ref[...].astype(F32) * 0.5).astype(BF16)
-    zi = jnp.zeros_like(wi)
-    wi2[:LEV, :HID] = wi
-    wi2[:LEV, HID:] = zi
-    wi2[LEV:, :HID] = zi
-    wi2[LEV:, HID:] = wi
-    wo = wo_ref[...]
-    zo = jnp.zeros_like(wo)
-    wo2[:HID, :] = jnp.concatenate([wo, zo], axis=1)
-    wo2[HID:, :] = jnp.concatenate([zo, wo], axis=1)
+    for both, one in ((wi2, (wi_ref[...].astype(F32) * 0.5).astype(BF16)), (wo2, wo_ref[...])):
+        zero = jnp.zeros_like(one)
+        both[:LEV, :HID] = one
+        both[:LEV, HID:] = zero
+        both[LEV:, :HID] = zero
+        both[LEV:, HID:] = one
     gain = jnp.concatenate([g_ref[...]] * 2, axis=1)
     bi = jnp.concatenate([bi_ref[...]] * 2, axis=1) * 0.5
     bo = jnp.concatenate([bo_ref[...]] * 2, axis=1)
     row = lax.broadcasted_iota(jnp.int32, (2 * PV, PV), 0)
     col = lax.broadcasted_iota(jnp.int32, (2 * PV, PV), 1)
     halves = jnp.where((row % PV) // LEV == col // LEV, 1.0, 0.0).astype(BF16)
-    chunk = 8
+    chunk = PAIRS
     for first in range(0, 2 * PAIRS, chunk):
         x = jnp.concatenate(
             [x_ref[pl.ds(first + i, NMEM, stride=2 * PAIRS), :] for i in range(chunk)], axis=0
@@ -96,32 +97,26 @@
             normed = (x * inverse * gain).astype(BF16)
             h = dot(normed, wi2[...]) + bi
             hidden = (h + h * jnp.tanh(h)).astype(BF16)
-            x = x + dot(hidden, wo2[...]) + bo
+            x = x + dot_t(hidden, wo2[...]) + bo
         for i in range(chunk):
             patch = first + i
             o_ref[2 * owner_of(patch // 2) + patch % 2] = x[i * NMEM : (i + 1) * NMEM]
 
 
-def update_kernel(
-    idx_ref, f_ref, fl_ref, fr_ref, p_ref, pl_ref, pr_ref, slot_ref, var_ref, o_ref,
-    ah, al, bh, bl, dh, dl, s_ref, x_ref,
+def solve_kernel(
+    idx_ref, f_ref, fl_ref, fr_ref, slot_ref, var_ref, k_ref, ah, al, bh, bl, s_ref, x_ref
 ):
     members = NMEM * NMEM
     fields = (fl_ref, f_ref.at[:, 0], f_ref.at[:, 1], fr_ref)
-    readings = (pl_ref, p_ref.at[:, 0], p_ref.at[:, 1], pr_ref)
     root = lax.rsqrt(var_ref[...])
     for w in range(4):
         x = fields[w][...].reshape(members, PV)
         if w in (1, 2):
             a = x - jnp.mean(x, axis=0, keepdims=True)
             ah[w - 1], al[w - 1] = split(a)
-        slots = jnp.broadcast_to(slot_ref[w : w + 1, :], (members, PV))
-        y = jnp.take_along_axis(x, slots, axis=1, mode="promise_in_bounds")
-        r = root[w : w + 1, :]
-        b = (y - jnp.mean(y, axis=0, keepdims=True)) * r
+        y = observe(x, slot_ref, w)
+        b = (y - jnp.mean(y, axis=0, keepdims=True)) * root[w : w + 1, :]
         bh[w], bl[w] = split(b)
-        d = (readings[w][...].reshape(members, PV) - y) * r
-        dh[w], dl[w] = split(d)
     eye = jnp.where(
         lax.broadcasted_iota(jnp.int32, (2 * PV, 2 * PV), 0)
         == lax.broadcasted_iota(jnp.int32, (2 * PV, 2 * PV), 1),
@@ -171,7 +166,22 @@
             k = k + dot3(
                 x, g - jnp.dot(s, k, precision=lax.Precision.HIGHEST, preferred_element_type=F32)
             )
-        kh, kl = split(k)
+        k_ref[j] = k
+
+
+def apply_kernel(
+    idx_ref, k_ref, f_ref, fl_ref, fr_ref, p_ref, pl_ref, pr_ref, slot_ref, var_ref, o_ref, dh, dl
+):
+    members = NMEM * NMEM
+    fields = (fl_ref, f_ref.at[:, 0], f_ref.at[:, 1], fr_ref)
+    readings = (pl_ref, p_ref.at[:, 0], p_ref.at[:, 1], pr_ref)
+    root = lax.rsqrt(var_ref[...])
+    for w in range(4):
+        y = observe(fields[w][...].reshape(members, PV), slot_ref, w)
+        d = (readings[w][...].reshape(members, PV) - y) * root[w : w + 1, :]
+        dh[w], dl[w] = split(d)
+    for j in range(2):
+        kh, kl = split(k_ref[j])
         one, two = idx_ref[j, 0], idx_ref[j, 1]
         ih = jnp.concatenate([dh[one], dh[two]], axis=1)
         il = jnp.concatenate([dl[one], dl[two]], axis=1)
@@ -179,7 +189,22 @@
         o_ref[:, j] = fields[1 + j][...] + gained.reshape(NMEM, NMEM, PV)
 
 
-def vmem_call(kernel, out, scratch=(), smem=0, limit=48, n_in=1):
+def observe(x, slot_ref, w):
+    slots = jnp.broadcast_to(slot_ref[w : w + 1, :], x.shape)
+    return jnp.take_along_axis(x, slots, axis=1, mode="promise_in_bounds")
+
+
+def from_sent(x):
+    return pl.pallas_call(
+        from_sent_kernel,
+        grid=(NMEM // STEP,),
+        out_shape=jax.ShapeDtypeStruct((2 * PAIRS * NMEM, PV), F32),
+        in_specs=[pl.BlockSpec((2 * PAIRS, STEP, PV), lambda i: (0, i, 0))],
+        out_specs=pl.BlockSpec((2 * PAIRS * STEP, PV), lambda i: (i, 0)),
+    )(x)
+
+
+def vmem_call(kernel, out, scratch=(), smem=0, limit=48, n_in=1, us=2):
     specs = [pl.BlockSpec(memory_space=pltpu.SMEM)] * smem
     specs += [pl.BlockSpec(memory_space=pltpu.VMEM)] * (n_in - smem)
     return pl.pallas_call(
@@ -189,6 +214,9 @@
         out_specs=pl.BlockSpec(memory_space=pltpu.VMEM),
         scratch_shapes=list(scratch),
         compiler_params=pltpu.CompilerParams(vmem_limit_bytes=limit << 20),
+        cost_estimate=pl.CostEstimate(
+            flops=us * 10**9, bytes_accessed=1 << 20, transcendentals=0
+        ),
     )
 
 
@@ -202,20 +230,18 @@
     both = ("mem", "space")
     first = 2 * pair_of(lax.axis_index("mem"))
 
-    pert_send = vmem_call(to_send_kernel, sent)(perturbed_obs.reshape(rows, PV))
-    pert = lax.all_to_all(pert_send.reshape(packed), "mem", 0, 0, tiled=True)
-
     field_send = vmem_call(
         forecast_kernel, sent,
-        [pltpu.VMEM((2 * LEV, 2 * HID), BF16), pltpu.VMEM((2 * HID, 2 * LEV), BF16)], n_in=6,
+        [pltpu.VMEM((2 * LEV, 2 * HID), BF16)] * 2, n_in=6, us=8,
     )(
         prior_sample_set.reshape(rows, PV), norm_gain.reshape(1, -1), w_in, b_in.reshape(1, -1),
-        w_out, b_out.reshape(1, -1),
-    )
-    meta = jnp.concatenate([measured_slot_table.astype(F32), obs_var], axis=-1)
-    field_send, meta = lax.optimization_barrier((field_send, meta))
+        w_out.T, b_out.reshape(1, -1),
+    )
+    field_send, readings, slot_table, variances, named = lax.optimization_barrier(
+        (field_send, perturbed_obs, measured_slot_table, obs_var, neighbours)
+    )
     field = lax.all_to_all(field_send.reshape(packed), "mem", 0, 0, tiled=True)
-
+    meta = jnp.concatenate([slot_table.astype(F32), variances], axis=-1)
     runs = [(i, (i + 1) % 8) for i in range(8)]
     before = lax.ppermute(meta[-1:], "space", runs)
     after = lax.ppermute(meta[:1], "space", [(j, i) for i, j in runs])
@@ -223,26 +249,37 @@
         jnp.concatenate([before, meta, after], axis=0), first, 4, 0
     )
     slots, variances = window[:, :PV].astype(jnp.int32), window[:, PV:]
-    named = lax.dynamic_slice_in_dim(neighbours, first, 2, 0)
     own = jnp.arange(2, dtype=jnp.int32)[:, None]
     place = lax.axis_index("space") * (2 * PAIRS) + first + own
-    index = (named - place + 1) % 512 + own
+    index = (lax.dynamic_slice_in_dim(named, first, 2, 0) - place + 1) % 512 + own
+
+    readings, slots, variances, index = lax.optimization_barrier(
+        (readings, slots, variances, index)
+    )
+    pert_send = vmem_call(to_send_kernel, sent)(readings.reshape(rows, PV))
 
     rightward, leftward = neighbour_moves(1), neighbour_moves(-1)
-    pert_left = lax.ppermute(pert[:, 1], both, rightward)
-    pert_right = lax.ppermute(pert[:, 0], both, leftward)
     field_left = lax.ppermute(field[:, 1], both, rightward)
     field_right = lax.ppermute(field[:, 0], both, leftward)
+    pert_send, _ = lax.optimization_barrier((pert_send, field))
+    pert = lax.all_to_all(pert_send.reshape(packed), "mem", 0, 0, tiled=True)
 
     members = NMEM * NMEM
     half = pltpu.VMEM((2, members, PV), BF16)
     full = pltpu.VMEM((4, members, PV), BF16)
     square = pltpu.VMEM((2, 2 * PV, 2 * PV), F32)
-    analysis = vmem_call(
-        update_kernel, packed, [half, half, full, full, full, full, square, square], smem=1, n_in=9
-    )(index, field, field_left, field_right, pert, pert_left, pert_right, slots, variances)
+    gain = vmem_call(
+        solve_kernel, (2, 2 * PV, PV), [half, half, full, full, square, square], smem=1, n_in=6,
+        us=15,
+    )(index, field, field_left, field_right, slots, variances)
+    pert, gain = lax.optimization_barrier((pert, gain))
+    pert_left = lax.ppermute(pert[:, 1], both, rightward)
+    pert_right = lax.ppermute(pert[:, 0], both, leftward)
+    analysis = vmem_call(apply_kernel, packed, [full, full], smem=1, n_in=10)(
+        index, gain, field, field_left, field_right, pert, pert_left, pert_right, slots, variances
+    )
     returned = lax.all_to_all(analysis, "mem", 0, 0, tiled=True)
-    out = vmem_call(from_sent_kernel, (rows, PV))(returned.reshape(sent))
+    out = from_sent(returned.reshape(sent))
     return out.reshape(prior_sample_set.shape)
 
 

time: 142 us -> 150 us (1.056)
  starting transfers between devices: 25.7 us -> 37.3 us
  waiting for transfers between devices: 44.7 us -> 40 us
    all_to_all x1, waiting for transfers between devices: 17.7 us -> 2.12 us  [body(): pert = lax.all_to_all(pert_send.reshape(packed), 'mem', 0, 0, tiled=True)]
    ppermute x1, starting transfers between devices: 0.92 us -> 14.3 us  [body(): pert_right = lax.ppermute(pert[:, 0], both, leftward)]
    all_to_all x1, starting transfers between devices: 10.5 us -> 4.68 us  [body(): pert = lax.all_to_all(pert_send.reshape(packed), 'mem', 0, 0, tiled=True)]
    all_to_all x1, starting transfers between devices: 4.68 us -> 10.5 us  [body(): field = lax.all_to_all(field_send.reshape(packed), 'mem', 0, 0, tiled=True)]
    ppermute x1, waiting for transfers between devices: 7.03 us -> 11.9 us  [body(): field_right = lax.ppermute(field[:, 0], both, leftward)]
    ppermute x1, waiting for transfers between devices: 0.01 us -> 4.59 us  [body(): pert_left = lax.ppermute(pert[:, 1], both, rightward)]
    unnamed x22 -> x20, local copies, waits for them, and re-layouts: 2.98 us -> 5.01 us
    ppermute x1, starting transfers between devices: 1.72 us -> 0.01 us  [body(): pert_left = lax.ppermute(pert[:, 1], both, rightward)]
  transfers between devices with their start and end apart: 8 -> 8, of which waited for: 3 -> 6; matrix products, arithmetic and copies ran while one was open for 2% -> 0% of each run, Pallas kernels for 6% -> 9%
where the time goes in v2:
time: 150 us; the launch traced here: 149 us
  blocking collectives  40.1 us (27%)
  waiting for transfers between devices  40 us (27%)
  starting transfers between devices  37.3 us (25%)
  Pallas kernels  26.2 us (17%)
  local copies, waits for them, and re-layouts  5.26 us (4%)
    all_to_all x1, blocking collectives, body(): returned = lax.all_to_all(analysis, 'mem', 0, 0, tiled=True)  40.1 us
    all_to_all x1, waiting for transfers between devices, body(): field = lax.all_to_all(field_send.reshape(packed), 'mem', 0, 0, tiled=True)  19.8 us
    ppermute x1, starting transfers between devices, body(): pert_right = lax.ppermute(pert[:, 0], both, leftward)  14.3 us
    pallas_call x1, Pallas kernels, body(): vmem_call(solve_kernel, (2, 2 * PV, PV), [half, half, full, full, square,...  12.1 us
    ppermute x1, waiting for transfers between devices, body(): field_right = lax.ppermute(field[:, 0], both, leftward)  11.9 us
    all_to_all x1, starting transfers between devices, body(): field = lax.all_to_all(field_send.reshape(packed), 'mem', 0, 0, tiled=True)  10.5 us
    pallas_call x1, Pallas kernels, body(): vmem_call(forecast_kernel, sent, [pltpu.VMEM((2 * LEV, 2 * HID), BF16)] *...  6.73 us
    unnamed x20, local copies, waits for them, and re-layouts  5.01 us
  transfers between devices with their start and end apart: 8, of which 6 were waited for; matrix products, arithmetic and copies ran while one was open for 0% of the time, Pallas kernels for 9%

profile of v2, /device:TPU:3, one launch (start us, length us, event | category | flops | bytes accessed | tf_op | source)
XLA Modules:
  0.0 149.2 jit_solution(4724129237316146465)
XLA Ops:
  0.0 0.7 copy-done.4
  0.7 1.2 copy-done
  1.9 0.8 copy-done.2
  2.8 0.8 copy-done.3
  3.6 6.7 %shard_map.100 = f32[64,32,128]{2,1,0:T(8,128)} custom-call(f32[2048,128]{1,0:T(8,128)S(1)} %bitcast.22, f32[1,64]{1,0:T(1,128)S(1)} %bitcast.26, bf16[64,512]{1,0:T(8,128)(2,1)S(1)} %copy-done.2, f32[1,512]{1,0:T(1,128)S(1)} %bitcast.25, bf16[64,512]{1,0:T(8,128)(2,1)S(1)} %bitcast.24, f32[1,64]{1,0:T(1,128)S(1)} %bitcast.27), custom_call_target="tpu_custom_call" | custom-call | flops 8000000000 | bytes 1048576 | tf_op jit(solution)/shard_map/pallas_call | solution.py:233
  10.3 10.5 %all-to-all-start = ((f32[32,2,32,128]{3,2,1,0:T(8,128)}), f32[32,2,32,128]{3,2,1,0:T(8,128)S(1)}, u32[]{:S(2)}, u32[]{:S(2)}) async-start(f32[32,2,32,128]{3,2,1,0:T(8,128)} %bitcast.6), calls=%async_computation | async-start | bytes 2097152 | tf_op jit(solution)/shard_map/all_to_all | solution.py:243
  20.9 0.0 copy-start.7
  20.9 0.7 copy-done.7
  21.6 1.3 collective-permute-start
  22.9 3.8 %collective-permute-start.1 = (f32[1,256]{1,0:T(1,128)S(1)}, f32[1,256]{1,0:T(1,128)S(1)}, u32[]{:S(2)}, u32[]{:S(2)}) collective-permute-start(f32[1,256]{1,0:T(1,128)S(1)} %get-tuple-element.34), channel_id=1, source_target_pairs={{1,0},{2,1},{3,2},{4,3},{5,4},{6,5},{7,6},{0,7},{9,8},{10,9},{11,1... | collective-permute-start | bytes 3080 | tf_op jit(solution)/shard_map/ppermute | solution.py:247
  26.7 0.7 copy-done.9
  27.4 0.1 copy.21
  27.5 0.1 fusion.3.idx_ref
  27.6 0.1 collective-permute-done
  27.7 0.0 collective-permute-done.1
  27.7 1.6 %shard_map.101 = f32[64,32,128]{2,1,0:T(8,128)} custom-call(f32[2048,128]{1,0:T(8,128)S(1)} %bitcast.23), custom_call_target="tpu_custom_call" | custom-call | flops 2000000000 | bytes 1048576 | tf_op jit(solution)/shard_map/pallas_call | solution.py:259
  29.3 19.8 %all-to-all-done.f_ref = f32[32,2,32,128]{3,2,1,0:T(8,128)S(1)} async-done(((f32[32,2,32,128]{3,2,1,0:T(8,128)}), f32[32,2,32,128]{3,2,1,0:T(8,128)S(1)}, u32[]{:S(2)}, u32[]{:S(2)}) %all-to-all-start) | async-done | bytes 1048608 | tf_op jit(solution)/shard_map/all_to_all | solution.py:243
  49.1 4.7 %all-to-all-start.1 = ((f32[32,2,32,128]{3,2,1,0:T(8,128)}), f32[32,2,32,128]{3,2,1,0:T(8,128)S(1)}, u32[]{:S(2)}, u32[]{:S(2)}) async-start(f32[32,2,32,128]{3,2,1,0:T(8,128)} %bitcast.7), calls=%async_computation.1 | async-start | bytes 2097152 | tf_op jit(solution)/shard_map/all_to_all | solution.py:265
  53.8 0.1 slice_bitcast_fusion.2
  53.9 0.4 collective-permute-start.3
  54.3 2.3 %collective-permute-start.2 = (f32[32,32,128]{2,1,0:T(8,128)S(1)}, f32[32,32,128]{2,1,0:T(8,128)S(1)}, u32[]{:S(2)}, u32[]{:S(2)}) collective-permute-start(f32[32,32,128]{2,1,0:T(8,128)S(1)} %get-tuple-element.32), channel_id=1, source_target_pairs={{0,8},{8,32},{32,40},{40,64},{64,72},{72,96},{96,104},{104,128},{1... | collective-permute-start | bytes 1572872 | tf_op jit(solution)/shard_map/ppermute | solution.py:262
  56.6 11.9 %collective-permute-done.3.fr_ref = f32[32,32,128]{2,1,0:T(8,128)S(1)} collective-permute-done((f32[32,32,128]{2,1,0:T(8,128)S(1)}, f32[32,32,128]{2,1,0:T(8,128)S(1)}, u32[]{:S(2)}, u32[]{:S(2)}) %collective-permute-start.3) | collective-permute-done | bytes 524320 | tf_op jit(solution)/shard_map/ppermute | solution.py:263
  68.5 0.0 collective-permute-done.2.fl_ref
  68.5 12.1 %shard_map.102.k_ref = f32[2,256,128]{2,1,0:T(8,128)S(1)} custom-call(s32[2,2]{1,0:T(2,128)S(1)} %fusion.3.idx_ref, f32[32,2,32,128]{3,2,1,0:T(8,128)S(1)} %all-to-all-done.f_ref, f32[32,32,128]{2,1,0:T(8,128)S(1)} %collective-permute-done.2.fl_ref, f32[32,32,128]{2,1,0:T(8,128)S(1)} %collective-permute-done.3.fr_ref, ...), custom_call_target="tpu_custom_call" | custom-call | flops 15000000512 | bytes 1048576 | tf_op jit(solution)/shard_map/pallas_call | solution.py:271
  80.6 2.1 %all-to-all-done.1.p_ref = f32[32,2,32,128]{3,2,1,0:T(8,128)S(1)} async-done(((f32[32,2,32,128]{3,2,1,0:T(8,128)}), f32[32,2,32,128]{3,2,1,0:T(8,128)S(1)}, u32[]{:S(2)}, u32[]{:S(2)}) %all-to-all-start.1) | async-done | bytes 1048608 | tf_op jit(solution)/shard_map/all_to_all | solution.py:265
  82.7 0.1 slice_bitcast_fusion
  82.8 14.3 %collective-permute-start.5 = (f32[32,32,128]{2,1,0:T(8,128)S(1)}, f32[32,32,128]{2,1,0:T(8,128)S(1)}, u32[]{:S(2)}, u32[]{:S(2)}) collective-permute-start(f32[32,32,128]{2,1,0:T(8,128)S(1)} %get-tuple-element.29), channel_id=1, source_target_pairs={{0,31},{8,0},{32,8},{40,32},{64,40},{72,64},{96,72},{104,96},{128,... | collective-permute-start | bytes 1572872 | tf_op jit(solution)/shard_map/ppermute | solution.py:277
  97.1 1.5 %collective-permute-done.5.pr_ref = f32[32,32,128]{2,1,0:T(8,128)S(1)} collective-permute-done((f32[32,32,128]{2,1,0:T(8,128)S(1)}, f32[32,32,128]{2,1,0:T(8,128)S(1)}, u32[]{:S(2)}, u32[]{:S(2)}) %collective-permute-start.5) | collective-permute-done | bytes 524320 | tf_op jit(solution)/shard_map/ppermute | solution.py:277
  98.7 4.6 %collective-permute-done.4.pl_ref = f32[32,32,128]{2,1,0:T(8,128)S(1)} collective-permute-done((f32[32,32,128]{2,1,0:T(8,128)S(1)}, f32[32,32,128]{2,1,0:T(8,128)S(1)}, u32[]{:S(2)}, u32[]{:S(2)}) %collective-permute-start.4) | collective-permute-done | bytes 524320 | tf_op jit(solution)/shard_map/ppermute | solution.py:276
  103.3 2.1 %shard_map.103 = f32[32,2,32,128]{3,2,1,0:T(8,128)S(1)} custom-call(s32[2,2]{1,0:T(2,128)S(1)} %fusion.3.idx_ref, f32[2,256,128]{2,1,0:T(8,128)S(1)} %shard_map.102.k_ref, f32[32,2,32,128]{3,2,1,0:T(8,128)S(1)} %all-to-all-done.f_ref, f32[32,32,128]{2,1,0:T(8,128)S(1)} %collective-permute-done.2.fl_ref, f32[32,32,128]{2,1,0:T(8,128)S(1)} %collective-permute-done.3.fr_ref, ...), custom_call_target="tpu_custom_call" | custom-call | flops 2000000000 | bytes 1048576 | tf_op jit(solution)/shard_map/pallas_call | solution.py:278
  105.4 40.1 %all_to_all.15 = f32[32,2,32,128]{3,2,1,0:T(8,128)} all-to-all(f32[32,2,32,128]{3,2,1,0:T(8,128)S(1)} %shard_map.103), channel_id=1, replica_groups=mesh['mem'=32,'space'=8] {'mem'}, dimensions={0} | all-to-all | bytes 2097152 | tf_op jit(solution)/shard_map/all_to_all | solution.py:281
  145.5 3.6 %shard_map.104 = f32[2048,128]{1,0:T(8,128)} custom-call(f32[64,32,128]{2,1,0:T(8,128)} %bitcast.28), custom_call_target="tpu_custom_call" | custom-call | tf_op jit(solution)/shard_map/pallas_call | solution.py:198
  (19 shorter events, 0.1 us)
Async XLA Ops:
  0.0 0.7 copy-start.4
  0.0 0.7 copy-start.5
  0.0 0.7 copy-start.6
  0.7 1.2 copy-start
  1.9 0.8 copy-start.2
  2.8 0.8 copy-start.3
  10.3 10.5 %copy-start.8 = (s32[64,128]{1,0:T(8,128)S(1)}, s32[64,128]{1,0:T(8,128)}, u32[]{:S(2)}) copy-start(s32[64,128]{1,0:T(8,128)} %param.12) | copy-start | bytes 98308
  10.3 17.4 %copy-start.1 = (f32[32,64,128]{2,1,0:T(8,128)S(1)}, f32[32,64,128]{2,1,0:T(8,128)}, u32[]{:S(2)}) copy-start(f32[32,64,128]{2,1,0:T(8,128)} %param.11) | copy-start | bytes 3145732
  10.3 38.8 %all-to-all-start = ((f32[32,2,32,128]{3,2,1,0:T(8,128)}), f32[32,2,32,128]{3,2,1,0:T(8,128)S(1)}, u32[]{:S(2)}, u32[]{:S(2)}) async-start(f32[32,2,32,128]{3,2,1,0:T(8,128)} %bitcast.6), calls=%async_computation | async-start | bytes 2097152 | tf_op jit(solution)/shard_map/all_to_all | solution.py:243
  20.9 0.8 copy-start.7
  21.6 6.0 %collective-permute-start = (f32[1,256]{1,0:T(1,128)S(1)}, f32[1,256]{1,0:T(1,128)S(1)}, u32[]{:S(2)}, u32[]{:S(2)}) collective-permute-start(f32[1,256]{1,0:T(1,128)S(1)} %get-tuple-element.33), channel_id=1, source_target_pairs={{0,1},{1,2},{2,3},{3,4},{4,5},{5,6},{6,7},{7,0},{8,9},{9,10},{10,1... | collective-permute-start | bytes 3080 | tf_op jit(solution)/shard_map/ppermute | solution.py:246
  22.9 4.7 %collective-permute-start.1 = (f32[1,256]{1,0:T(1,128)S(1)}, f32[1,256]{1,0:T(1,128)S(1)}, u32[]{:S(2)}, u32[]{:S(2)}) collective-permute-start(f32[1,256]{1,0:T(1,128)S(1)} %get-tuple-element.34), channel_id=1, source_target_pairs={{1,0},{2,1},{3,2},{4,3},{5,4},{6,5},{7,6},{0,7},{9,8},{10,9},{11,1... | collective-permute-start | bytes 3080 | tf_op jit(solution)/shard_map/ppermute | solution.py:247
  26.7 0.7 copy-start.9
  49.1 33.6 %all-to-all-start.1 = ((f32[32,2,32,128]{3,2,1,0:T(8,128)}), f32[32,2,32,128]{3,2,1,0:T(8,128)S(1)}, u32[]{:S(2)}, u32[]{:S(2)}) async-start(f32[32,2,32,128]{3,2,1,0:T(8,128)} %bitcast.7), calls=%async_computation.1 | async-start | bytes 2097152 | tf_op jit(solution)/shard_map/all_to_all | solution.py:265
  53.9 14.6 %collective-permute-start.3 = (f32[32,32,128]{2,1,0:T(8,128)S(1)}, f32[32,32,128]{2,1,0:T(8,128)S(1)}, u32[]{:S(2)}, u32[]{:S(2)}) collective-permute-start(f32[32,32,128]{2,1,0:T(8,128)S(1)} %get-tuple-element.31), channel_id=1, source_target_pairs={{0,31},{8,0},{32,8},{40,32},{64,40},{72,64},{96,72},{104,96},{128,... | collective-permute-start | bytes 1572872 | tf_op jit(solution)/shard_map/ppermute | solution.py:263
  54.3 14.2 %collective-permute-start.2 = (f32[32,32,128]{2,1,0:T(8,128)S(1)}, f32[32,32,128]{2,1,0:T(8,128)S(1)}, u32[]{:S(2)}, u32[]{:S(2)}) collective-permute-start(f32[32,32,128]{2,1,0:T(8,128)S(1)} %get-tuple-element.32), channel_id=1, source_target_pairs={{0,8},{8,32},{32,40},{40,64},{64,72},{72,96},{96,104},{104,128},{1... | collective-permute-start | bytes 1572872 | tf_op jit(solution)/shard_map/ppermute | solution.py:262
  82.8 15.9 %collective-permute-start.5 = (f32[32,32,128]{2,1,0:T(8,128)S(1)}, f32[32,32,128]{2,1,0:T(8,128)S(1)}, u32[]{:S(2)}, u32[]{:S(2)}) collective-permute-start(f32[32,32,128]{2,1,0:T(8,128)S(1)} %get-tuple-element.29), channel_id=1, source_target_pairs={{0,31},{8,0},{32,8},{40,32},{64,40},{72,64},{96,72},{104,96},{128,... | collective-permute-start | bytes 1572872 | tf_op jit(solution)/shard_map/ppermute | solution.py:277
  97.1 6.1 %collective-permute-start.4 = (f32[32,32,128]{2,1,0:T(8,128)S(1)}, f32[32,32,128]{2,1,0:T(8,128)S(1)}, u32[]{:S(2)}, u32[]{:S(2)}) collective-permute-start(f32[32,32,128]{2,1,0:T(8,128)S(1)} %get-tuple-element.30), channel_id=1, source_target_pairs={{0,8},{8,32},{32,40},{40,64},{64,72},{72,96},{96,104},{104,128},{1... | collective-permute-start | bytes 1572872 | tf_op jit(solution)/shard_map/ppermute | solution.py:276

commit v3 on v0

--- a/solution.py
+++ b/solution.py
@@ -42,6 +42,10 @@
     return jnp.dot(a, b, preferred_element_type=F32)
 
 
+def dot_t(a, b):
+    return lax.dot_general(a, b, (((1,), (1,)), ((), ())), preferred_element_type=F32)
+
+
 def tdot(a, b):
     return lax.dot_general(a, b, (((0,), (0,)), ((), ())), preferred_element_type=F32)
 
@@ -69,23 +73,19 @@
 
 
 def forecast_kernel(x_ref, g_ref, wi_ref, bi_ref, wo_ref, bo_ref, o_ref, wi2, wo2):
-    wi = (wi_ref[...].astype(F32) * 0.5).astype(BF16)
-    zi = jnp.zeros_like(wi)
-    wi2[:LEV, :HID] = wi
-    wi2[:LEV, HID:] = zi
-    wi2[LEV:, :HID] = zi
-    wi2[LEV:, HID:] = wi
-    wo = wo_ref[...]
-    zo = jnp.zeros_like(wo)
-    wo2[:HID, :] = jnp.concatenate([wo, zo], axis=1)
-    wo2[HID:, :] = jnp.concatenate([zo, wo], axis=1)
+    for both, one in ((wi2, (wi_ref[...].astype(F32) * 0.5).astype(BF16)), (wo2, wo_ref[...])):
+        zero = jnp.zeros_like(one)
+        both[:LEV, :HID] = one
+        both[:LEV, HID:] = zero
+        both[LEV:, :HID] = zero
+        both[LEV:, HID:] = one
     gain = jnp.concatenate([g_ref[...]] * 2, axis=1)
     bi = jnp.concatenate([bi_ref[...]] * 2, axis=1) * 0.5
     bo = jnp.concatenate([bo_ref[...]] * 2, axis=1)
     row = lax.broadcasted_iota(jnp.int32, (2 * PV, PV), 0)
     col = lax.broadcasted_iota(jnp.int32, (2 * PV, PV), 1)
     halves = jnp.where((row % PV) // LEV == col // LEV, 1.0, 0.0).astype(BF16)
-    chunk = 8
+    chunk = PAIRS
     for first in range(0, 2 * PAIRS, chunk):
         x = jnp.concatenate(
             [x_ref[pl.ds(first + i, NMEM, stride=2 * PAIRS), :] for i in range(chunk)], axis=0
@@ -96,47 +96,34 @@
             normed = (x * inverse * gain).astype(BF16)
             h = dot(normed, wi2[...]) + bi
             hidden = (h + h * jnp.tanh(h)).astype(BF16)
-            x = x + dot(hidden, wo2[...]) + bo
+            x = x + dot_t(hidden, wo2[...]) + bo
         for i in range(chunk):
             patch = first + i
             o_ref[2 * owner_of(patch // 2) + patch % 2] = x[i * NMEM : (i + 1) * NMEM]
 
 
-def update_kernel(
-    idx_ref, f_ref, fl_ref, fr_ref, p_ref, pl_ref, pr_ref, slot_ref, var_ref, o_ref,
-    ah, al, bh, bl, dh, dl, s_ref, x_ref,
-):
-    members = NMEM * NMEM
-    fields = (fl_ref, f_ref.at[:, 0], f_ref.at[:, 1], fr_ref)
-    readings = (pl_ref, p_ref.at[:, 0], p_ref.at[:, 1], pr_ref)
-    root = lax.rsqrt(var_ref[...])
-    for w in range(4):
-        x = fields[w][...].reshape(members, PV)
-        if w in (1, 2):
-            a = x - jnp.mean(x, axis=0, keepdims=True)
-            ah[w - 1], al[w - 1] = split(a)
-        slots = jnp.broadcast_to(slot_ref[w : w + 1, :], (members, PV))
-        y = jnp.take_along_axis(x, slots, axis=1, mode="promise_in_bounds")
-        r = root[w : w + 1, :]
-        b = (y - jnp.mean(y, axis=0, keepdims=True)) * r
-        bh[w], bl[w] = split(b)
-        d = (readings[w][...].reshape(members, PV) - y) * r
-        dh[w], dl[w] = split(d)
-    eye = jnp.where(
-        lax.broadcasted_iota(jnp.int32, (2 * PV, 2 * PV), 0)
-        == lax.broadcasted_iota(jnp.int32, (2 * PV, 2 * PV), 1),
-        1.0,
-        0.0,
-    )
-    scale = 1.0 / (members - 1)
-    cross, deltas = [], []
-    for j in range(2):
-        one, two = idx_ref[j, 0], idx_ref[j, 1]
-        rh = jnp.concatenate([bh[one], bh[two]], axis=1)
-        rl = jnp.concatenate([bl[one], bl[two]], axis=1)
-        mixed = tdot(rh, rl)
-        s = (tdot(rh, rh) + (mixed + mixed.T)) * scale + eye
-        cross.append((tdot(rh, ah[j]) + (tdot(rh, al[j]) + tdot(rl, ah[j]))) * scale)
+def exact(a, b):
+    return jnp.dot(a, b, precision=lax.Precision.HIGHEST, preferred_element_type=F32)
+
+
+def observe(x, slots):
+    slots = jnp.broadcast_to(slots, x.shape)
+    return jnp.take_along_axis(x, slots, axis=1, mode="promise_in_bounds")
+
+
+def centred(x):
+    return x - jnp.mean(x, axis=0, keepdims=True)
+
+
+def identity():
+    row = lax.broadcasted_iota(jnp.int32, (PV, PV), 0)
+    return jnp.where(row == lax.broadcasted_iota(jnp.int32, (PV, PV), 1), 1.0, 0.0)
+
+
+def inverses(matrices, s_ref, x_ref):
+    deltas = []
+    eye = identity()
+    for j, s in enumerate(matrices):
         s2 = dot3(s, s)
         top = jnp.max(jnp.sqrt(jnp.sum(jnp.abs(s2), axis=0, keepdims=True)))
         c = 2.0 / (top + 1.0)
@@ -164,31 +151,93 @@
         return tuple(after)
 
     lax.while_loop(more, sharpen, tuple(deltas))
+
+
+def own_kernel(
+    idx_ref, f_ref, p_ref, slot_ref, var_ref,
+    ah, al, bh, bl, dh, dl, inv_ref, part_ref, s_ref, x_ref,
+):
+    members = NMEM * NMEM
+    root = lax.rsqrt(var_ref[...])
+    for w in range(2):
+        x = f_ref[:, w].reshape(members, PV)
+        y = observe(x, slot_ref[w + 1 : w + 2, :])
+        r = root[w + 1 : w + 2, :]
+        ah[w], al[w] = split(centred(x))
+        bh[w], bl[w] = split(centred(y) * r)
+        dh[w], dl[w] = split((p_ref[:, w].reshape(members, PV) - y) * r)
+    scale = 1.0 / (members - 1)
+    matrices, crosses = [], []
     for j in range(2):
-        s, x, g = s_ref[j], x_ref[j], cross[j]
-        k = dot3(x, g)
+        o = idx_ref[j, 0] - 1
+        high, low = bh[o], bl[o]
+        mixed = tdot(high, low)
+        matrices.append((tdot(high, high) + (mixed + mixed.T)) * scale + identity())
+        crosses.append((tdot(high, ah[j]) + (tdot(high, al[j]) + tdot(low, ah[j]))) * scale)
+    inverses(matrices, s_ref, x_ref)
+    for j in range(2):
+        s, x = s_ref[j], x_ref[j]
+        x = 2.0 * x - dot3(x, dot3(s, x))
+        x = 2.0 * x - exact(x, exact(s, x))
+        inv_ref[j] = x
+        part_ref[j] = exact(x, crosses[j])
+
+
+def update_kernel(
+    idx_ref, f_ref, fl_ref, fr_ref, p_ref, pl_ref, pr_ref, slot_ref, var_ref,
+    ah, al, bh, bl, dh, dl, inv_ref, part_ref, o_ref, hh, hl, s_ref, x_ref,
+):
+    members = NMEM * NMEM
+    scale = 1.0 / (members - 1)
+    fields, readings = (fl_ref, fr_ref), (pl_ref, pr_ref)
+    complements, links, crosses = [], [], []
+    for j in range(2):
+        o, h = idx_ref[j, 0] - 1, idx_ref[j, 1]
+        apart = h == 3 * j
+        x = jnp.where(apart, fields[j][...], f_ref[:, j]).reshape(members, PV)
+        p = jnp.where(apart, readings[j][...], p_ref[:, j]).reshape(members, PV)
+        y = observe(x, slot_ref[pl.ds(h, 1), :])
+        r = lax.rsqrt(var_ref[pl.ds(h, 1), :])
+        high, low = split(centred(y) * r)
+        hh[j], hl[j] = split((p - y) * r)
+        right = jnp.concatenate([bh[o], high, ah[j]], axis=1)
+        under = jnp.concatenate([bl[o], low, al[j]], axis=1)
+        gram = (tdot(high, right) + (tdot(high, under) + tdot(low, right))) * scale
+        s_ho, s_hh, g_h = gram[:, :PV], gram[:, PV : 2 * PV] + identity(), gram[:, 2 * PV :]
+        link = dot3(s_ho, inv_ref[j])
+        complements.append(s_hh - dot3(link, s_ho.T))
+        links.append(link)
+        crosses.append(g_h - dot3(s_ho, part_ref[j]))
+    inverses(complements, s_ref, x_ref)
+    for j in range(2):
+        s, x, g = s_ref[j], x_ref[j], crosses[j]
+        k_h = dot3(x, g)
         for _ in range(2):
-            k = k + dot3(
-                x, g - jnp.dot(s, k, precision=lax.Precision.HIGHEST, preferred_element_type=F32)
-            )
-        kh, kl = split(k)
-        one, two = idx_ref[j, 0], idx_ref[j, 1]
-        ih = jnp.concatenate([dh[one], dh[two]], axis=1)
-        il = jnp.concatenate([dl[one], dl[two]], axis=1)
+            k_h = k_h + dot3(x, g - exact(s, k_h))
+        k_o = part_ref[j] - dot3(links[j].T, k_h)
+        kh, kl = split(jnp.concatenate([k_o, k_h], axis=0))
+        o = idx_ref[j, 0] - 1
+        ih = jnp.concatenate([dh[o], hh[j]], axis=1)
+        il = jnp.concatenate([dl[o], hl[j]], axis=1)
         gained = dot(ih, kh) + (dot(ih, kl) + dot(il, kh))
-        o_ref[:, j] = fields[1 + j][...] + gained.reshape(NMEM, NMEM, PV)
-
-
-def vmem_call(kernel, out, scratch=(), smem=0, limit=48, n_in=1):
+        o_ref[:, j] = f_ref[:, j] + gained.reshape(NMEM, NMEM, PV)
+
+
+def vmem_call(kernel, out, scratch=(), smem=0, limit=24, n_in=1, us=2):
     specs = [pl.BlockSpec(memory_space=pltpu.SMEM)] * smem
     specs += [pl.BlockSpec(memory_space=pltpu.VMEM)] * (n_in - smem)
+    single = isinstance(out, tuple)
+    shapes = jax.ShapeDtypeStruct(out, F32) if single else out
     return pl.pallas_call(
         kernel,
-        out_shape=jax.ShapeDtypeStruct(out, F32),
+        out_shape=shapes,
         in_specs=specs,
-        out_specs=pl.BlockSpec(memory_space=pltpu.VMEM),
+        out_specs=jax.tree.map(lambda _: pl.BlockSpec(memory_space=pltpu.VMEM), shapes),
         scratch_shapes=list(scratch),
         compiler_params=pltpu.CompilerParams(vmem_limit_bytes=limit << 20),
+        cost_estimate=pl.CostEstimate(
+            flops=us * 10**9, bytes_accessed=1 << 20, transcendentals=0
+        ),
     )
 
 
@@ -207,10 +256,10 @@
 
     field_send = vmem_call(
         forecast_kernel, sent,
-        [pltpu.VMEM((2 * LEV, 2 * HID), BF16), pltpu.VMEM((2 * HID, 2 * LEV), BF16)], n_in=6,
+        [pltpu.VMEM((2 * LEV, 2 * HID), BF16)] * 2, n_in=6, us=7,
     )(
         prior_sample_set.reshape(rows, PV), norm_gain.reshape(1, -1), w_in, b_in.reshape(1, -1),
-        w_out, b_out.reshape(1, -1),
+        w_out.T, b_out.reshape(1, -1),
     )
     meta = jnp.concatenate([measured_slot_table.astype(F32), obs_var], axis=-1)
     field_send, meta = lax.optimization_barrier((field_send, meta))
@@ -235,12 +284,18 @@
     field_right = lax.ppermute(field[:, 0], both, leftward)
 
     members = NMEM * NMEM
+    pair = jax.ShapeDtypeStruct((2, members, PV), BF16)
+    small = jax.ShapeDtypeStruct((2, PV, PV), F32)
     half = pltpu.VMEM((2, members, PV), BF16)
-    full = pltpu.VMEM((4, members, PV), BF16)
-    square = pltpu.VMEM((2, 2 * PV, 2 * PV), F32)
-    analysis = vmem_call(
-        update_kernel, packed, [half, half, full, full, full, full, square, square], smem=1, n_in=9
-    )(index, field, field_left, field_right, pert, pert_left, pert_right, slots, variances)
+    square = pltpu.VMEM((2, PV, PV), F32)
+    index = jnp.concatenate([index[:1, ::-1], index[1:]], axis=0)
+    own_parts = vmem_call(
+        own_kernel, [pair] * 6 + [small] * 2, [square, square], smem=1, n_in=5, us=9
+    )(index, field, pert, slots, variances)
+    analysis = vmem_call(update_kernel, packed, [half, half, square, square], smem=1, n_in=17, us=7)(
+        index, field, field_left, field_right, pert, pert_left, pert_right, slots, variances,
+        *own_parts,
+    )
     returned = lax.all_to_all(analysis, "mem", 0, 0, tiled=True)
     out = vmem_call(from_sent_kernel, (rows, PV))(returned.reshape(sent))
     return out.reshape(prior_sample_set.shape)

time: 142 us -> 135 us (0.951)
  waiting for transfers between devices: 44.7 us -> 40.6 us
  Pallas kernels: 26.2 us -> 23.8 us
    ppermute x1, waiting for transfers between devices: 7.03 us -> 1.13 us  [body(): field_right = lax.ppermute(field[:, 0], both, leftward)]
    pallas_call x2 -> x3, Pallas kernels: 22.6 us -> 20.2 us  [the longest x1 7.76 us: body(): vmem_call(update_kernel, packed, [half, half, square, square], smem=1, n_...]
    all_to_all x1, waiting for transfers between devices: 17.7 us -> 19.8 us  [body(): pert = lax.all_to_all(pert_send.reshape(packed), 'mem', 0, 0, tiled=True)]
    unnamed x22 -> x21, local copies, waits for them, and re-layouts: 2.98 us -> 2.92 us
  transfers between devices with their start and end apart: 8 -> 8, of which waited for: 3 -> 4; matrix products, arithmetic and copies ran while one was open for 2% -> 1% of each run, Pallas kernels for 6% -> 9%
where the time goes in v3:
time: 135 us; the launch traced here: 134 us
  waiting for transfers between devices  40.6 us (30%)
  blocking collectives  39.5 us (29%)
  starting transfers between devices  25.7 us (19%)
  Pallas kernels  23.8 us (18%)
  local copies, waits for them, and re-layouts  4.26 us (3%)
    all_to_all x1, blocking collectives, body(): returned = lax.all_to_all(analysis, 'mem', 0, 0, tiled=True)  39.5 us
    all_to_all x1, waiting for transfers between devices, body(): pert = lax.all_to_all(pert_send.reshape(packed), 'mem', 0, 0, tiled=True)  19.8 us
    all_to_all x1, waiting for transfers between devices, body(): field = lax.all_to_all(field_send.reshape(packed), 'mem', 0, 0, tiled=True)  18.9 us
    all_to_all x1, starting transfers between devices, body(): pert = lax.all_to_all(pert_send.reshape(packed), 'mem', 0, 0, tiled=True)  10.5 us
    pallas_call x1, Pallas kernels, body(): vmem_call(update_kernel, packed, [half, half, square, square], smem=1, n_...  7.76 us
    pallas_call x1, Pallas kernels, body(): vmem_call(forecast_kernel, sent, [pltpu.VMEM((2 * LEV, 2 * HID), BF16)] *...  6.79 us
    pallas_call x1, Pallas kernels, body(): vmem_call(own_kernel, [pair] * 6 + [small] * 2, [square, square], smem=1,...  5.7 us
    all_to_all x1, starting transfers between devices, body(): field = lax.all_to_all(field_send.reshape(packed), 'mem', 0, 0, tiled=True)  4.68 us
  transfers between devices with their start and end apart: 8, of which 4 were waited for; matrix products, arithmetic and copies ran while one was open for 1% of the time, Pallas kernels for 9%

profile of v3, /device:TPU:3, one launch (start us, length us, event | category | flops | bytes accessed | tf_op | source)
XLA Modules:
  0.0 134.2 jit_solution(10028944721456374070)
XLA Ops:
  0.0 1.2 copy-done.1
  1.2 1.6 %shard_map.101 = f32[64,32,128]{2,1,0:T(8,128)} custom-call(f32[2048,128]{1,0:T(8,128)S(1)} %bitcast.27), custom_call_target="tpu_custom_call" | custom-call | flops 2000000000 | bytes 1048576 | tf_op jit(solution)/shard_map/pallas_call | solution.py:254
  2.9 10.5 %all-to-all-start.1 = ((f32[32,2,32,128]{3,2,1,0:T(8,128)}), f32[32,2,32,128]{3,2,1,0:T(8,128)S(1)}, u32[]{:S(2)}, u32[]{:S(2)}) async-start(f32[32,2,32,128]{3,2,1,0:T(8,128)} %bitcast.9), calls=%async_computation.1 | async-start | bytes 2097152 | tf_op jit(solution)/shard_map/all_to_all | solution.py:255
  13.4 0.0 copy-start.9
  13.4 0.7 copy-done.9
  14.2 0.0 copy-start.5
  14.2 0.0 copy-start.6
  14.2 0.0 copy-start.7
  14.2 0.8 copy-done.3
  15.0 0.0 copy-done.4
  15.0 6.8 %shard_map.100 = f32[64,32,128]{2,1,0:T(8,128)} custom-call(f32[2048,128]{1,0:T(8,128)S(1)} %bitcast.28, f32[1,64]{1,0:T(1,128)S(1)} %bitcast.31, bf16[64,512]{1,0:T(8,128)(2,1)S(1)} %copy-done.3, f32[1,512]{1,0:T(1,128)S(1)} %bitcast.30, bf16[64,512]{1,0:T(8,128)(2,1)S(1)} %bitcast.29, f32[1,64]{1,0:T(1,128)S(1)} %bitcast.32), custom_call_target="tpu_custom_call" | custom-call | flops 7000000000 | bytes 1048576 | tf_op jit(solution)/shard_map/pallas_call | solution.py:257
  21.8 19.8 %all-to-all-done.1.p_ref = f32[32,2,32,128]{3,2,1,0:T(8,128)S(1)} async-done(((f32[32,2,32,128]{3,2,1,0:T(8,128)}), f32[32,2,32,128]{3,2,1,0:T(8,128)S(1)}, u32[]{:S(2)}, u32[]{:S(2)}) %all-to-all-start.1) | async-done | bytes 1048608 | tf_op jit(solution)/shard_map/all_to_all | solution.py:255
  41.6 4.7 %all-to-all-start = ((f32[32,2,32,128]{3,2,1,0:T(8,128)}), f32[32,2,32,128]{3,2,1,0:T(8,128)S(1)}, u32[]{:S(2)}, u32[]{:S(2)}) async-start(f32[32,2,32,128]{3,2,1,0:T(8,128)} %bitcast.5), calls=%async_computation | async-start | bytes 2097152 | tf_op jit(solution)/shard_map/all_to_all | solution.py:266
  46.3 1.4 %collective-permute-start.4 = (f32[1,256]{1,0:T(1,128)S(1)}, f32[1,256]{1,0:T(1,128)S(1)}, u32[]{:S(2)}, u32[]{:S(2)}) collective-permute-start(f32[1,256]{1,0:T(1,128)S(1)} %get-tuple-element.29), channel_id=1, source_target_pairs={{0,1},{1,2},{2,3},{3,4},{4,5},{5,6},{6,7},{7,0},{8,9},{9,10},{10,1... | collective-permute-start | bytes 3080 | tf_op jit(solution)/shard_map/ppermute | solution.py:269
  47.7 3.8 %collective-permute-start.5 = (f32[1,256]{1,0:T(1,128)S(1)}, f32[1,256]{1,0:T(1,128)S(1)}, u32[]{:S(2)}, u32[]{:S(2)}) collective-permute-start(f32[1,256]{1,0:T(1,128)S(1)} %get-tuple-element.30), channel_id=1, source_target_pairs={{1,0},{2,1},{3,2},{4,3},{5,4},{6,5},{7,6},{0,7},{9,8},{10,9},{11,1... | collective-permute-start | bytes 3080 | tf_op jit(solution)/shard_map/ppermute | solution.py:270
  51.5 0.1 constant_dynamic-slice_fusion
  51.6 0.1 copy.28
  51.7 0.1 fusion.2
  51.8 0.1 rev.3
  51.9 0.7 collective-permute-done.4
  52.7 1.1 slice_bitcast_fusion
  53.7 1.4 %collective-permute-start.3 = (f32[32,32,128]{2,1,0:T(8,128)}, f32[32,32,128]{2,1,0:T(8,128)S(1)}, u32[]{:S(2)}, u32[]{:S(2)}) collective-permute-start(f32[32,32,128]{2,1,0:T(8,128)} %get-tuple-element.25), channel_id=1, source_target_pairs={{0,31},{8,0},{32,8},{40,32},{64,40},{72,64},{96,72},{104,96},{128,... | collective-permute-start | bytes 1572872 | tf_op jit(solution)/shard_map/ppermute | solution.py:282
  55.1 1.3 collective-permute-start.2
  56.4 18.9 %all-to-all-done.f_ref = f32[32,2,32,128]{3,2,1,0:T(8,128)S(1)} async-done(((f32[32,2,32,128]{3,2,1,0:T(8,128)}), f32[32,2,32,128]{3,2,1,0:T(8,128)S(1)}, u32[]{:S(2)}, u32[]{:S(2)}) %all-to-all-start) | async-done | bytes 1048608 | tf_op jit(solution)/shard_map/all_to_all | solution.py:266
  75.3 0.1 slice_bitcast_fusion.2
  75.4 0.7 collective-permute-start.1
  76.0 2.0 %collective-permute-start = (f32[32,32,128]{2,1,0:T(8,128)S(1)}, f32[32,32,128]{2,1,0:T(8,128)S(1)}, u32[]{:S(2)}, u32[]{:S(2)}) collective-permute-start(f32[32,32,128]{2,1,0:T(8,128)S(1)} %get-tuple-element.28), channel_id=1, source_target_pairs={{0,8},{8,32},{32,40},{40,64},{64,72},{72,96},{96,104},{104,128},{1... | collective-permute-start | bytes 1572872 | tf_op jit(solution)/shard_map/ppermute | solution.py:283
  78.1 5.7 %shard_map.102 = (bf16[2,1024,128]{2,1,0:T(8,128)(2,1)S(1)}, bf16[2,1024,128]{2,1,0:T(8,128)(2,1)S(1)}, bf16[2,1024,128]{2,1,0:T(8,128)(2,1)S(1)}, bf16[2,1024,1...) custom-call(s32[2,2]{1,0:T(2,128)S(1)} %pad_add_fusion.idx_ref, ...), custom_call_target="tpu_custom_call" | custom-call | flops 8999999488 | bytes 1048576 | tf_op jit(solution)/shard_map/pallas_call | solution.py:292
  83.8 1.1 collective-permute-done.1.fr_ref
  84.9 7.8 %shard_map.103 = f32[32,2,32,128]{3,2,1,0:T(8,128)S(1)} custom-call(s32[2,2]{1,0:T(2,128)S(1)} %pad_add_fusion.idx_ref, f32[32,2,32,128]{3,2,1,0:T(8,128)S(1)} %all-to-all-done.f_ref, f32[32,32,128]{2,1,0:T(8,128)S(1)} %collective-permute-done.fl_ref, f32[32,32,128]{2,1,0:T(8,128)S(1)} %collective-permute-done.1.fr_ref, ...), custom_call_target="tpu_custom_call" | custom-call | flops 7000000000 | bytes 1048576 | tf_op jit(solution)/shard_map/pallas_call | solution.py:295
  92.7 39.5 %all_to_all.15 = f32[32,2,32,128]{3,2,1,0:T(8,128)S(1)} all-to-all(f32[32,2,32,128]{3,2,1,0:T(8,128)S(1)} %shard_map.103), channel_id=1, replica_groups=mesh['mem'=32,'space'=8] {'mem'}, dimensions={0} | all-to-all | bytes 2097152 | tf_op jit(solution)/shard_map/all_to_all | solution.py:299
  132.2 1.9 %shard_map.104 = f32[2048,128]{1,0:T(8,128)} custom-call(f32[64,32,128]{2,1,0:T(8,128)S(1)} %bitcast.26), custom_call_target="tpu_custom_call" | custom-call | flops 2000000000 | bytes 1048576 | tf_op jit(solution)/shard_map/pallas_call | solution.py:300
  (24 shorter events, 0.1 us)
Async XLA Ops:
  0.0 51.5 %copy-start = (s32[64,2]{0,1:T(2,128)S(1)}, s32[64,2]{0,1:T(2,128)}, u32[]{:S(2)}) copy-start(s32[64,2]{0,1:T(2,128)} %param.14) | copy-start | bytes 1540
  0.0 1.2 copy-start.1
  2.9 10.5 %copy-start.8 = (s32[64,128]{1,0:T(8,128)S(1)}, s32[64,128]{1,0:T(8,128)}, u32[]{:S(2)}) copy-start(s32[64,128]{1,0:T(8,128)} %param.12) | copy-start | bytes 98308
  2.9 11.4 %copy-start.2 = (f32[32,64,128]{2,1,0:T(8,128)S(1)}, f32[32,64,128]{2,1,0:T(8,128)}, u32[]{:S(2)}) copy-start(f32[32,64,128]{2,1,0:T(8,128)} %param.10) | copy-start | bytes 3145732
  2.9 38.8 %all-to-all-start.1 = ((f32[32,2,32,128]{3,2,1,0:T(8,128)}), f32[32,2,32,128]{3,2,1,0:T(8,128)S(1)}, u32[]{:S(2)}, u32[]{:S(2)}) async-start(f32[32,2,32,128]{3,2,1,0:T(8,128)} %bitcast.9), calls=%async_computation.1 | async-start | bytes 2097152 | tf_op jit(solution)/shard_map/all_to_all | solution.py:255
  13.4 0.8 copy-start.9
  14.2 0.8 copy-start.3
  14.2 0.9 copy-start.4
  14.2 0.9 copy-start.5
  14.2 0.9 copy-start.6
  14.2 0.8 copy-start.7
  41.6 33.6 %all-to-all-start = ((f32[32,2,32,128]{3,2,1,0:T(8,128)}), f32[32,2,32,128]{3,2,1,0:T(8,128)S(1)}, u32[]{:S(2)}, u32[]{:S(2)}) async-start(f32[32,2,32,128]{3,2,1,0:T(8,128)} %bitcast.5), calls=%async_computation | async-start | bytes 2097152 | tf_op jit(solution)/shard_map/all_to_all | solution.py:266
  46.3 6.3 %collective-permute-start.4 = (f32[1,256]{1,0:T(1,128)S(1)}, f32[1,256]{1,0:T(1,128)S(1)}, u32[]{:S(2)}, u32[]{:S(2)}) collective-permute-start(f32[1,256]{1,0:T(1,128)S(1)} %get-tuple-element.29), channel_id=1, source_target_pairs={{0,1},{1,2},{2,3},{3,4},{4,5},{5,6},{6,7},{7,0},{8,9},{9,10},{10,1... | collective-permute-start | bytes 3080 | tf_op jit(solution)/shard_map/ppermute | solution.py:269
  47.7 4.9 %collective-permute-start.5 = (f32[1,256]{1,0:T(1,128)S(1)}, f32[1,256]{1,0:T(1,128)S(1)}, u32[]{:S(2)}, u32[]{:S(2)}) collective-permute-start(f32[1,256]{1,0:T(1,128)S(1)} %get-tuple-element.30), channel_id=1, source_target_pairs={{1,0},{2,1},{3,2},{4,3},{5,4},{6,5},{7,6},{0,7},{9,8},{10,9},{11,1... | collective-permute-start | bytes 3080 | tf_op jit(solution)/shard_map/ppermute | solution.py:270
  53.7 30.1 %collective-permute-start.3 = (f32[32,32,128]{2,1,0:T(8,128)}, f32[32,32,128]{2,1,0:T(8,128)S(1)}, u32[]{:S(2)}, u32[]{:S(2)}) collective-permute-start(f32[32,32,128]{2,1,0:T(8,128)} %get-tuple-element.25), channel_id=1, source_target_pairs={{0,31},{8,0},{32,8},{40,32},{64,40},{72,64},{96,72},{104,96},{128,... | collective-permute-start | bytes 1572872 | tf_op jit(solution)/shard_map/ppermute | solution.py:282
  55.1 28.7 %collective-permute-start.2 = (f32[32,32,128]{2,1,0:T(8,128)}, f32[32,32,128]{2,1,0:T(8,128)S(1)}, u32[]{:S(2)}, u32[]{:S(2)}) collective-permute-start(f32[32,32,128]{2,1,0:T(8,128)} %get-tuple-element.26), channel_id=1, source_target_pairs={{0,8},{8,32},{32,40},{40,64},{64,72},{72,96},{96,104},{104,128},{1... | collective-permute-start | bytes 1572872 | tf_op jit(solution)/shard_map/ppermute | solution.py:281
  75.4 9.6 %collective-permute-start.1 = (f32[32,32,128]{2,1,0:T(8,128)S(1)}, f32[32,32,128]{2,1,0:T(8,128)S(1)}, u32[]{:S(2)}, u32[]{:S(2)}) collective-permute-start(f32[32,32,128]{2,1,0:T(8,128)S(1)} %get-tuple-element.27), channel_id=1, source_target_pairs={{0,31},{8,0},{32,8},{40,32},{64,40},{72,64},{96,72},{104,96},{128,... | collective-permute-start | bytes 1572872 | tf_op jit(solution)/shard_map/ppermute | solution.py:284
  76.0 8.9 %collective-permute-start = (f32[32,32,128]{2,1,0:T(8,128)S(1)}, f32[32,32,128]{2,1,0:T(8,128)S(1)}, u32[]{:S(2)}, u32[]{:S(2)}) collective-permute-start(f32[32,32,128]{2,1,0:T(8,128)S(1)} %get-tuple-element.28), channel_id=1, source_target_pairs={{0,8},{8,32},{32,40},{40,64},{64,72},{72,96},{96,104},{104,128},{1... | collective-permute-start | bytes 1572872 | tf_op jit(solution)/shard_map/ppermute | solution.py:283

commit v4 on v3

--- a/solution.py
+++ b/solution.py
@@ -10,6 +10,7 @@
 HOPS = 2
 PV = 128
 NMEM = 32
+PIECES = 4
 PAIRS = 32
 F32 = jnp.float32
 BF16 = jnp.bfloat16
@@ -60,16 +61,44 @@
     return dot(ah, bh) + (dot(ah, bl) + dot(al, bh))
 
 
-def to_send_kernel(x_ref, o_ref):
-    for patch in range(2 * PAIRS):
-        row = 2 * owner_of(patch // 2) + patch % 2
-        o_ref[row] = x_ref[pl.ds(patch, NMEM, stride=2 * PAIRS), :]
-
-
-def from_sent_kernel(x_ref, o_ref):
-    for patch in range(2 * PAIRS):
-        row = 2 * owner_of(patch // 2) + patch % 2
-        o_ref[pl.ds(patch, NMEM, stride=2 * PAIRS), :] = x_ref[row]
+def sent_row(patch):
+    return 2 * owner_of(patch // 2) + patch % 2
+
+
+def to_send_kernel(x_ref, o_ref, came, put, in_sems, out_sems):
+    group = 2 * PAIRS // PIECES
+    for g in range(PIECES):
+        part = pl.ds(g * group, group)
+        pltpu.make_async_copy(x_ref.at[:, part], came.at[:, part], in_sems.at[g]).start()
+    rows = came.reshape(2 * PAIRS * NMEM, PV)
+    copies = []
+    for g in range(PIECES):
+        part = pl.ds(g * group, group)
+        pltpu.make_async_copy(x_ref.at[:, part], came.at[:, part], in_sems.at[g]).wait()
+        for chip in range(g * group // 4, (g + 1) * group // 4):
+            for patch in range(4 * chip, 4 * chip + 4):
+                put[sent_row(patch)] = rows[pl.ds(patch, NMEM, stride=2 * PAIRS), :]
+            part = pl.ds(sent_row(4 * chip), 4)
+            copies.append(pltpu.make_async_copy(put.at[part], o_ref.at[part], out_sems.at[chip]))
+            copies[-1].start()
+    for copy in copies:
+        copy.wait()
+
+
+def from_sent_kernel(x_ref, o_ref, put, sems):
+    step = NMEM // PIECES
+    copies = []
+    for g in range(PIECES):
+        first = g * step * 2 * PAIRS
+        for patch in range(2 * PAIRS):
+            put[pl.ds(first + patch, step, stride=2 * PAIRS), :] = x_ref[
+                sent_row(patch), g * step : (g + 1) * step
+            ]
+        part = pl.ds(first, step * 2 * PAIRS)
+        copies.append(pltpu.make_async_copy(put.at[part], o_ref.at[part], sems.at[g]))
+        copies[-1].start()
+    for copy in copies:
+        copy.wait()
 
 
 def forecast_kernel(x_ref, g_ref, wi_ref, bi_ref, wo_ref, bo_ref, o_ref, wi2, wo2):
@@ -99,7 +128,7 @@
             x = x + dot_t(hidden, wo2[...]) + bo
         for i in range(chunk):
             patch = first + i
-            o_ref[2 * owner_of(patch // 2) + patch % 2] = x[i * NMEM : (i + 1) * NMEM]
+            o_ref[sent_row(patch)] = x[i * NMEM : (i + 1) * NMEM]
 
 
 def exact(a, b):
@@ -125,7 +154,8 @@
     eye = identity()
     for j, s in enumerate(matrices):
         s2 = dot3(s, s)
-        top = jnp.max(jnp.sqrt(jnp.sum(jnp.abs(s2), axis=0, keepdims=True)))
+        norms = jnp.sum(jnp.abs(s2), axis=0, keepdims=True)
+        top = jnp.sqrt(jnp.max(norms, axis=1, keepdims=True))
         c = 2.0 / (top + 1.0)
         delta = (top - 1.0) / (top + 1.0)
         mu = 2.0 / (2.0 - delta * delta)
@@ -135,7 +165,7 @@
         mu = 2.0 / (2.0 - delta * delta)
         s_ref[j] = s
         x_ref[j] = mu * (2.0 * x1 - dot3(x1, t1))
-        deltas.append(delta * delta / (2.0 - delta * delta))
+        deltas.append(jnp.max(delta * delta / (2.0 - delta * delta)))
 
     def more(state):
         return jnp.maximum(state[0], state[1]) > 0.02
@@ -155,7 +185,7 @@
 
 def own_kernel(
     idx_ref, f_ref, p_ref, slot_ref, var_ref,
-    ah, al, bh, bl, dh, dl, inv_ref, part_ref, s_ref, x_ref,
+    ah, al, bh, bl, dh, dl, inv_ref, part_ref, base_ref, s_ref, x_ref,
 ):
     members = NMEM * NMEM
     root = lax.rsqrt(var_ref[...])
@@ -180,17 +210,22 @@
         x = 2.0 * x - dot3(x, dot3(s, x))
         x = 2.0 * x - exact(x, exact(s, x))
         inv_ref[j] = x
-        part_ref[j] = exact(x, crosses[j])
+        part = exact(x, crosses[j])
+        part_ref[j] = part
+        o = idx_ref[j, 0] - 1
+        ph, pl_ = split(part)
+        gained = dot(dh[o], ph) + (dot(dh[o], pl_) + dot(dl[o], ph))
+        base_ref[:, j] = f_ref[:, j] + gained.reshape(NMEM, NMEM, PV)
 
 
 def update_kernel(
     idx_ref, f_ref, fl_ref, fr_ref, p_ref, pl_ref, pr_ref, slot_ref, var_ref,
-    ah, al, bh, bl, dh, dl, inv_ref, part_ref, o_ref, hh, hl, s_ref, x_ref,
+    ah, al, bh, bl, dh, dl, inv_ref, part_ref, base_ref, o_ref, hh, hl, s_ref, x_ref,
 ):
     members = NMEM * NMEM
     scale = 1.0 / (members - 1)
     fields, readings = (fl_ref, fr_ref), (pl_ref, pr_ref)
-    complements, links, crosses = [], [], []
+    complements, crosses = [], []
     for j in range(2):
         o, h = idx_ref[j, 0] - 1, idx_ref[j, 1]
         apart = h == 3 * j
@@ -199,28 +234,37 @@
         y = observe(x, slot_ref[pl.ds(h, 1), :])
         r = lax.rsqrt(var_ref[pl.ds(h, 1), :])
         high, low = split(centred(y) * r)
-        hh[j], hl[j] = split((p - y) * r)
         right = jnp.concatenate([bh[o], high, ah[j]], axis=1)
         under = jnp.concatenate([bl[o], low, al[j]], axis=1)
         gram = (tdot(high, right) + (tdot(high, under) + tdot(low, right))) * scale
         s_ho, s_hh, g_h = gram[:, :PV], gram[:, PV : 2 * PV] + identity(), gram[:, 2 * PV :]
         link = dot3(s_ho, inv_ref[j])
         complements.append(s_hh - dot3(link, s_ho.T))
-        links.append(link)
         crosses.append(g_h - dot3(s_ho, part_ref[j]))
+        lh, ll = split(link)
+        carried = dot_t(dh[o], lh) + (dot_t(dh[o], ll) + dot_t(dl[o], lh))
+        hh[j], hl[j] = split((p - y) * r - carried)
     inverses(complements, s_ref, x_ref)
     for j in range(2):
         s, x, g = s_ref[j], x_ref[j], crosses[j]
         k_h = dot3(x, g)
         for _ in range(2):
             k_h = k_h + dot3(x, g - exact(s, k_h))
-        k_o = part_ref[j] - dot3(links[j].T, k_h)
-        kh, kl = split(jnp.concatenate([k_o, k_h], axis=0))
-        o = idx_ref[j, 0] - 1
-        ih = jnp.concatenate([dh[o], hh[j]], axis=1)
-        il = jnp.concatenate([dl[o], hl[j]], axis=1)
-        gained = dot(ih, kh) + (dot(ih, kl) + dot(il, kh))
-        o_ref[:, j] = f_ref[:, j] + gained.reshape(NMEM, NMEM, PV)
+        kh, kl = split(k_h)
+        gained = dot(hh[j], kh) + (dot(hh[j], kl) + dot(hl[j], kh))
+        o_ref[:, j] = base_ref[:, j] + gained.reshape(NMEM, NMEM, PV)
+
+
+def copying_call(kernel, out, space, scratch, limit=16):
+    return pl.pallas_call(
+        kernel,
+        out_shape=jax.ShapeDtypeStruct(out, F32),
+        in_specs=[pl.BlockSpec(memory_space=space)],
+        out_specs=pl.BlockSpec(memory_space=pl.ANY),
+        scratch_shapes=scratch,
+        compiler_params=pltpu.CompilerParams(vmem_limit_bytes=limit << 20),
+        cost_estimate=pl.CostEstimate(flops=10**9, bytes_accessed=2 << 20, transcendentals=0),
+    )
 
 
 def vmem_call(kernel, out, scratch=(), smem=0, limit=24, n_in=1, us=2):
@@ -251,7 +295,14 @@
     both = ("mem", "space")
     first = 2 * pair_of(lax.axis_index("mem"))
 
-    pert_send = vmem_call(to_send_kernel, sent)(perturbed_obs.reshape(rows, PV))
+    pert_send = copying_call(
+        to_send_kernel, sent, pl.ANY,
+        [
+            pltpu.VMEM(perturbed_obs.shape, F32), pltpu.VMEM(sent, F32),
+            pltpu.SemaphoreType.DMA((PIECES,)), pltpu.SemaphoreType.DMA((PAIRS // 2,)),
+        ],
+        limit=60,
+    )(perturbed_obs)
     pert = lax.all_to_all(pert_send.reshape(packed), "mem", 0, 0, tiled=True)
 
     field_send = vmem_call(
@@ -286,18 +337,22 @@
     members = NMEM * NMEM
     pair = jax.ShapeDtypeStruct((2, members, PV), BF16)
     small = jax.ShapeDtypeStruct((2, PV, PV), F32)
+    base = jax.ShapeDtypeStruct(packed, F32)
     half = pltpu.VMEM((2, members, PV), BF16)
     square = pltpu.VMEM((2, PV, PV), F32)
     index = jnp.concatenate([index[:1, ::-1], index[1:]], axis=0)
     own_parts = vmem_call(
-        own_kernel, [pair] * 6 + [small] * 2, [square, square], smem=1, n_in=5, us=9
+        own_kernel, [pair] * 6 + [small] * 2 + [base], [square, square], smem=1, n_in=5, us=9
     )(index, field, pert, slots, variances)
-    analysis = vmem_call(update_kernel, packed, [half, half, square, square], smem=1, n_in=17, us=7)(
+    analysis = vmem_call(update_kernel, packed, [half, half, square, square], smem=1, n_in=18, us=7)(
         index, field, field_left, field_right, pert, pert_left, pert_right, slots, variances,
         *own_parts,
     )
     returned = lax.all_to_all(analysis, "mem", 0, 0, tiled=True)
-    out = vmem_call(from_sent_kernel, (rows, PV))(returned.reshape(sent))
+    out = copying_call(
+        from_sent_kernel, (rows, PV), pltpu.VMEM,
+        [pltpu.VMEM((rows, PV), F32), pltpu.SemaphoreType.DMA((PIECES,))],
+    )(returned.reshape(sent))
     return out.reshape(prior_sample_set.shape)
 
 

time: 135 us -> 133 us (0.985)
    unnamed x21 -> x19, local copies, waits for them, and re-layouts: 2.92 us -> 1.69 us
  transfers between devices with their start and end apart: 8 -> 8, of which waited for: 4 -> 4; matrix products, arithmetic and copies ran while one was open for 1% -> 1% of each run, Pallas kernels for 9% -> 10%
where the time goes in v4:
time: 133 us; the launch traced here: 132 us
  waiting for transfers between devices  39.7 us (30%)
  blocking collectives  39.5 us (30%)
  starting transfers between devices  25.7 us (19%)
  Pallas kernels  23.8 us (18%)
  local copies, waits for them, and re-layouts  3.01 us (2%)
    all_to_all x1, blocking collectives, body(): returned = lax.all_to_all(analysis, 'mem', 0, 0, tiled=True)  39.5 us
    all_to_all x1, waiting for transfers between devices, body(): pert = lax.all_to_all(pert_send.reshape(packed), 'mem', 0, 0, tiled=True)  19.8 us
    all_to_all x1, waiting for transfers between devices, body(): field = lax.all_to_all(field_send.reshape(packed), 'mem', 0, 0, tiled=True)  18.9 us
    all_to_all x1, starting transfers between devices, body(): pert = lax.all_to_all(pert_send.reshape(packed), 'mem', 0, 0, tiled=True)  10.5 us
    pallas_call x1, Pallas kernels, body(): vmem_call(forecast_kernel, sent, [pltpu.VMEM((2 * LEV, 2 * HID), BF16)] *...  6.8 us
    pallas_call x1, Pallas kernels, body(): vmem_call(update_kernel, packed, [half, half, square, square], smem=1, n_...  6.7 us
    pallas_call x1, Pallas kernels, body(): vmem_call(own_kernel, [pair] * 6 + [small] * 2 + [base], [square, square]...  6.54 us
    all_to_all x1, starting transfers between devices, body(): field = lax.all_to_all(field_send.reshape(packed), 'mem', 0, 0, tiled=True)  4.68 us
  transfers between devices with their start and end apart: 8, of which 4 were waited for; matrix products, arithmetic and copies ran while one was open for 1% of the time, Pallas kernels for 10%

profile of v4, /device:TPU:3, one launch (start us, length us, event | category | flops | bytes accessed | tf_op | source)
XLA Modules:
  0.0 132.2 jit_solution(15889335559557933147)
XLA Ops:
  0.0 2.4 %shard_map.101 = f32[64,32,128]{2,1,0:T(8,128)} custom-call(f32[32,64,128]{2,1,0:T(8,128)} %x_ref.1), custom_call_target="tpu_custom_call" | custom-call | flops 1000000000 | bytes 2097152 | tf_op jit(solution)/shard_map/pallas_call | solution.py:298
  2.4 0.0 copy-start.7
  2.4 0.0 copy-start.1
  2.4 10.5 %all-to-all-start.1 = ((f32[32,2,32,128]{3,2,1,0:T(8,128)}), f32[32,2,32,128]{3,2,1,0:T(8,128)S(1)}, u32[]{:S(2)}, u32[]{:S(2)}) async-start(f32[32,2,32,128]{3,2,1,0:T(8,128)} %bitcast.31), calls=%async_computation.1 | async-start | bytes 2097152 | tf_op jit(solution)/shard_map/all_to_all | solution.py:306
  13.0 0.0 copy-start.8
  13.0 0.7 copy-done.8
  13.8 0.0 copy-start.4
  13.8 0.0 copy-start.5
  13.8 0.8 copy-done.2
  14.6 0.0 copy-done.3
  14.6 6.8 %shard_map.100 = f32[64,32,128]{2,1,0:T(8,128)} custom-call(f32[2048,128]{1,0:T(8,128)S(1)} %bitcast.26, f32[1,64]{1,0:T(1,128)S(1)} %bitcast.29, bf16[64,512]{1,0:T(8,128)(2,1)S(1)} %copy-done.2, f32[1,512]{1,0:T(1,128)S(1)} %bitcast.28, bf16[64,512]{1,0:T(8,128)(2,1)S(1)} %bitcast.27, f32[1,64]{1,0:T(1,128)S(1)} %bitcast.30), custom_call_target="tpu_custom_call" | custom-call | flops 7000000000 | bytes 1048576 | tf_op jit(solution)/shard_map/pallas_call | solution.py:308
  21.4 19.8 %all-to-all-done.1.p_ref = f32[32,2,32,128]{3,2,1,0:T(8,128)S(1)} async-done(((f32[32,2,32,128]{3,2,1,0:T(8,128)}), f32[32,2,32,128]{3,2,1,0:T(8,128)S(1)}, u32[]{:S(2)}, u32[]{:S(2)}) %all-to-all-start.1) | async-done | bytes 1048608 | tf_op jit(solution)/shard_map/all_to_all | solution.py:306
  41.2 4.7 %all-to-all-start = ((f32[32,2,32,128]{3,2,1,0:T(8,128)}), f32[32,2,32,128]{3,2,1,0:T(8,128)S(1)}, u32[]{:S(2)}, u32[]{:S(2)}) async-start(f32[32,2,32,128]{3,2,1,0:T(8,128)} %bitcast.5), calls=%async_computation | async-start | bytes 2097152 | tf_op jit(solution)/shard_map/all_to_all | solution.py:317
  45.9 1.4 %collective-permute-start.4 = (f32[1,256]{1,0:T(1,128)S(1)}, f32[1,256]{1,0:T(1,128)S(1)}, u32[]{:S(2)}, u32[]{:S(2)}) collective-permute-start(f32[1,256]{1,0:T(1,128)S(1)} %get-tuple-element.31), channel_id=1, source_target_pairs={{0,1},{1,2},{2,3},{3,4},{4,5},{5,6},{6,7},{7,0},{8,9},{9,10},{10,1... | collective-permute-start | bytes 3080 | tf_op jit(solution)/shard_map/ppermute | solution.py:320
  47.3 3.8 %collective-permute-start.5 = (f32[1,256]{1,0:T(1,128)S(1)}, f32[1,256]{1,0:T(1,128)S(1)}, u32[]{:S(2)}, u32[]{:S(2)}) collective-permute-start(f32[1,256]{1,0:T(1,128)S(1)} %get-tuple-element.32), channel_id=1, source_target_pairs={{1,0},{2,1},{3,2},{4,3},{5,4},{6,5},{7,6},{0,7},{9,8},{10,9},{11,1... | collective-permute-start | bytes 3080 | tf_op jit(solution)/shard_map/ppermute | solution.py:321
  51.1 0.1 constant_dynamic-slice_fusion
  51.2 0.1 copy.28
  51.3 0.1 fusion.2
  51.4 0.1 rev.3
  51.5 0.7 collective-permute-done.4
  52.2 1.1 slice_bitcast_fusion
  53.3 1.4 %collective-permute-start.3 = (f32[32,32,128]{2,1,0:T(8,128)}, f32[32,32,128]{2,1,0:T(8,128)S(1)}, u32[]{:S(2)}, u32[]{:S(2)}) collective-permute-start(f32[32,32,128]{2,1,0:T(8,128)} %get-tuple-element.27), channel_id=1, source_target_pairs={{0,31},{8,0},{32,8},{40,32},{64,40},{72,64},{96,72},{104,96},{128,... | collective-permute-start | bytes 1572872 | tf_op jit(solution)/shard_map/ppermute | solution.py:333
  54.7 1.3 collective-permute-start.2
  56.0 18.9 %all-to-all-done.f_ref = f32[32,2,32,128]{3,2,1,0:T(8,128)S(1)} async-done(((f32[32,2,32,128]{3,2,1,0:T(8,128)}), f32[32,2,32,128]{3,2,1,0:T(8,128)S(1)}, u32[]{:S(2)}, u32[]{:S(2)}) %all-to-all-start) | async-done | bytes 1048608 | tf_op jit(solution)/shard_map/all_to_all | solution.py:317
  74.9 0.1 slice_bitcast_fusion.2
  74.9 0.7 collective-permute-start.1
  75.6 2.0 %collective-permute-start = (f32[32,32,128]{2,1,0:T(8,128)S(1)}, f32[32,32,128]{2,1,0:T(8,128)S(1)}, u32[]{:S(2)}, u32[]{:S(2)}) collective-permute-start(f32[32,32,128]{2,1,0:T(8,128)S(1)} %get-tuple-element.30), channel_id=1, source_target_pairs={{0,8},{8,32},{32,40},{40,64},{64,72},{72,96},{96,104},{104,128},{1... | collective-permute-start | bytes 1572872 | tf_op jit(solution)/shard_map/ppermute | solution.py:334
  77.7 6.5 %shard_map.102 = (bf16[2,1024,128]{2,1,0:T(8,128)(2,1)S(1)}, bf16[2,1024,128]{2,1,0:T(8,128)(2,1)S(1)}, bf16[2,1024,128]{2,1,0:T(8,128)(2,1)S(1)}, bf16[2,1024,1...) custom-call(s32[2,2]{1,0:T(2,128)S(1)} %pad_add_fusion.idx_ref, ...), custom_call_target="tpu_custom_call" | custom-call | flops 8999999488 | bytes 1048576 | tf_op jit(solution)/shard_map/pallas_call | solution.py:344
  84.2 0.3 collective-permute-done.1.fr_ref
  84.5 6.7 %shard_map.103 = f32[32,2,32,128]{3,2,1,0:T(8,128)S(1)} custom-call(s32[2,2]{1,0:T(2,128)S(1)} %pad_add_fusion.idx_ref, f32[32,2,32,128]{3,2,1,0:T(8,128)S(1)} %all-to-all-done.f_ref, f32[32,32,128]{2,1,0:T(8,128)S(1)} %collective-permute-done.fl_ref, f32[32,32,128]{2,1,0:T(8,128)S(1)} %collective-permute-done.1.fr_ref, ...), custom_call_target="tpu_custom_call" | custom-call | flops 7000000000 | bytes 1048576 | tf_op jit(solution)/shard_map/pallas_call | solution.py:347
  91.2 39.5 %all_to_all.15 = f32[32,2,32,128]{3,2,1,0:T(8,128)S(1)} all-to-all(f32[32,2,32,128]{3,2,1,0:T(8,128)S(1)} %shard_map.103), channel_id=1, replica_groups=mesh['mem'=32,'space'=8] {'mem'}, dimensions={0} | all-to-all | bytes 2097152 | tf_op jit(solution)/shard_map/all_to_all | solution.py:351
  130.8 1.3 %shard_map.104 = f32[2048,128]{1,0:T(8,128)} custom-call(f32[64,32,128]{2,1,0:T(8,128)S(1)} %bitcast.25), custom_call_target="tpu_custom_call" | custom-call | flops 1000000000 | bytes 2097152 | tf_op jit(solution)/shard_map/pallas_call | solution.py:352
  (22 shorter events, 0.1 us)
Async XLA Ops:
  0.0 51.1 %copy-start = (s32[64,2]{0,1:T(2,128)S(1)}, s32[64,2]{0,1:T(2,128)}, u32[]{:S(2)}) copy-start(s32[64,2]{0,1:T(2,128)} %param.14) | copy-start | bytes 1540
  2.4 10.6 %copy-start.7 = (s32[64,128]{1,0:T(8,128)S(1)}, s32[64,128]{1,0:T(8,128)}, u32[]{:S(2)}) copy-start(s32[64,128]{1,0:T(8,128)} %param.12) | copy-start | bytes 98308
  2.4 11.4 %copy-start.1 = (f32[32,64,128]{2,1,0:T(8,128)S(1)}, f32[32,64,128]{2,1,0:T(8,128)}, u32[]{:S(2)}) copy-start(f32[32,64,128]{2,1,0:T(8,128)} %param.10) | copy-start | bytes 3145732
  2.4 38.8 %all-to-all-start.1 = ((f32[32,2,32,128]{3,2,1,0:T(8,128)}), f32[32,2,32,128]{3,2,1,0:T(8,128)S(1)}, u32[]{:S(2)}, u32[]{:S(2)}) async-start(f32[32,2,32,128]{3,2,1,0:T(8,128)} %bitcast.31), calls=%async_computation.1 | async-start | bytes 2097152 | tf_op jit(solution)/shard_map/all_to_all | solution.py:306
  13.0 0.8 copy-start.8
  13.8 0.8 copy-start.2
  13.8 0.9 copy-start.3
  13.8 0.9 copy-start.4
  13.8 0.9 copy-start.5
  13.8 0.8 copy-start.6
  41.2 33.6 %all-to-all-start = ((f32[32,2,32,128]{3,2,1,0:T(8,128)}), f32[32,2,32,128]{3,2,1,0:T(8,128)S(1)}, u32[]{:S(2)}, u32[]{:S(2)}) async-start(f32[32,2,32,128]{3,2,1,0:T(8,128)} %bitcast.5), calls=%async_computation | async-start | bytes 2097152 | tf_op jit(solution)/shard_map/all_to_all | solution.py:317
  45.9 6.3 %collective-permute-start.4 = (f32[1,256]{1,0:T(1,128)S(1)}, f32[1,256]{1,0:T(1,128)S(1)}, u32[]{:S(2)}, u32[]{:S(2)}) collective-permute-start(f32[1,256]{1,0:T(1,128)S(1)} %get-tuple-element.31), channel_id=1, source_target_pairs={{0,1},{1,2},{2,3},{3,4},{4,5},{5,6},{6,7},{7,0},{8,9},{9,10},{10,1... | collective-permute-start | bytes 3080 | tf_op jit(solution)/shard_map/ppermute | solution.py:320
  47.3 4.9 %collective-permute-start.5 = (f32[1,256]{1,0:T(1,128)S(1)}, f32[1,256]{1,0:T(1,128)S(1)}, u32[]{:S(2)}, u32[]{:S(2)}) collective-permute-start(f32[1,256]{1,0:T(1,128)S(1)} %get-tuple-element.32), channel_id=1, source_target_pairs={{1,0},{2,1},{3,2},{4,3},{5,4},{6,5},{7,6},{0,7},{9,8},{10,9},{11,1... | collective-permute-start | bytes 3080 | tf_op jit(solution)/shard_map/ppermute | solution.py:321
  53.3 30.9 %collective-permute-start.3 = (f32[32,32,128]{2,1,0:T(8,128)}, f32[32,32,128]{2,1,0:T(8,128)S(1)}, u32[]{:S(2)}, u32[]{:S(2)}) collective-permute-start(f32[32,32,128]{2,1,0:T(8,128)} %get-tuple-element.27), channel_id=1, source_target_pairs={{0,31},{8,0},{32,8},{40,32},{64,40},{72,64},{96,72},{104,96},{128,... | collective-permute-start | bytes 1572872 | tf_op jit(solution)/shard_map/ppermute | solution.py:333
  54.7 29.6 %collective-permute-start.2 = (f32[32,32,128]{2,1,0:T(8,128)}, f32[32,32,128]{2,1,0:T(8,128)S(1)}, u32[]{:S(2)}, u32[]{:S(2)}) collective-permute-start(f32[32,32,128]{2,1,0:T(8,128)} %get-tuple-element.28), channel_id=1, source_target_pairs={{0,8},{8,32},{32,40},{40,64},{64,72},{72,96},{96,104},{104,128},{1... | collective-permute-start | bytes 1572872 | tf_op jit(solution)/shard_map/ppermute | solution.py:332
  74.9 9.6 %collective-permute-start.1 = (f32[32,32,128]{2,1,0:T(8,128)S(1)}, f32[32,32,128]{2,1,0:T(8,128)S(1)}, u32[]{:S(2)}, u32[]{:S(2)}) collective-permute-start(f32[32,32,128]{2,1,0:T(8,128)S(1)} %get-tuple-element.29), channel_id=1, source_target_pairs={{0,31},{8,0},{32,8},{40,32},{64,40},{72,64},{96,72},{104,96},{128,... | collective-permute-start | bytes 1572872 | tf_op jit(solution)/shard_map/ppermute | solution.py:335
  75.6 8.9 %collective-permute-start = (f32[32,32,128]{2,1,0:T(8,128)S(1)}, f32[32,32,128]{2,1,0:T(8,128)S(1)}, u32[]{:S(2)}, u32[]{:S(2)}) collective-permute-start(f32[32,32,128]{2,1,0:T(8,128)S(1)} %get-tuple-element.30), channel_id=1, source_target_pairs={{0,8},{8,32},{32,40},{40,64},{64,72},{72,96},{96,104},{104,128},{1... | collective-permute-start | bytes 1572872 | tf_op jit(solution)/shard_map/ppermute | solution.py:334

commit v5 on v4

--- a/solution.py
+++ b/solution.py
@@ -22,21 +22,23 @@
     return (z * 2 + x) * 2 + core
 
 
-def pair_of(member):
-    z, x, core = member // 4, (member // 2) % 2, member % 2
+def mirrored(run):
+    return (run + 1 + run // 4) % 2
+
+
+def pair_of(member, run):
+    z, x, core = member // 4, (member // 2 + mirrored(run)) % 2, member % 2
     return 2 * jnp.where(x == 0, z, 15 - z) + core
 
 
 def neighbour_moves(step):
     runs = 8
-    moves = []
-    for run in range(runs):
-        for pair in range(PAIRS):
-            there = (run * PAIRS + pair + step) % (runs * PAIRS)
-            moves.append(
-                (owner_of(pair) * runs + run, owner_of(there % PAIRS) * runs + there // PAIRS)
-            )
-    return moves
+
+    def device(patches):
+        run, pair = patches // PAIRS % runs, patches % PAIRS
+        return (owner_of(pair) ^ 2 * mirrored(run)) * runs + run
+
+    return [(device(here), device(here + step)) for here in range(runs * PAIRS)]
 
 
 def dot(a, b):
@@ -61,11 +63,17 @@
     return dot(ah, bh) + (dot(ah, bl) + dot(al, bh))
 
 
-def sent_row(patch):
-    return 2 * owner_of(patch // 2) + patch % 2
+def row_shift():
+    return 4 * mirrored(lax.axis_index("space"))
+
+
+def sent_row(patch, shift):
+    row = 2 * owner_of(patch // 2) + patch % 2
+    return row - shift if row & 4 else row + shift
 
 
 def to_send_kernel(x_ref, o_ref, came, put, in_sems, out_sems):
+    shift = row_shift()
     group = 2 * PAIRS // PIECES
     for g in range(PIECES):
         part = pl.ds(g * group, group)
@@ -77,8 +85,8 @@
         pltpu.make_async_copy(x_ref.at[:, part], came.at[:, part], in_sems.at[g]).wait()
         for chip in range(g * group // 4, (g + 1) * group // 4):
             for patch in range(4 * chip, 4 * chip + 4):
-                put[sent_row(patch)] = rows[pl.ds(patch, NMEM, stride=2 * PAIRS), :]
-            part = pl.ds(sent_row(4 * chip), 4)
+                put[sent_row(patch, shift)] = rows[pl.ds(patch, NMEM, stride=2 * PAIRS), :]
+            part = pl.ds(sent_row(4 * chip, shift), 4)
             copies.append(pltpu.make_async_copy(put.at[part], o_ref.at[part], out_sems.at[chip]))
             copies[-1].start()
     for copy in copies:
@@ -86,13 +94,14 @@
 
 
 def from_sent_kernel(x_ref, o_ref, put, sems):
+    shift = row_shift()
     step = NMEM // PIECES
     copies = []
     for g in range(PIECES):
         first = g * step * 2 * PAIRS
         for patch in range(2 * PAIRS):
             put[pl.ds(first + patch, step, stride=2 * PAIRS), :] = x_ref[
-                sent_row(patch), g * step : (g + 1) * step
+                sent_row(patch, shift), g * step : (g + 1) * step
             ]
         part = pl.ds(first, step * 2 * PAIRS)
         copies.append(pltpu.make_async_copy(put.at[part], o_ref.at[part], sems.at[g]))
@@ -114,7 +123,7 @@
     row = lax.broadcasted_iota(jnp.int32, (2 * PV, PV), 0)
     col = lax.broadcasted_iota(jnp.int32, (2 * PV, PV), 1)
     halves = jnp.where((row % PV) // LEV == col // LEV, 1.0, 0.0).astype(BF16)
-    chunk = PAIRS
+    chunk, shift = PAIRS, row_shift()
     for first in range(0, 2 * PAIRS, chunk):
         x = jnp.concatenate(
             [x_ref[pl.ds(first + i, NMEM, stride=2 * PAIRS), :] for i in range(chunk)], axis=0
@@ -128,7 +137,7 @@
             x = x + dot_t(hidden, wo2[...]) + bo
         for i in range(chunk):
             patch = first + i
-            o_ref[sent_row(patch)] = x[i * NMEM : (i + 1) * NMEM]
+            o_ref[sent_row(patch, shift)] = x[i * NMEM : (i + 1) * NMEM]
 
 
 def exact(a, b):
@@ -293,7 +302,7 @@
     sent = (2 * PAIRS, NMEM, PV)
     packed = (NMEM, 2, NMEM, PV)
     both = ("mem", "space")
-    first = 2 * pair_of(lax.axis_index("mem"))
+    first = 2 * pair_of(lax.axis_index("mem"), lax.axis_index("space"))
 
     pert_send = copying_call(
         to_send_kernel, sent, pl.ANY,

time: 133 us -> 130 us (0.977)
  blocking collectives: 39.5 us -> 36 us
    all_to_all x1, blocking collectives: 39.5 us -> 36 us  [body(): returned = lax.all_to_all(analysis, 'mem', 0, 0, tiled=True)]
where the time goes in v5:
time: 130 us; the launch traced here: 128 us
  waiting for transfers between devices  39.9 us (31%)
  blocking collectives  36 us (28%)
  starting transfers between devices  24.8 us (19%)
  Pallas kernels  23.8 us (18%)
  local copies, waits for them, and re-layouts  3.01 us (2%)
    all_to_all x1, blocking collectives, body(): returned = lax.all_to_all(analysis, 'mem', 0, 0, tiled=True)  36 us
    all_to_all x1, waiting for transfers between devices, body(): pert = lax.all_to_all(pert_send.reshape(packed), 'mem', 0, 0, tiled=True)  19.8 us
    all_to_all x1, waiting for transfers between devices, body(): field = lax.all_to_all(field_send.reshape(packed), 'mem', 0, 0, tiled=True)  18.8 us
    all_to_all x1, starting transfers between devices, body(): pert = lax.all_to_all(pert_send.reshape(packed), 'mem', 0, 0, tiled=True)  10.5 us
    pallas_call x1, Pallas kernels, body(): vmem_call(forecast_kernel, sent, [pltpu.VMEM((2 * LEV, 2 * HID), BF16)] *...  6.81 us
    pallas_call x1, Pallas kernels, body(): vmem_call(update_kernel, packed, [half, half, square, square], smem=1, n_...  6.7 us
    pallas_call x1, Pallas kernels, body(): vmem_call(own_kernel, [pair] * 6 + [small] * 2 + [base], [square, square]...  6.53 us
    all_to_all x1, starting transfers between devices, body(): field = lax.all_to_all(field_send.reshape(packed), 'mem', 0, 0, tiled=True)  4.68 us
  transfers between devices with their start and end apart: 8, of which 4 were waited for; matrix products, arithmetic and copies ran while one was open for 1% of the time, Pallas kernels for 10%

profile of v5, /device:TPU:3, one launch (start us, length us, event | category | flops | bytes accessed | tf_op | source)
XLA Modules:
  0.0 128.0 jit_solution(16582833600351421854)
XLA Ops:
  0.0 2.4 %shard_map.101 = f32[64,32,128]{2,1,0:T(8,128)} custom-call(f32[32,64,128]{2,1,0:T(8,128)} %x_ref.1), custom_call_target="tpu_custom_call" | custom-call | flops 1000000000 | bytes 2097152 | tf_op jit(solution)/shard_map/pallas_call | solution.py:307
  2.4 0.0 copy-start.7
  2.4 0.0 copy-start.1
  2.4 10.5 %all-to-all-start.1 = ((f32[32,2,32,128]{3,2,1,0:T(8,128)}), f32[32,2,32,128]{3,2,1,0:T(8,128)S(1)}, u32[]{:S(2)}, u32[]{:S(2)}) async-start(f32[32,2,32,128]{3,2,1,0:T(8,128)} %bitcast.31), calls=%async_computation.1 | async-start | bytes 2097152 | tf_op jit(solution)/shard_map/all_to_all | solution.py:315
  13.0 0.0 copy-start.8
  13.0 0.7 copy-done.8
  13.8 0.0 copy-start.4
  13.8 0.0 copy-start.6
  13.8 0.8 copy-done.2
  14.6 0.0 copy-done.3
  14.6 6.8 %shard_map.100 = f32[64,32,128]{2,1,0:T(8,128)} custom-call(f32[2048,128]{1,0:T(8,128)S(1)} %bitcast.26, f32[1,64]{1,0:T(1,128)S(1)} %bitcast.29, bf16[64,512]{1,0:T(8,128)(2,1)S(1)} %copy-done.2, f32[1,512]{1,0:T(1,128)S(1)} %bitcast.28, bf16[64,512]{1,0:T(8,128)(2,1)S(1)} %bitcast.27, f32[1,64]{1,0:T(1,128)S(1)} %bitcast.30), custom_call_target="tpu_custom_call" | custom-call | flops 7000000000 | bytes 1048576 | tf_op jit(solution)/shard_map/pallas_call | solution.py:317
  21.4 19.8 %all-to-all-done.1.p_ref = f32[32,2,32,128]{3,2,1,0:T(8,128)S(1)} async-done(((f32[32,2,32,128]{3,2,1,0:T(8,128)}), f32[32,2,32,128]{3,2,1,0:T(8,128)S(1)}, u32[]{:S(2)}, u32[]{:S(2)}) %all-to-all-start.1) | async-done | bytes 1048608 | tf_op jit(solution)/shard_map/all_to_all | solution.py:315
  41.2 4.7 %all-to-all-start = ((f32[32,2,32,128]{3,2,1,0:T(8,128)}), f32[32,2,32,128]{3,2,1,0:T(8,128)S(1)}, u32[]{:S(2)}, u32[]{:S(2)}) async-start(f32[32,2,32,128]{3,2,1,0:T(8,128)} %bitcast.5), calls=%async_computation | async-start | bytes 2097152 | tf_op jit(solution)/shard_map/all_to_all | solution.py:326
  45.9 1.4 %collective-permute-start.4 = (f32[1,256]{1,0:T(1,128)S(1)}, f32[1,256]{1,0:T(1,128)S(1)}, u32[]{:S(2)}, u32[]{:S(2)}) collective-permute-start(f32[1,256]{1,0:T(1,128)S(1)} %get-tuple-element.31), channel_id=1, source_target_pairs={{0,1},{1,2},{2,3},{3,4},{4,5},{5,6},{6,7},{7,0},{8,9},{9,10},{10,1... | collective-permute-start | bytes 3080 | tf_op jit(solution)/shard_map/ppermute | solution.py:329
  47.3 3.8 %collective-permute-start.5 = (f32[1,256]{1,0:T(1,128)S(1)}, f32[1,256]{1,0:T(1,128)S(1)}, u32[]{:S(2)}, u32[]{:S(2)}) collective-permute-start(f32[1,256]{1,0:T(1,128)S(1)} %get-tuple-element.32), channel_id=1, source_target_pairs={{1,0},{2,1},{3,2},{4,3},{5,4},{6,5},{7,6},{0,7},{9,8},{10,9},{11,1... | collective-permute-start | bytes 3080 | tf_op jit(solution)/shard_map/ppermute | solution.py:330
  51.1 0.1 constant_dynamic-slice_fusion
  51.2 0.1 copy.28
  51.3 0.1 fusion.2
  51.4 0.1 rev.3
  51.5 0.7 collective-permute-done.4
  52.2 1.1 slice_bitcast_fusion
  53.3 1.4 %collective-permute-start.3 = (f32[32,32,128]{2,1,0:T(8,128)}, f32[32,32,128]{2,1,0:T(8,128)S(1)}, u32[]{:S(2)}, u32[]{:S(2)}) collective-permute-start(f32[32,32,128]{2,1,0:T(8,128)} %get-tuple-element.27), channel_id=1, source_target_pairs={{16,15},{24,16},{48,24},{56,48},{80,56},{88,80},{112,88},{120,112}... | collective-permute-start | bytes 1572872 | tf_op jit(solution)/shard_map/ppermute | solution.py:342
  54.7 1.3 collective-permute-start.2
  55.9 18.8 %all-to-all-done.f_ref = f32[32,2,32,128]{3,2,1,0:T(8,128)S(1)} async-done(((f32[32,2,32,128]{3,2,1,0:T(8,128)}), f32[32,2,32,128]{3,2,1,0:T(8,128)S(1)}, u32[]{:S(2)}, u32[]{:S(2)}) %all-to-all-start) | async-done | bytes 1048608 | tf_op jit(solution)/shard_map/all_to_all | solution.py:326
  74.7 0.1 slice_bitcast_fusion.2
  74.8 0.7 collective-permute-start.1
  75.5 1.1 collective-permute-start
  76.6 6.5 %shard_map.102 = (bf16[2,1024,128]{2,1,0:T(8,128)(2,1)S(1)}, bf16[2,1024,128]{2,1,0:T(8,128)(2,1)S(1)}, bf16[2,1024,128]{2,1,0:T(8,128)(2,1)S(1)}, bf16[2,1024,1...) custom-call(s32[2,2]{1,0:T(2,128)S(1)} %pad_add_fusion.idx_ref, ...), custom_call_target="tpu_custom_call" | custom-call | flops 8999999488 | bytes 1048576 | tf_op jit(solution)/shard_map/pallas_call | solution.py:353
  83.2 0.6 collective-permute-done.1.fr_ref
  83.7 6.7 %shard_map.103 = f32[32,2,32,128]{3,2,1,0:T(8,128)S(1)} custom-call(s32[2,2]{1,0:T(2,128)S(1)} %pad_add_fusion.idx_ref, f32[32,2,32,128]{3,2,1,0:T(8,128)S(1)} %all-to-all-done.f_ref, f32[32,32,128]{2,1,0:T(8,128)S(1)} %collective-permute-done.fl_ref, f32[32,32,128]{2,1,0:T(8,128)S(1)} %collective-permute-done.1.fr_ref, ...), custom_call_target="tpu_custom_call" | custom-call | flops 7000000000 | bytes 1048576 | tf_op jit(solution)/shard_map/pallas_call | solution.py:356
  90.5 36.0 %all_to_all.15 = f32[32,2,32,128]{3,2,1,0:T(8,128)S(1)} all-to-all(f32[32,2,32,128]{3,2,1,0:T(8,128)S(1)} %shard_map.103), channel_id=1, replica_groups=mesh['mem'=32,'space'=8] {'mem'}, dimensions={0} | all-to-all | bytes 2097152 | tf_op jit(solution)/shard_map/all_to_all | solution.py:360
  126.4 1.4 %shard_map.104 = f32[2048,128]{1,0:T(8,128)} custom-call(f32[64,32,128]{2,1,0:T(8,128)S(1)} %bitcast.25), custom_call_target="tpu_custom_call" | custom-call | flops 1000000000 | bytes 2097152 | tf_op jit(solution)/shard_map/pallas_call | solution.py:361
  (22 shorter events, 0.1 us)
Async XLA Ops:
  0.0 51.1 %copy-start = (s32[64,2]{0,1:T(2,128)S(1)}, s32[64,2]{0,1:T(2,128)}, u32[]{:S(2)}) copy-start(s32[64,2]{0,1:T(2,128)} %param.14) | copy-start | bytes 1540
  2.4 10.6 %copy-start.7 = (s32[64,128]{1,0:T(8,128)S(1)}, s32[64,128]{1,0:T(8,128)}, u32[]{:S(2)}) copy-start(s32[64,128]{1,0:T(8,128)} %param.12) | copy-start | bytes 98308
  2.4 11.4 %copy-start.1 = (f32[32,64,128]{2,1,0:T(8,128)S(1)}, f32[32,64,128]{2,1,0:T(8,128)}, u32[]{:S(2)}) copy-start(f32[32,64,128]{2,1,0:T(8,128)} %param.10) | copy-start | bytes 3145732
  2.4 38.8 %all-to-all-start.1 = ((f32[32,2,32,128]{3,2,1,0:T(8,128)}), f32[32,2,32,128]{3,2,1,0:T(8,128)S(1)}, u32[]{:S(2)}, u32[]{:S(2)}) async-start(f32[32,2,32,128]{3,2,1,0:T(8,128)} %bitcast.31), calls=%async_computation.1 | async-start | bytes 2097152 | tf_op jit(solution)/shard_map/all_to_all | solution.py:315
  13.0 0.8 copy-start.8
  13.7 0.8 copy-start.2
  13.7 0.9 copy-start.3
  13.8 0.9 copy-start.4
  13.8 0.9 copy-start.5
  13.8 0.8 copy-start.6
  41.2 33.5 %all-to-all-start = ((f32[32,2,32,128]{3,2,1,0:T(8,128)}), f32[32,2,32,128]{3,2,1,0:T(8,128)S(1)}, u32[]{:S(2)}, u32[]{:S(2)}) async-start(f32[32,2,32,128]{3,2,1,0:T(8,128)} %bitcast.5), calls=%async_computation | async-start | bytes 2097152 | tf_op jit(solution)/shard_map/all_to_all | solution.py:326
  45.9 6.3 %collective-permute-start.4 = (f32[1,256]{1,0:T(1,128)S(1)}, f32[1,256]{1,0:T(1,128)S(1)}, u32[]{:S(2)}, u32[]{:S(2)}) collective-permute-start(f32[1,256]{1,0:T(1,128)S(1)} %get-tuple-element.31), channel_id=1, source_target_pairs={{0,1},{1,2},{2,3},{3,4},{4,5},{5,6},{6,7},{7,0},{8,9},{9,10},{10,1... | collective-permute-start | bytes 3080 | tf_op jit(solution)/shard_map/ppermute | solution.py:329
  47.3 4.9 %collective-permute-start.5 = (f32[1,256]{1,0:T(1,128)S(1)}, f32[1,256]{1,0:T(1,128)S(1)}, u32[]{:S(2)}, u32[]{:S(2)}) collective-permute-start(f32[1,256]{1,0:T(1,128)S(1)} %get-tuple-element.32), channel_id=1, source_target_pairs={{1,0},{2,1},{3,2},{4,3},{5,4},{6,5},{7,6},{0,7},{9,8},{10,9},{11,1... | collective-permute-start | bytes 3080 | tf_op jit(solution)/shard_map/ppermute | solution.py:330
  53.3 29.8 %collective-permute-start.3 = (f32[32,32,128]{2,1,0:T(8,128)}, f32[32,32,128]{2,1,0:T(8,128)S(1)}, u32[]{:S(2)}, u32[]{:S(2)}) collective-permute-start(f32[32,32,128]{2,1,0:T(8,128)} %get-tuple-element.27), channel_id=1, source_target_pairs={{16,15},{24,16},{48,24},{56,48},{80,56},{88,80},{112,88},{120,112}... | collective-permute-start | bytes 1572872 | tf_op jit(solution)/shard_map/ppermute | solution.py:342
  54.7 28.5 %collective-permute-start.2 = (f32[32,32,128]{2,1,0:T(8,128)}, f32[32,32,128]{2,1,0:T(8,128)S(1)}, u32[]{:S(2)}, u32[]{:S(2)}) collective-permute-start(f32[32,32,128]{2,1,0:T(8,128)} %get-tuple-element.28), channel_id=1, source_target_pairs={{16,24},{24,48},{48,56},{56,80},{80,88},{88,112},{112,120},{120,14... | collective-permute-start | bytes 1572872 | tf_op jit(solution)/shard_map/ppermute | solution.py:341
  74.8 9.0 %collective-permute-start.1 = (f32[32,32,128]{2,1,0:T(8,128)S(1)}, f32[32,32,128]{2,1,0:T(8,128)S(1)}, u32[]{:S(2)}, u32[]{:S(2)}) collective-permute-start(f32[32,32,128]{2,1,0:T(8,128)S(1)} %get-tuple-element.29), channel_id=1, source_target_pairs={{16,15},{24,16},{48,24},{56,48},{80,56},{88,80},{112,88},{120,112}... | collective-permute-start | bytes 1572872 | tf_op jit(solution)/shard_map/ppermute | solution.py:344
  75.5 8.2 %collective-permute-start = (f32[32,32,128]{2,1,0:T(8,128)S(1)}, f32[32,32,128]{2,1,0:T(8,128)S(1)}, u32[]{:S(2)}, u32[]{:S(2)}) collective-permute-start(f32[32,32,128]{2,1,0:T(8,128)S(1)} %get-tuple-element.30), channel_id=1, source_target_pairs={{16,24},{24,48},{48,56},{56,80},{80,88},{88,112},{112,120},{120,14... | collective-permute-start | bytes 1572872 | tf_op jit(solution)/shard_map/ppermute | solution.py:343

commit v6 on v5

--- a/solution.py
+++ b/solution.py
@@ -11,6 +11,7 @@
 PV = 128
 NMEM = 32
 PIECES = 4
+WIDE = 100.0
 PAIRS = 32
 F32 = jnp.float32
 BF16 = jnp.bfloat16
@@ -158,10 +159,18 @@
     return jnp.where(row == lax.broadcasted_iota(jnp.int32, (PV, PV), 1), 1.0, 0.0)
 
 
-def inverses(matrices, s_ref, x_ref):
-    deltas = []
+def closer(delta):
+    return delta * delta / (2.0 - delta * delta)
+
+
+def sharper(s, x, delta, product=dot3):
+    return (2.0 / (2.0 - delta * delta)) * (2.0 * x - product(x, product(s, x)))
+
+
+def inverses(matrices, s_ref, x_ref, steps, goal):
     eye = identity()
-    for j, s in enumerate(matrices):
+    xs, deltas, tops = [], [], []
+    for s in matrices:
         s2 = dot3(s, s)
         norms = jnp.sum(jnp.abs(s2), axis=0, keepdims=True)
         top = jnp.sqrt(jnp.max(norms, axis=1, keepdims=True))
@@ -170,26 +179,41 @@
         mu = 2.0 / (2.0 - delta * delta)
         x1 = (mu * c) * (2.0 * eye - c * s)
         t1 = (mu * c) * (2.0 * s - c * s2)
-        delta = delta * delta / (2.0 - delta * delta)
-        mu = 2.0 / (2.0 - delta * delta)
-        s_ref[j] = s
-        x_ref[j] = mu * (2.0 * x1 - dot3(x1, t1))
-        deltas.append(jnp.max(delta * delta / (2.0 - delta * delta)))
+        delta = closer(delta)
+        xs.append((2.0 / (2.0 - delta * delta)) * (2.0 * x1 - dot3(x1, t1)))
+        deltas.append(closer(delta))
+        tops.append(jnp.max(top))
+    for _ in range(steps):
+        xs = [sharper(*it) for it in zip(matrices, xs, deltas)]
+        deltas = [closer(delta) for delta in deltas]
+    for j in range(2):
+        s_ref[j] = matrices[j]
+        x_ref[j] = xs[j]
 
     def more(state):
-        return jnp.maximum(state[0], state[1]) > 0.02
+        return jnp.maximum(state[0], state[1]) > goal
 
     def sharpen(state):
-        after = []
         for j in range(2):
-            delta = state[j]
-            x = x_ref[j]
-            mu = 2.0 / (2.0 - delta * delta)
-            x_ref[j] = mu * (2.0 * x - dot3(x, dot3(s_ref[j], x)))
-            after.append(delta * delta / (2.0 - delta * delta))
-        return tuple(after)
-
-    lax.while_loop(more, sharpen, tuple(deltas))
+            x_ref[j] = sharper(s_ref[j], x_ref[j], state[j])
+        return tuple(closer(delta) for delta in state)
+
+    last = lax.while_loop(more, sharpen, tuple(jnp.max(delta) for delta in deltas))
+
+    @pl.when(jnp.maximum(*tops) > WIDE)
+    def _():
+        for j in range(2):
+            x_ref[j] = (2.0 / (tops[j] + 1.0)) * eye
+
+            def once(delta, j=j):
+                x_ref[j] = sharper(s_ref[j], x_ref[j], delta, exact)
+                return closer(delta)
+
+            start = (tops[j] - 1.0) / (tops[j] + 1.0)
+            lax.while_loop(lambda delta: delta > 1e-4, once, once(start))
+            x_ref[j] = 2.0 * x_ref[j] - exact(x_ref[j], exact(s_ref[j], x_ref[j]))
+
+    return jnp.maximum(*last), jnp.maximum(*tops)
 
 
 def own_kernel(
@@ -211,13 +235,13 @@
         o = idx_ref[j, 0] - 1
         high, low = bh[o], bl[o]
         mixed = tdot(high, low)
-        matrices.append((tdot(high, high) + (mixed + mixed.T)) * scale + identity())
-        crosses.append((tdot(high, ah[j]) + (tdot(high, al[j]) + tdot(low, ah[j]))) * scale)
-    inverses(matrices, s_ref, x_ref)
-    for j in range(2):
-        s, x = s_ref[j], x_ref[j]
-        x = 2.0 * x - dot3(x, dot3(s, x))
-        x = 2.0 * x - exact(x, exact(s, x))
+        small = mixed + (mixed.T + tdot(low, low))
+        matrices.append((tdot(high, high) + small) * scale + identity())
+        small = tdot(high, al[j]) + (tdot(low, ah[j]) + tdot(low, al[j]))
+        crosses.append((tdot(high, ah[j]) + small) * scale)
+    inverses(matrices, s_ref, x_ref, 3, 1e-4)
+    for j in range(2):
+        x = x_ref[j]
         inv_ref[j] = x
         part = exact(x, crosses[j])
         part_ref[j] = part
@@ -230,11 +254,12 @@
 def update_kernel(
     idx_ref, f_ref, fl_ref, fr_ref, p_ref, pl_ref, pr_ref, slot_ref, var_ref,
     ah, al, bh, bl, dh, dl, inv_ref, part_ref, base_ref, o_ref, hh, hl, s_ref, x_ref,
+    g_ref, k_ref, link_ref, gram_ref, d_ref,
 ):
     members = NMEM * NMEM
     scale = 1.0 / (members - 1)
     fields, readings = (fl_ref, fr_ref), (pl_ref, pr_ref)
-    complements, crosses = [], []
+    norms = []
     for j in range(2):
         o, h = idx_ref[j, 0] - 1, idx_ref[j, 1]
         apart = h == 3 * j
@@ -243,23 +268,49 @@
         y = observe(x, slot_ref[pl.ds(h, 1), :])
         r = lax.rsqrt(var_ref[pl.ds(h, 1), :])
         high, low = split(centred(y) * r)
+        d_ref[j] = (p - y) * r
         right = jnp.concatenate([bh[o], high, ah[j]], axis=1)
         under = jnp.concatenate([bl[o], low, al[j]], axis=1)
-        gram = (tdot(high, right) + (tdot(high, under) + tdot(low, right))) * scale
-        s_ho, s_hh, g_h = gram[:, :PV], gram[:, PV : 2 * PV] + identity(), gram[:, 2 * PV :]
-        link = dot3(s_ho, inv_ref[j])
-        complements.append(s_hh - dot3(link, s_ho.T))
-        crosses.append(g_h - dot3(s_ho, part_ref[j]))
-        lh, ll = split(link)
+        small = tdot(high, under) + (tdot(low, right) + tdot(low, under))
+        gram = (tdot(high, right) + small) * scale
+        gram_ref[j] = gram
+        norms.append(jnp.sum(gram * gram))
+
+    def eliminate(j, product):
+        s_ho, s_hh, g_h = (gram_ref[j, :, n * PV : (n + 1) * PV] for n in range(3))
+        link = product(s_ho, inv_ref[j])
+        link_ref[j] = link
+        s_ref[j] = s_hh + identity() - product(link, s_ho.T)
+        g_ref[j] = g_h - product(s_ho, part_ref[j])
+
+    for j in range(2):
+        eliminate(j, dot3)
+
+    @pl.when(jnp.maximum(*norms) > 300.0**2)
+    def _():
+        for j in range(2):
+            eliminate(j, exact)
+
+    for j in range(2):
+        o = idx_ref[j, 0] - 1
+        lh, ll = split(link_ref[j])
         carried = dot_t(dh[o], lh) + (dot_t(dh[o], ll) + dot_t(dl[o], lh))
-        hh[j], hl[j] = split((p - y) * r - carried)
-    inverses(complements, s_ref, x_ref)
-    for j in range(2):
-        s, x, g = s_ref[j], x_ref[j], crosses[j]
-        k_h = dot3(x, g)
-        for _ in range(2):
-            k_h = k_h + dot3(x, g - exact(s, k_h))
-        kh, kl = split(k_h)
+        hh[j], hl[j] = split(d_ref[j] - carried)
+    complements = [s_ref[j] for j in range(2)]
+    delta, top = inverses(complements, s_ref, x_ref, 2, 0.01)
+    for j in range(2):
+        s, x, g = s_ref[j], x_ref[j], g_ref[j]
+        k = dot3(x, g)
+        k_ref[j] = k + dot3(x, g - dot3(s, k))
+
+    @pl.when(jnp.maximum(delta * (WIDE / 0.0055), top) > WIDE)
+    def _():
+        for j in range(2):
+            for _ in range(2):
+                k_ref[j] += dot3(x_ref[j], g_ref[j] - exact(s_ref[j], k_ref[j]))
+
+    for j in range(2):
+        kh, kl = split(k_ref[j])
         gained = dot(hh[j], kh) + (dot(hh[j], kl) + dot(hl[j], kh))
         o_ref[:, j] = base_ref[:, j] + gained.reshape(NMEM, NMEM, PV)
 
@@ -349,11 +400,13 @@
     base = jax.ShapeDtypeStruct(packed, F32)
     half = pltpu.VMEM((2, members, PV), BF16)
     square = pltpu.VMEM((2, PV, PV), F32)
+    scratch = [half, half] + [square] * 5
+    scratch += [pltpu.VMEM((2, PV, 3 * PV), F32), pltpu.VMEM((2, members, PV), F32)]
     index = jnp.concatenate([index[:1, ::-1], index[1:]], axis=0)
     own_parts = vmem_call(
         own_kernel, [pair] * 6 + [small] * 2 + [base], [square, square], smem=1, n_in=5, us=9
     )(index, field, pert, slots, variances)
-    analysis = vmem_call(update_kernel, packed, [half, half, square, square], smem=1, n_in=18, us=7)(
+    analysis = vmem_call(update_kernel, packed, scratch, smem=1, n_in=18, us=7)(
         index, field, field_left, field_right, pert, pert_left, pert_right, slots, variances,
         *own_parts,
     )

time: 130 us -> 138 us (1.062)
  Pallas kernels: 23.8 us -> 35.6 us
  blocking collectives: 36 us -> 32.7 us
    pallas_call x1, Pallas kernels: 6.7 us -> 13.7 us  [body(): vmem_call(update_kernel, packed, scratch, smem=1, n_in=18, us=7)]
    pallas_call x1, Pallas kernels: 6.53 us -> 11.4 us  [body(): vmem_call(own_kernel, [pair] * 6 + [small] * 2 + [base], [square, square]...]
    all_to_all x1, blocking collectives: 36 us -> 32.7 us  [body(): returned = lax.all_to_all(analysis, 'mem', 0, 0, tiled=True)]
  transfers between devices with their start and end apart: 8 -> 8, of which waited for: 4 -> 3; matrix products, arithmetic and copies ran while one was open for 1% -> 1% of each run, Pallas kernels for 10% -> 13%
where the time goes in v6:
time: 138 us; the launch traced here: 136 us
  waiting for transfers between devices  39.3 us (28%)
  Pallas kernels  35.6 us (26%)
  blocking collectives  32.7 us (24%)
  starting transfers between devices  24.8 us (18%)
  local copies, waits for them, and re-layouts  3.01 us (2%)
    all_to_all x1, blocking collectives, body(): returned = lax.all_to_all(analysis, 'mem', 0, 0, tiled=True)  32.7 us
    all_to_all x1, waiting for transfers between devices, body(): pert = lax.all_to_all(pert_send.reshape(packed), 'mem', 0, 0, tiled=True)  19.8 us
    all_to_all x1, waiting for transfers between devices, body(): field = lax.all_to_all(field_send.reshape(packed), 'mem', 0, 0, tiled=True)  18.8 us
    pallas_call x1, Pallas kernels, body(): vmem_call(update_kernel, packed, scratch, smem=1, n_in=18, us=7)  13.7 us
    pallas_call x1, Pallas kernels, body(): vmem_call(own_kernel, [pair] * 6 + [small] * 2 + [base], [square, square]...  11.4 us
    all_to_all x1, starting transfers between devices, body(): pert = lax.all_to_all(pert_send.reshape(packed), 'mem', 0, 0, tiled=True)  10.5 us
    pallas_call x1, Pallas kernels, body(): vmem_call(forecast_kernel, sent, [pltpu.VMEM((2 * LEV, 2 * HID), BF16)] *...  6.81 us
    all_to_all x1, starting transfers between devices, body(): field = lax.all_to_all(field_send.reshape(packed), 'mem', 0, 0, tiled=True)  4.68 us
  transfers between devices with their start and end apart: 8, of which 3 were waited for; matrix products, arithmetic and copies ran while one was open for 1% of the time, Pallas kernels for 13%

profile of v6, /device:TPU:3, one launch (start us, length us, event | category | flops | bytes accessed | tf_op | source)
XLA Modules:
  0.0 136.0 jit_solution(16987415879991212061)
XLA Ops:
  0.0 2.4 %shard_map.101 = f32[64,32,128]{2,1,0:T(8,128)} custom-call(f32[32,64,128]{2,1,0:T(8,128)} %x_ref.1), custom_call_target="tpu_custom_call" | custom-call | flops 1000000000 | bytes 2097152 | tf_op jit(solution)/shard_map/pallas_call | solution.py:358
  2.4 0.0 copy-start.7
  2.4 0.0 copy-start.1
  2.4 10.5 %all-to-all-start.1 = ((f32[32,2,32,128]{3,2,1,0:T(8,128)}), f32[32,2,32,128]{3,2,1,0:T(8,128)S(1)}, u32[]{:S(2)}, u32[]{:S(2)}) async-start(f32[32,2,32,128]{3,2,1,0:T(8,128)} %bitcast.31), calls=%async_computation.1 | async-start | bytes 2097152 | tf_op jit(solution)/shard_map/all_to_all | solution.py:366
  13.0 0.0 copy-start.8
  13.0 0.7 copy-done.8
  13.8 0.0 copy-start.4
  13.8 0.0 copy-start.5
  13.8 0.0 copy-start.6
  13.8 0.8 copy-done.2
  14.6 0.0 copy-done.3
  14.6 6.8 %shard_map.100 = f32[64,32,128]{2,1,0:T(8,128)} custom-call(f32[2048,128]{1,0:T(8,128)S(1)} %bitcast.26, f32[1,64]{1,0:T(1,128)S(1)} %bitcast.29, bf16[64,512]{1,0:T(8,128)(2,1)S(1)} %copy-done.2, f32[1,512]{1,0:T(1,128)S(1)} %bitcast.28, bf16[64,512]{1,0:T(8,128)(2,1)S(1)} %bitcast.27, f32[1,64]{1,0:T(1,128)S(1)} %bitcast.30), custom_call_target="tpu_custom_call" | custom-call | flops 7000000000 | bytes 1048576 | tf_op jit(solution)/shard_map/pallas_call | solution.py:368
  21.4 19.8 %all-to-all-done.1.p_ref = f32[32,2,32,128]{3,2,1,0:T(8,128)S(1)} async-done(((f32[32,2,32,128]{3,2,1,0:T(8,128)}), f32[32,2,32,128]{3,2,1,0:T(8,128)S(1)}, u32[]{:S(2)}, u32[]{:S(2)}) %all-to-all-start.1) | async-done | bytes 1048608 | tf_op jit(solution)/shard_map/all_to_all | solution.py:366
  41.2 4.7 %all-to-all-start = ((f32[32,2,32,128]{3,2,1,0:T(8,128)}), f32[32,2,32,128]{3,2,1,0:T(8,128)S(1)}, u32[]{:S(2)}, u32[]{:S(2)}) async-start(f32[32,2,32,128]{3,2,1,0:T(8,128)} %bitcast.5), calls=%async_computation | async-start | bytes 2097152 | tf_op jit(solution)/shard_map/all_to_all | solution.py:377
  45.9 1.4 %collective-permute-start.4 = (f32[1,256]{1,0:T(1,128)S(1)}, f32[1,256]{1,0:T(1,128)S(1)}, u32[]{:S(2)}, u32[]{:S(2)}) collective-permute-start(f32[1,256]{1,0:T(1,128)S(1)} %get-tuple-element.31), channel_id=1, source_target_pairs={{0,1},{1,2},{2,3},{3,4},{4,5},{5,6},{6,7},{7,0},{8,9},{9,10},{10,1... | collective-permute-start | bytes 3080 | tf_op jit(solution)/shard_map/ppermute | solution.py:380
  47.3 3.8 %collective-permute-start.5 = (f32[1,256]{1,0:T(1,128)S(1)}, f32[1,256]{1,0:T(1,128)S(1)}, u32[]{:S(2)}, u32[]{:S(2)}) collective-permute-start(f32[1,256]{1,0:T(1,128)S(1)} %get-tuple-element.32), channel_id=1, source_target_pairs={{1,0},{2,1},{3,2},{4,3},{5,4},{6,5},{7,6},{0,7},{9,8},{10,9},{11,1... | collective-permute-start | bytes 3080 | tf_op jit(solution)/shard_map/ppermute | solution.py:381
  51.1 0.1 constant_dynamic-slice_fusion
  51.2 0.1 copy.28
  51.3 0.1 fusion.2
  51.4 0.1 rev.3
  51.5 0.7 collective-permute-done.4
  52.2 1.1 slice_bitcast_fusion
  53.3 1.4 collective-permute-start.3
  54.7 1.3 collective-permute-start.2
  55.9 18.8 %all-to-all-done.f_ref = f32[32,2,32,128]{3,2,1,0:T(8,128)S(1)} async-done(((f32[32,2,32,128]{3,2,1,0:T(8,128)}), f32[32,2,32,128]{3,2,1,0:T(8,128)S(1)}, u32[]{:S(2)}, u32[]{:S(2)}) %all-to-all-start) | async-done | bytes 1048608 | tf_op jit(solution)/shard_map/all_to_all | solution.py:377
  74.7 0.1 slice_bitcast_fusion.2
  74.8 0.7 collective-permute-start.1
  75.5 1.1 collective-permute-start
  76.6 11.4 %shard_map.102 = (bf16[2,1024,128]{2,1,0:T(8,128)(2,1)S(1)}, bf16[2,1024,128]{2,1,0:T(8,128)(2,1)S(1)}, bf16[2,1024,128]{2,1,0:T(8,128)(2,1)S(1)}, bf16[2,1024,1...) custom-call(s32[2,2]{1,0:T(2,128)S(1)} %pad_add_fusion.idx_ref, ...), custom_call_target="tpu_custom_call" | custom-call | flops 8999999488 | bytes 1048576 | tf_op jit(solution)/shard_map/pallas_call | solution.py:406
  88.0 13.7 %shard_map.103 = f32[32,2,32,128]{3,2,1,0:T(8,128)S(1)} custom-call(s32[2,2]{1,0:T(2,128)S(1)} %pad_add_fusion.idx_ref, f32[32,2,32,128]{3,2,1,0:T(8,128)S(1)} %all-to-all-done.f_ref, f32[32,32,128]{2,1,0:T(8,128)S(1)} %collective-permute-done.fl_ref, f32[32,32,128]{2,1,0:T(8,128)S(1)} %collective-permute-done.1.fr_ref, ...), custom_call_target="tpu_custom_call" | custom-call | flops 7000000000 | bytes 1048576 | tf_op jit(solution)/shard_map/pallas_call | solution.py:409
  101.7 32.7 %all_to_all.15 = f32[32,2,32,128]{3,2,1,0:T(8,128)S(1)} all-to-all(f32[32,2,32,128]{3,2,1,0:T(8,128)S(1)} %shard_map.103), channel_id=1, replica_groups=mesh['mem'=32,'space'=8] {'mem'}, dimensions={0} | all-to-all | bytes 2097152 | tf_op jit(solution)/shard_map/all_to_all | solution.py:413
  134.4 1.4 %shard_map.104 = f32[2048,128]{1,0:T(8,128)} custom-call(f32[64,32,128]{2,1,0:T(8,128)S(1)} %bitcast.25), custom_call_target="tpu_custom_call" | custom-call | flops 1000000000 | bytes 2097152 | tf_op jit(solution)/shard_map/pallas_call | solution.py:414
  (22 shorter events, 0.1 us)
Async XLA Ops:
  0.0 51.1 %copy-start = (s32[64,2]{0,1:T(2,128)S(1)}, s32[64,2]{0,1:T(2,128)}, u32[]{:S(2)}) copy-start(s32[64,2]{0,1:T(2,128)} %param.14) | copy-start | bytes 1540
  2.4 10.6 %copy-start.7 = (s32[64,128]{1,0:T(8,128)S(1)}, s32[64,128]{1,0:T(8,128)}, u32[]{:S(2)}) copy-start(s32[64,128]{1,0:T(8,128)} %param.12) | copy-start | bytes 98308
  2.4 11.4 %copy-start.1 = (f32[32,64,128]{2,1,0:T(8,128)S(1)}, f32[32,64,128]{2,1,0:T(8,128)}, u32[]{:S(2)}) copy-start(f32[32,64,128]{2,1,0:T(8,128)} %param.10) | copy-start | bytes 3145732
  2.4 38.8 %all-to-all-start.1 = ((f32[32,2,32,128]{3,2,1,0:T(8,128)}), f32[32,2,32,128]{3,2,1,0:T(8,128)S(1)}, u32[]{:S(2)}, u32[]{:S(2)}) async-start(f32[32,2,32,128]{3,2,1,0:T(8,128)} %bitcast.31), calls=%async_computation.1 | async-start | bytes 2097152 | tf_op jit(solution)/shard_map/all_to_all | solution.py:366
  13.0 0.8 copy-start.8
  13.7 0.8 copy-start.2
  13.7 0.9 copy-start.3
  13.8 0.9 copy-start.4
  13.8 0.9 copy-start.5
  13.8 0.8 copy-start.6
  41.2 33.5 %all-to-all-start = ((f32[32,2,32,128]{3,2,1,0:T(8,128)}), f32[32,2,32,128]{3,2,1,0:T(8,128)S(1)}, u32[]{:S(2)}, u32[]{:S(2)}) async-start(f32[32,2,32,128]{3,2,1,0:T(8,128)} %bitcast.5), calls=%async_computation | async-start | bytes 2097152 | tf_op jit(solution)/shard_map/all_to_all | solution.py:377
  45.9 6.3 %collective-permute-start.4 = (f32[1,256]{1,0:T(1,128)S(1)}, f32[1,256]{1,0:T(1,128)S(1)}, u32[]{:S(2)}, u32[]{:S(2)}) collective-permute-start(f32[1,256]{1,0:T(1,128)S(1)} %get-tuple-element.31), channel_id=1, source_target_pairs={{0,1},{1,2},{2,3},{3,4},{4,5},{5,6},{6,7},{7,0},{8,9},{9,10},{10,1... | collective-permute-start | bytes 3080 | tf_op jit(solution)/shard_map/ppermute | solution.py:380
  47.3 4.9 %collective-permute-start.5 = (f32[1,256]{1,0:T(1,128)S(1)}, f32[1,256]{1,0:T(1,128)S(1)}, u32[]{:S(2)}, u32[]{:S(2)}) collective-permute-start(f32[1,256]{1,0:T(1,128)S(1)} %get-tuple-element.32), channel_id=1, source_target_pairs={{1,0},{2,1},{3,2},{4,3},{5,4},{6,5},{7,6},{0,7},{9,8},{10,9},{11,1... | collective-permute-start | bytes 3080 | tf_op jit(solution)/shard_map/ppermute | solution.py:381
  53.3 34.7 %collective-permute-start.3 = (f32[32,32,128]{2,1,0:T(8,128)}, f32[32,32,128]{2,1,0:T(8,128)S(1)}, u32[]{:S(2)}, u32[]{:S(2)}) collective-permute-start(f32[32,32,128]{2,1,0:T(8,128)} %get-tuple-element.27), channel_id=1, source_target_pairs={{16,15},{24,16},{48,24},{56,48},{80,56},{88,80},{112,88},{120,112}... | collective-permute-start | bytes 1572872 | tf_op jit(solution)/shard_map/ppermute | solution.py:393
  54.7 33.3 %collective-permute-start.2 = (f32[32,32,128]{2,1,0:T(8,128)}, f32[32,32,128]{2,1,0:T(8,128)S(1)}, u32[]{:S(2)}, u32[]{:S(2)}) collective-permute-start(f32[32,32,128]{2,1,0:T(8,128)} %get-tuple-element.28), channel_id=1, source_target_pairs={{16,24},{24,48},{48,56},{56,80},{80,88},{88,112},{112,120},{120,14... | collective-permute-start | bytes 1572872 | tf_op jit(solution)/shard_map/ppermute | solution.py:392
  74.8 13.2 %collective-permute-start.1 = (f32[32,32,128]{2,1,0:T(8,128)S(1)}, f32[32,32,128]{2,1,0:T(8,128)S(1)}, u32[]{:S(2)}, u32[]{:S(2)}) collective-permute-start(f32[32,32,128]{2,1,0:T(8,128)S(1)} %get-tuple-element.29), channel_id=1, source_target_pairs={{16,15},{24,16},{48,24},{56,48},{80,56},{88,80},{112,88},{120,112}... | collective-permute-start | bytes 1572872 | tf_op jit(solution)/shard_map/ppermute | solution.py:395
  75.5 12.5 %collective-permute-start = (f32[32,32,128]{2,1,0:T(8,128)S(1)}, f32[32,32,128]{2,1,0:T(8,128)S(1)}, u32[]{:S(2)}, u32[]{:S(2)}) collective-permute-start(f32[32,32,128]{2,1,0:T(8,128)S(1)} %get-tuple-element.30), channel_id=1, source_target_pairs={{16,24},{24,48},{48,56},{56,80},{80,88},{88,112},{112,120},{120,14... | collective-permute-start | bytes 1572872 | tf_op jit(solution)/shard_map/ppermute | solution.py:394

commit v7 on v6

--- a/solution.py
+++ b/solution.py
@@ -48,10 +48,6 @@
 
 def dot_t(a, b):
     return lax.dot_general(a, b, (((1,), (1,)), ((), ())), preferred_element_type=F32)
-
-
-def tdot(a, b):
-    return lax.dot_general(a, b, (((0,), (0,)), ((), ())), preferred_element_type=F32)
 
 
 def split(a):
@@ -218,7 +214,7 @@
 
 def own_kernel(
     idx_ref, f_ref, p_ref, slot_ref, var_ref,
-    ah, al, bh, bl, dh, dl, inv_ref, part_ref, base_ref, s_ref, x_ref,
+    ath, atl, bth, btl, dh, dl, inv_ref, part_ref, base_ref, ah, al, bh, bl, s_ref, x_ref,
 ):
     members = NMEM * NMEM
     root = lax.rsqrt(var_ref[...])
@@ -226,19 +222,22 @@
         x = f_ref[:, w].reshape(members, PV)
         y = observe(x, slot_ref[w + 1 : w + 2, :])
         r = root[w + 1 : w + 2, :]
-        ah[w], al[w] = split(centred(x))
-        bh[w], bl[w] = split(centred(y) * r)
+        a, b = centred(x), centred(y) * r
+        ah[w], al[w] = split(a)
+        bh[w], bl[w] = split(b)
+        ath[w], atl[w] = split(a.T)
+        bth[w], btl[w] = split(b.T)
         dh[w], dl[w] = split((p_ref[:, w].reshape(members, PV) - y) * r)
     scale = 1.0 / (members - 1)
     matrices, crosses = [], []
     for j in range(2):
         o = idx_ref[j, 0] - 1
-        high, low = bh[o], bl[o]
-        mixed = tdot(high, low)
-        small = mixed + (mixed.T + tdot(low, low))
-        matrices.append((tdot(high, high) + small) * scale + identity())
-        small = tdot(high, al[j]) + (tdot(low, ah[j]) + tdot(low, al[j]))
-        crosses.append((tdot(high, ah[j]) + small) * scale)
+        high, low = bth[o], btl[o]
+        mixed = dot(high, bl[o])
+        small = mixed + (mixed.T + dot(low, bl[o]))
+        matrices.append((dot(high, bh[o]) + small) * scale + identity())
+        small = dot(high, al[j]) + (dot(low, ah[j]) + dot(low, al[j]))
+        crosses.append((dot(high, ah[j]) + small) * scale)
     inverses(matrices, s_ref, x_ref, 3, 1e-4)
     for j in range(2):
         x = x_ref[j]
@@ -253,7 +252,7 @@
 
 def update_kernel(
     idx_ref, f_ref, fl_ref, fr_ref, p_ref, pl_ref, pr_ref, slot_ref, var_ref,
-    ah, al, bh, bl, dh, dl, inv_ref, part_ref, base_ref, o_ref, hh, hl, s_ref, x_ref,
+    ath, atl, bth, btl, dh, dl, inv_ref, part_ref, base_ref, o_ref, hh, hl, s_ref, x_ref,
     g_ref, k_ref, link_ref, gram_ref, d_ref,
 ):
     members = NMEM * NMEM
@@ -267,12 +266,13 @@
         p = jnp.where(apart, readings[j][...], p_ref[:, j]).reshape(members, PV)
         y = observe(x, slot_ref[pl.ds(h, 1), :])
         r = lax.rsqrt(var_ref[pl.ds(h, 1), :])
-        high, low = split(centred(y) * r)
+        b = centred(y) * r
         d_ref[j] = (p - y) * r
-        right = jnp.concatenate([bh[o], high, ah[j]], axis=1)
-        under = jnp.concatenate([bl[o], low, al[j]], axis=1)
-        small = tdot(high, under) + (tdot(low, right) + tdot(low, under))
-        gram = (tdot(high, right) + small) * scale
+        rows = [bth[o], btl[o], *split(b.T), ath[j], atl[j]]
+        both = dot(jnp.concatenate(rows, axis=0), jnp.concatenate(split(b), axis=1))
+        both = both[:, :PV] + both[:, PV:]
+        s_oh, s_hh, g = (both[n : n + PV] + both[n + PV : n + 2 * PV] for n in (0, 2 * PV, 4 * PV))
+        gram = jnp.concatenate([s_oh.T, s_hh, g.T], axis=1) * scale
         gram_ref[j] = gram
         norms.append(jnp.sum(gram * gram))
 
@@ -396,6 +396,7 @@
 
     members = NMEM * NMEM
     pair = jax.ShapeDtypeStruct((2, members, PV), BF16)
+    turned = jax.ShapeDtypeStruct((2, PV, members), BF16)
     small = jax.ShapeDtypeStruct((2, PV, PV), F32)
     base = jax.ShapeDtypeStruct(packed, F32)
     half = pltpu.VMEM((2, members, PV), BF16)
@@ -404,7 +405,8 @@
     scratch += [pltpu.VMEM((2, PV, 3 * PV), F32), pltpu.VMEM((2, members, PV), F32)]
     index = jnp.concatenate([index[:1, ::-1], index[1:]], axis=0)
     own_parts = vmem_call(
-        own_kernel, [pair] * 6 + [small] * 2 + [base], [square, square], smem=1, n_in=5, us=9
+        own_kernel, [turned] * 4 + [pair] * 2 + [small] * 2 + [base], [half] * 4 + [square] * 2,
+        smem=1, n_in=5, us=9,
     )(index, field, pert, slots, variances)
     analysis = vmem_call(update_kernel, packed, scratch, smem=1, n_in=18, us=7)(
         index, field, field_left, field_right, pert, pert_left, pert_right, slots, variances,

time: 138 us -> 136 us (0.986)
  the two profiles are of different devices: /device:TPU:3 before, /device:TPU:30 now
where the time goes in v7:
time: 136 us; the launch traced here: 135 us
  waiting for transfers between devices  48.4 us (36%)
  blocking collectives  44.3 us (33%)
  Pallas kernels  21.8 us (16%)
  starting transfers between devices  17.4 us (13%)
  local copies, waits for them, and re-layouts  3.01 us (2%)
    all_to_all x1, blocking collectives, body(): returned = lax.all_to_all(analysis, 'mem', 0, 0, tiled=True)  44.3 us
    all_to_all x1, waiting for transfers between devices, body(): pert = lax.all_to_all(pert_send.reshape(packed), 'mem', 0, 0, tiled=True)  20.5 us
    all_to_all x1, waiting for transfers between devices, body(): field = lax.all_to_all(field_send.reshape(packed), 'mem', 0, 0, tiled=True)  19.1 us
    all_to_all x1, starting transfers between devices, body(): pert = lax.all_to_all(pert_send.reshape(packed), 'mem', 0, 0, tiled=True)  10.2 us
    pallas_call x1, Pallas kernels, body(): vmem_call(forecast_kernel, sent, [pltpu.VMEM((2 * LEV, 2 * HID), BF16)] *...  6.81 us
    pallas_call x1, Pallas kernels, body(): vmem_call(update_kernel, packed, scratch, smem=1, n_in=18, us=7)  5.73 us
    pallas_call x1, Pallas kernels, body(): vmem_call(own_kernel, [turned] * 4 + [pair] * 2 + [small] * 2 + [base], [...  5.53 us
    ppermute x1, waiting for transfers between devices, body(): after = lax.ppermute(meta[:1], 'space', [(j, i) for i, j in runs])  4.68 us
  transfers between devices with their start and end apart: 8, of which 6 were waited for; matrix products, arithmetic and copies ran while one was open for 1% of the time, Pallas kernels for 9%

profile of v7, /device:TPU:30, one launch (start us, length us, event | category | flops | bytes accessed | tf_op | source)
XLA Modules:
  0.0 135.4 jit_solution(18058468742635212912)
XLA Ops:
  0.0 2.4 %shard_map.101 = f32[64,32,128]{2,1,0:T(8,128)} custom-call(f32[32,64,128]{2,1,0:T(8,128)} %x_ref.1), custom_call_target="tpu_custom_call" | custom-call | flops 1000000000 | bytes 2097152 | tf_op jit(solution)/shard_map/pallas_call | solution.py:358
  2.4 0.0 copy-start.7
  2.4 0.0 copy-start.1
  2.4 10.2 %all-to-all-start.1 = ((f32[32,2,32,128]{3,2,1,0:T(8,128)}), f32[32,2,32,128]{3,2,1,0:T(8,128)S(1)}, u32[]{:S(2)}, u32[]{:S(2)}) async-start(f32[32,2,32,128]{3,2,1,0:T(8,128)} %bitcast.31), calls=%async_computation.1 | async-start | bytes 2097152 | tf_op jit(solution)/shard_map/all_to_all | solution.py:366
  12.7 0.0 copy-start.8
  12.7 0.7 copy-done.8
  13.5 0.0 copy-start.6
  13.5 0.8 copy-done.2
  14.3 0.0 copy-done.3
  14.3 6.8 %shard_map.100 = f32[64,32,128]{2,1,0:T(8,128)} custom-call(f32[2048,128]{1,0:T(8,128)S(1)} %bitcast.26, f32[1,64]{1,0:T(1,128)S(1)} %bitcast.29, bf16[64,512]{1,0:T(8,128)(2,1)S(1)} %copy-done.2, f32[1,512]{1,0:T(1,128)S(1)} %bitcast.28, bf16[64,512]{1,0:T(8,128)(2,1)S(1)} %bitcast.27, f32[1,64]{1,0:T(1,128)S(1)} %bitcast.30), custom_call_target="tpu_custom_call" | custom-call | flops 7000000000 | bytes 1048576 | tf_op jit(solution)/shard_map/pallas_call | solution.py:368
  21.1 20.5 %all-to-all-done.1.p_ref = f32[32,2,32,128]{3,2,1,0:T(8,128)S(1)} async-done(((f32[32,2,32,128]{3,2,1,0:T(8,128)}), f32[32,2,32,128]{3,2,1,0:T(8,128)S(1)}, u32[]{:S(2)}, u32[]{:S(2)}) %all-to-all-start.1) | async-done | bytes 1048608 | tf_op jit(solution)/shard_map/all_to_all | solution.py:366
  41.6 4.0 %all-to-all-start = ((f32[32,2,32,128]{3,2,1,0:T(8,128)}), f32[32,2,32,128]{3,2,1,0:T(8,128)S(1)}, u32[]{:S(2)}, u32[]{:S(2)}) async-start(f32[32,2,32,128]{3,2,1,0:T(8,128)} %bitcast.5), calls=%async_computation | async-start | bytes 2097152 | tf_op jit(solution)/shard_map/all_to_all | solution.py:377
  45.6 1.1 collective-permute-start.4
  46.8 1.0 collective-permute-start.5
  47.7 0.1 constant_dynamic-slice_fusion
  47.8 0.1 copy.28
  47.9 0.1 fusion.2
  48.0 0.1 rev.3
  48.1 1.2 collective-permute-done.4
  49.3 4.7 %collective-permute-done.5 = f32[1,256]{1,0:T(1,128)S(1)} collective-permute-done((f32[1,256]{1,0:T(1,128)S(1)}, f32[1,256]{1,0:T(1,128)S(1)}, u32[]{:S(2)}, u32[]{:S(2)}) %collective-permute-start.5) | collective-permute-done | bytes 1056 | tf_op jit(solution)/shard_map/ppermute | solution.py:381
  54.0 1.1 slice_bitcast_fusion
  55.1 0.5 collective-permute-start.2
  55.6 19.1 %all-to-all-done.f_ref = f32[32,2,32,128]{3,2,1,0:T(8,128)S(1)} async-done(((f32[32,2,32,128]{3,2,1,0:T(8,128)}), f32[32,2,32,128]{3,2,1,0:T(8,128)S(1)}, u32[]{:S(2)}, u32[]{:S(2)}) %all-to-all-start) | async-done | bytes 1048608 | tf_op jit(solution)/shard_map/all_to_all | solution.py:377
  74.7 0.1 slice_bitcast_fusion.2
  74.7 0.5 collective-permute-start.1
  75.2 0.1 collective-permute-start
  75.3 5.5 %shard_map.102 = (bf16[2,128,1024]{2,1,0:T(8,128)(2,1)S(1)}, bf16[2,128,1024]{2,1,0:T(8,128)(2,1)S(1)}, bf16[2,128,1024]{2,1,0:T(8,128)(2,1)S(1)}, bf16[2,128,10...) custom-call(s32[2,2]{1,0:T(2,128)S(1)} %pad_add_fusion.idx_ref, ...), custom_call_target="tpu_custom_call" | custom-call | flops 8999999488 | bytes 1048576 | tf_op jit(solution)/shard_map/pallas_call | solution.py:407
  80.9 1.0 collective-permute-done.1.fr_ref
  81.9 1.9 %collective-permute-done.fl_ref = f32[32,32,128]{2,1,0:T(8,128)S(1)} collective-permute-done((f32[32,32,128]{2,1,0:T(8,128)S(1)}, f32[32,32,128]{2,1,0:T(8,128)S(1)}, u32[]{:S(2)}, u32[]{:S(2)}) %collective-permute-start) | collective-permute-done | bytes 524320 | tf_op jit(solution)/shard_map/ppermute | solution.py:394
  83.8 5.7 %shard_map.103 = f32[32,2,32,128]{3,2,1,0:T(8,128)S(1)} custom-call(s32[2,2]{1,0:T(2,128)S(1)} %pad_add_fusion.idx_ref, f32[32,2,32,128]{3,2,1,0:T(8,128)S(1)} %all-to-all-done.f_ref, f32[32,32,128]{2,1,0:T(8,128)S(1)} %collective-permute-done.fl_ref, f32[32,32,128]{2,1,0:T(8,128)S(1)} %collective-permute-done.1.fr_ref, ...), custom_call_target="tpu_custom_call" | custom-call | flops 7000000000 | bytes 1048576 | tf_op jit(solution)/shard_map/pallas_call | solution.py:411
  89.5 44.3 %all_to_all.15 = f32[32,2,32,128]{3,2,1,0:T(8,128)S(1)} all-to-all(f32[32,2,32,128]{3,2,1,0:T(8,128)S(1)} %shard_map.103), channel_id=1, replica_groups=mesh['mem'=32,'space'=8] {'mem'}, dimensions={0} | all-to-all | bytes 2097152 | tf_op jit(solution)/shard_map/all_to_all | solution.py:415
  133.9 1.4 %shard_map.104 = f32[2048,128]{1,0:T(8,128)} custom-call(f32[64,32,128]{2,1,0:T(8,128)S(1)} %bitcast.25), custom_call_target="tpu_custom_call" | custom-call | flops 1000000000 | bytes 2097152 | tf_op jit(solution)/shard_map/pallas_call | solution.py:416
  (22 shorter events, 0.1 us)
Async XLA Ops:
  0.0 47.7 %copy-start = (s32[64,2]{0,1:T(2,128)S(1)}, s32[64,2]{0,1:T(2,128)}, u32[]{:S(2)}) copy-start(s32[64,2]{0,1:T(2,128)} %param.14) | copy-start | bytes 1540
  2.4 10.3 %copy-start.7 = (s32[64,128]{1,0:T(8,128)S(1)}, s32[64,128]{1,0:T(8,128)}, u32[]{:S(2)}) copy-start(s32[64,128]{1,0:T(8,128)} %param.12) | copy-start | bytes 98308
  2.4 11.1 %copy-start.1 = (f32[32,64,128]{2,1,0:T(8,128)S(1)}, f32[32,64,128]{2,1,0:T(8,128)}, u32[]{:S(2)}) copy-start(f32[32,64,128]{2,1,0:T(8,128)} %param.10) | copy-start | bytes 3145732
  2.4 39.2 %all-to-all-start.1 = ((f32[32,2,32,128]{3,2,1,0:T(8,128)}), f32[32,2,32,128]{3,2,1,0:T(8,128)S(1)}, u32[]{:S(2)}, u32[]{:S(2)}) async-start(f32[32,2,32,128]{3,2,1,0:T(8,128)} %bitcast.31), calls=%async_computation.1 | async-start | bytes 2097152 | tf_op jit(solution)/shard_map/all_to_all | solution.py:366
  12.7 0.8 copy-start.8
  13.4 0.8 copy-start.2
  13.4 0.9 copy-start.3
  13.4 0.9 copy-start.4
  13.5 0.9 copy-start.5
  13.5 0.8 copy-start.6
  41.6 33.1 %all-to-all-start = ((f32[32,2,32,128]{3,2,1,0:T(8,128)}), f32[32,2,32,128]{3,2,1,0:T(8,128)S(1)}, u32[]{:S(2)}, u32[]{:S(2)}) async-start(f32[32,2,32,128]{3,2,1,0:T(8,128)} %bitcast.5), calls=%async_computation | async-start | bytes 2097152 | tf_op jit(solution)/shard_map/all_to_all | solution.py:377
  45.6 3.6 %collective-permute-start.4 = (f32[1,256]{1,0:T(1,128)S(1)}, f32[1,256]{1,0:T(1,128)S(1)}, u32[]{:S(2)}, u32[]{:S(2)}) collective-permute-start(f32[1,256]{1,0:T(1,128)S(1)} %get-tuple-element.31), channel_id=1, source_target_pairs={{0,1},{1,2},{2,3},{3,4},{4,5},{5,6},{6,7},{7,0},{8,9},{9,10},{10,1... | collective-permute-start | bytes 3080 | tf_op jit(solution)/shard_map/ppermute | solution.py:380
  46.8 7.2 %collective-permute-start.5 = (f32[1,256]{1,0:T(1,128)S(1)}, f32[1,256]{1,0:T(1,128)S(1)}, u32[]{:S(2)}, u32[]{:S(2)}) collective-permute-start(f32[1,256]{1,0:T(1,128)S(1)} %get-tuple-element.32), channel_id=1, source_target_pairs={{1,0},{2,1},{3,2},{4,3},{5,4},{6,5},{7,6},{0,7},{9,8},{10,9},{11,1... | collective-permute-start | bytes 3080 | tf_op jit(solution)/shard_map/ppermute | solution.py:381
  55.0 25.8 %collective-permute-start.3 = (f32[32,32,128]{2,1,0:T(8,128)}, f32[32,32,128]{2,1,0:T(8,128)S(1)}, u32[]{:S(2)}, u32[]{:S(2)}) collective-permute-start(f32[32,32,128]{2,1,0:T(8,128)} %get-tuple-element.27), channel_id=1, source_target_pairs={{16,15},{24,16},{48,24},{56,48},{80,56},{88,80},{112,88},{120,112}... | collective-permute-start | bytes 1572872 | tf_op jit(solution)/shard_map/ppermute | solution.py:393
  55.1 25.8 %collective-permute-start.2 = (f32[32,32,128]{2,1,0:T(8,128)}, f32[32,32,128]{2,1,0:T(8,128)S(1)}, u32[]{:S(2)}, u32[]{:S(2)}) collective-permute-start(f32[32,32,128]{2,1,0:T(8,128)} %get-tuple-element.28), channel_id=1, source_target_pairs={{16,24},{24,48},{48,56},{56,80},{80,88},{88,112},{112,120},{120,14... | collective-permute-start | bytes 1572872 | tf_op jit(solution)/shard_map/ppermute | solution.py:392
  74.7 7.2 %collective-permute-start.1 = (f32[32,32,128]{2,1,0:T(8,128)S(1)}, f32[32,32,128]{2,1,0:T(8,128)S(1)}, u32[]{:S(2)}, u32[]{:S(2)}) collective-permute-start(f32[32,32,128]{2,1,0:T(8,128)S(1)} %get-tuple-element.29), channel_id=1, source_target_pairs={{16,15},{24,16},{48,24},{56,48},{80,56},{88,80},{112,88},{120,112}... | collective-permute-start | bytes 1572872 | tf_op jit(solution)/shard_map/ppermute | solution.py:395
  75.2 8.6 %collective-permute-start = (f32[32,32,128]{2,1,0:T(8,128)S(1)}, f32[32,32,128]{2,1,0:T(8,128)S(1)}, u32[]{:S(2)}, u32[]{:S(2)}) collective-permute-start(f32[32,32,128]{2,1,0:T(8,128)S(1)} %get-tuple-element.30), channel_id=1, source_target_pairs={{16,24},{24,48},{48,56},{56,80},{80,88},{88,112},{112,120},{120,14... | collective-permute-start | bytes 1572872 | tf_op jit(solution)/shard_map/ppermute | solution.py:394
